TPU v7x, 256 devices: a whole 4x4x8 slice. The times are simulated.
256 devices in a mesh: ty: 8 (over y, x_lo), tx: 32 (over z, x_hi, core).
Axes of the slice: x: 4 (x_hi: 2, x_lo: 2; x = x_hi * 2 + x_lo), y: 4, z: 8, core: 2. Of those that a mesh axis runs over, the one named last changes fastest.
Arguments:
- sky: bfloat16 [4096, 16384], P('ty', 'tx'), may hold values from -6 to 6
- point_count: int32 [8, 32], P('ty', 'tx'), may hold values from 0 to 4, as said below
- point_offset: int32 [8, 32, 4, 2], P('ty', 'tx'), may hold values from 0 to 511
- beam_width: bfloat16 [8, 32, 4], P('ty', 'tx'), may hold values from 128 to 340
- uv_bins: int32 [8, 32, 4, 2, 2], P('ty', 'tx'), may hold values from 0 to 7
- uv_count: int32 [8, 32, 4], P('ty', 'tx'), may hold values from 1 to 2
- uv_weight: bfloat16 [8, 32, 4, 2, 128, 128], P('ty', 'tx'), may hold values from 1 to 8
Outputs:
- curvature: float32 [4096, 16384], P('ty', 'tx')
Inputs may be any that keep to these rules, and one draw needn't show every extreme that they name: `point_count`: each tile holds at most 4 pointings, and the tiles of columns 2i and 2i + 1 of one row hold at most 4 together; in every draw some such pair holds exactly 4, all on one of its tiles. `point_offset`: entries of slots at or beyond a tile's count are ignored. `uv_bins`: entries of uv slots at or beyond a pointing's uv_count are ignored.
All inputs are finite; a program needn't handle non-finite values.
Results may differ from a plain program's by a relative error of at most 0.0085.
Values may be sent and summed in bfloat16 or wider, within the bound.
No kernel may reach another device: no remote copies, remote signals or barrier semaphores. Data moves between devices by JAX's collectives and lax.ppermute only.
A program may use at most 128 MiB of HBM per device.

v0:
```python
import math

import jax
import jax.numpy as jnp
from jax import lax
from jax.sharding import PartitionSpec as P


def padded(block, sides, width):
    for axis, dim in sides:
        count = lax.axis_size(axis)
        forward = [(i, i + 1) for i in range(count - 1)]
        backward = [(target, source) for source, target in forward]
        low = lax.ppermute(
            lax.slice_in_dim(block, block.shape[dim] - width, None, axis=dim), axis, forward
        )
        high = lax.ppermute(lax.slice_in_dim(block, 0, width, axis=dim), axis, backward)
        block = jnp.concatenate([low, block, high], axis=dim)
    return block


def swapped(x, axis, apart):
    return lax.ppermute(x, axis, [(i, i ^ 1 << apart) for i in range(lax.axis_size(axis))])


def shifted(value, axis, steps):
    count = lax.axis_size(axis)
    first, last = (max(0, -steps), min(count, count - steps))
    return lax.ppermute(value, axis, [(source, source + steps) for source in range(first, last)])


def for_sending(x):

    def short(part):
        return part.astype(jnp.bfloat16) if part.dtype == jnp.float32 else part

    return jax.tree.map(short, x)


def dft_tables(blocks, block_size, length):
    rows = blocks[:, None] * block_size + jnp.arange(block_size, dtype=jnp.int32)[None, :]
    pixels = jnp.arange(length, dtype=jnp.int32)
    phase = rows[:, :, None] * pixels[None, None, :] % length
    angle = phase.astype(jnp.float32) * (2.0 * math.pi / length)
    factor = 1.0 / math.sqrt(length)
    return (
        (jnp.cos(angle) * factor).astype(jnp.bfloat16),
        (jnp.sin(angle) * factor).astype(jnp.bfloat16),
    )


def beam_map(width, length):
    offset = jnp.arange(length, dtype=jnp.float32) - length // 2
    square = offset * offset
    radius = square[:, None] + square[None, :]
    spread = width.astype(jnp.float32)
    return jnp.exp(-radius / (2.0 * spread * spread))


def pointing_image(beamed, width, uv_pair, used, weight_tiles):
    slots_uv = weight_tiles.shape[0]
    block_size = weight_tiles.shape[1]
    length = beamed.shape[0]
    row_cos, row_sin = dft_tables(uv_pair[:, 0], block_size, length)
    col_cos, col_sin = dft_tables(uv_pair[:, 1], block_size, length)
    row_tables = jnp.stack([row_cos, row_sin], axis=1).reshape(slots_uv * 2 * block_size, length)
    col_tables = jnp.stack(
        [jnp.concatenate([col_cos, col_sin], axis=1), jnp.concatenate([-col_sin, col_cos], axis=1)],
        axis=1,
    )
    first = jnp.dot(row_tables, beamed, preferred_element_type=jnp.float32).astype(jnp.bfloat16)
    first = first.reshape(slots_uv, 2, block_size, length)
    visible = jnp.einsum("kcin,kcbn->kib", first, col_tables, preferred_element_type=jnp.float32)
    used_mask = (jnp.arange(slots_uv, dtype=jnp.int32) < used).astype(jnp.float32)
    weighted = weight_tiles.astype(jnp.float32) * used_mask[:, None, None]
    scaled = (visible * jnp.concatenate([weighted, weighted], axis=2)).astype(jnp.bfloat16)
    spread = jnp.einsum("kib,kcbn->kcin", scaled, col_tables, preferred_element_type=jnp.float32)
    spread = spread.astype(jnp.bfloat16).reshape(slots_uv * 2 * block_size, length)
    back = lax.dot_general(
        row_tables, spread, (((0,), (0,)), ((), ())), preferred_element_type=jnp.float32
    )
    return (beam_map(width, length) * back).astype(jnp.bfloat16)


def image_of(item):
    return pointing_image(item[0], item[1], item[2], item[3], item[4])


def add_patch(total, image, offset, live):
    patch_size = image.shape[0]
    current = lax.dynamic_slice(total, (offset[0], offset[1]), (patch_size, patch_size))
    update = jnp.where(live, image.astype(jnp.float32), jnp.zeros((), jnp.float32))
    return lax.dynamic_update_slice(total, current + update, (offset[0], offset[1]))


def shards(sky, point_count, point_offset, beam_width, uv_bins, uv_count, uv_weight):
    tile_size = sky.shape[0]
    patch_size = 2 * tile_size
    bordered = padded(sky, (("ty", 0), ("tx", 1)), tile_size)
    own_count = point_count[0, 0]
    offsets = point_offset[0, 0]
    widths = beam_width[0, 0]
    pair_bins = uv_bins[0, 0]
    used_counts = uv_count[0, 0]
    weight_tiles = uv_weight[0, 0]
    slots = offsets.shape[0]

    def beam_window(offset, width):
        window = lax.dynamic_slice(bordered, (offset[0], offset[1]), (patch_size, patch_size))
        return (beam_map(width, patch_size) * window.astype(jnp.float32)).astype(jnp.bfloat16)

    own_beamed = lax.map(lambda item: beam_window(item[0], item[1]), (offsets, widths))
    half_slots = slots // 2
    parity = lax.axis_index("tx") % 2
    first_slot = (1 - parity) * half_slots

    def pick(values):
        return lax.dynamic_slice_in_dim(values, first_slot, half_slots, 0)

    received = swapped(
        (
            pick(own_beamed),
            pick(widths),
            pick(pair_bins),
            pick(used_counts),
            pick(weight_tiles),
            point_count[0],
        ),
        "tx",
        0,
    )
    partner_count = received[5][0]
    first_count = jnp.where(parity == 0, own_count, partner_count)
    total_count = own_count + partner_count
    local_index = jnp.arange(half_slots, dtype=jnp.int32)
    combined = parity * half_slots + local_index
    even_side = combined < first_count
    pool_index = jnp.where(
        parity == 0,
        jnp.where(even_side, combined, slots + combined - first_count),
        jnp.where(even_side, slots + combined - half_slots, combined - first_count),
    )
    pool_index = jnp.clip(pool_index, 0, slots + half_slots - 1)

    def gather_pool(own_values, got_values):
        return jnp.take(jnp.concatenate([own_values, got_values], axis=0), pool_index, axis=0)

    items = (
        gather_pool(own_beamed, received[0]),
        gather_pool(widths, received[1]),
        gather_pool(pair_bins, received[2]),
        gather_pool(used_counts, received[3]),
        gather_pool(weight_tiles, received[4]),
    )
    images = lax.map(image_of, items)
    returned = swapped(images, "tx", 0)
    partner_combined = (1 - parity) * half_slots + local_index
    all_combined = jnp.concatenate([combined, partner_combined])
    all_images = jnp.concatenate([images, returned], axis=0)
    owner_odd = (all_combined >= first_count).astype(jnp.int32)
    slot_index = jnp.clip(all_combined - owner_odd * first_count, 0, slots - 1)
    live_flags = (owner_odd == parity) & (all_combined < total_count)
    placed = jnp.take(offsets, slot_index, axis=0)
    gathered = jnp.zeros((3 * tile_size, 3 * tile_size), jnp.float32)
    for position in range(all_images.shape[0]):
        gathered = add_patch(gathered, all_images[position], placed[position], live_flags[position])
    middle = gathered[:, tile_size : 2 * tile_size]
    middle = middle + shifted(gathered[:, :tile_size].astype(jnp.bfloat16), "tx", -1).astype(
        jnp.float32
    )
    middle = middle + shifted(gathered[:, 2 * tile_size :].astype(jnp.bfloat16), "tx", 1).astype(
        jnp.float32
    )
    result = middle[tile_size : 2 * tile_size, :]
    result = result + shifted(for_sending(middle[:tile_size, :]), "ty", -1)
    result = result + shifted(for_sending(middle[2 * tile_size :, :]), "ty", 1)
    return result


def solution(mesh):
    in_specs = (
        P("ty", "tx"),
        P("ty", "tx"),
        P("ty", "tx", None, None),
        P("ty", "tx", None),
        P("ty", "tx", None, None, None),
        P("ty", "tx", None),
        P("ty", "tx", None, None, None, None),
    )
    out_specs = P("ty", "tx")
    return jax.shard_map(shards, mesh=mesh, in_specs=in_specs, out_specs=out_specs, check_vma=False)
```

profile of v0, /device:TPU:6, one launch (start us, length us, event | category | flops | bytes accessed | tf_op | source)
XLA Modules:
  0.0 443.8 jit_solution(11096528925307795640)
XLA Ops:
  5.9 10.5 %collective-permute-done.3 = bf16[512,512]{1,0:T(8,128)(2,1)S(1)} collective-permute-done((bf16[512,512]{1,0:T(8,128)(2,1)}, bf16[512,512]{1,0:T(8,128)(2,1)S(1)}, u32[]{:S(2)}, u32[]{:S(2)}) %collective-permute-start.3) | collective-permute-done | bytes 524320 | tf_op jit(solution)/shard_map/ppermute | solution.py:14
  17.5 10.5 %collective-permute-done.4 = bf16[512,512]{1,0:T(8,128)(2,1)S(1)} collective-permute-done((bf16[512,512]{1,0:T(8,128)(2,1)}, bf16[512,512]{1,0:T(8,128)(2,1)S(1)}, u32[]{:S(2)}, u32[]{:S(2)}) %collective-permute-start.4) | collective-permute-done | bytes 524320 | tf_op jit(solution)/shard_map/ppermute | solution.py:17
  30.0 5.1 %collective-permute-start.6 = (bf16[1536,512]{1,0:T(8,128)(2,1)S(1)}, bf16[1536,512]{1,0:T(8,128)(2,1)}, u32[]{:S(2)}, u32[]{:S(2)}) collective-permute-start(bf16[1536,512]{1,0:T(8,128)(2,1)S(1)} %constant_dynamic-update-slice_fusion), channel_id=1, source_target_pairs={{1,0},{2,1},{3,2},{4,3},{5,4},{6,5},{7,6},{8,7},{9,8},{10,9},{11,1... | collective-permute-start | bytes 4718600 | tf_op jit(solution)/shard_map/ppermute | solution.py:17
  35.2 32.9 %collective-permute-done.5 = bf16[1536,512]{1,0:T(8,128)(2,1)S(1)} collective-permute-done((bf16[1536,512]{1,0:T(8,128)(2,1)S(1)}, bf16[1536,512]{1,0:T(8,128)(2,1)S(1)}, u32[]{:S(2)}, u32[]{:S(2)}) %collective-permute-start.5) | collective-permute-done | bytes 1572896 | tf_op jit(solution)/shard_map/ppermute | solution.py:14
  71.6 45.2 %while.24 = (s32[]{:T(128)}, bf16[4,1024,1024]{2,1,0:T(8,128)(2,1)}, bf16[4]{0:T(256)(128)(2,1)S(1)}, s32[4,2]{0,1:T(2,128)S(1)}, bf16[1536,1536]{1,0:T(8,128)(2...) while((s32[]{:T(128)}, bf16[4,1024,1024]{2,1,0:T(8,128)(2,1)}, bf16[4]{0:T(256)(128)(2,1)S(1)}, ...), condition=%wide.region_1.2_spmd, body=%wide.region_0.1_spmd.sunk | while | flops 6293514 | bytes 4207341 | solution.py:112
  78.0 4.9 %fusion.67 = bf16[4,1024,1024]{2,1,0:T(8,128)(2,1)} fusion(bf16[4,1024,1024]{2,1,0:T(8,128)(2,1)} %get-tuple-element.338, s32[]{:T(128)} %get-tuple-element.337, bf16[1536,1536]{1,0:T(8,128)(2,1)} %get-tuple-element.350, s32[]{:T(128)S(6)} %select_n.387, s32[]{:T(128)S(6)} %select_n.388, f32[]{:T(128)S(6)} %mul.410, f32[1024]{0:T(1024)S(1)} %add_multiply_fusion.4), kind=kLoop, calls=%fused_computation.9.clone.1 | loop fusion | flops 6291456 | bytes 4203020 | tf_op jit(solution)/shard_map/while/body/jit(dynamic_update_index_in_dim)/dynamic_update_slice | solution.py:112
  89.2 4.9 %fusion.67 = bf16[4,1024,1024]{2,1,0:T(8,128)(2,1)} fusion(bf16[4,1024,1024]{2,1,0:T(8,128)(2,1)} %get-tuple-element.338, s32[]{:T(128)} %get-tuple-element.337, bf16[1536,1536]{1,0:T(8,128)(2,1)} %get-tuple-element.350, s32[]{:T(128)S(6)} %select_n.387, s32[]{:T(128)S(6)} %select_n.388, f32[]{:T(128)S(6)} %mul.410, f32[1024]{0:T(1024)S(1)} %add_multiply_fusion.4), kind=kLoop, calls=%fused_computation.9.clone.1 | loop fusion | flops 6291456 | bytes 4203020 | tf_op jit(solution)/shard_map/while/body/jit(dynamic_update_index_in_dim)/dynamic_update_slice | solution.py:112
  100.5 5.0 %fusion.67 = bf16[4,1024,1024]{2,1,0:T(8,128)(2,1)} fusion(bf16[4,1024,1024]{2,1,0:T(8,128)(2,1)} %get-tuple-element.338, s32[]{:T(128)} %get-tuple-element.337, bf16[1536,1536]{1,0:T(8,128)(2,1)} %get-tuple-element.350, s32[]{:T(128)S(6)} %select_n.387, s32[]{:T(128)S(6)} %select_n.388, f32[]{:T(128)S(6)} %mul.410, f32[1024]{0:T(1024)S(1)} %add_multiply_fusion.4), kind=kLoop, calls=%fused_computation.9.clone.1 | loop fusion | flops 6291456 | bytes 4203020 | tf_op jit(solution)/shard_map/while/body/jit(dynamic_update_index_in_dim)/dynamic_update_slice | solution.py:112
  111.9 4.9 %fusion.67 = bf16[4,1024,1024]{2,1,0:T(8,128)(2,1)} fusion(bf16[4,1024,1024]{2,1,0:T(8,128)(2,1)} %get-tuple-element.338, s32[]{:T(128)} %get-tuple-element.337, bf16[1536,1536]{1,0:T(8,128)(2,1)} %get-tuple-element.350, s32[]{:T(128)S(6)} %select_n.387, s32[]{:T(128)S(6)} %select_n.388, f32[]{:T(128)S(6)} %mul.410, f32[1024]{0:T(1024)S(1)} %add_multiply_fusion.4), kind=kLoop, calls=%fused_computation.9.clone.1 | loop fusion | flops 6291456 | bytes 4203020 | tf_op jit(solution)/shard_map/while/body/jit(dynamic_update_index_in_dim)/dynamic_update_slice | solution.py:112
  123.7 5.2 %collective-permute-done = s32[1]{0:T(128)} collective-permute-done((s32[1]{0:T(128)}, s32[1]{0:T(128)}, u32[]{:S(2)}, u32[]{:S(2)}) %collective-permute-start) | collective-permute-done | bytes 36 | tf_op jit(solution)/shard_map/ppermute | solution.py:23
  132.9 7.6 %constant_dynamic-update-slice_fusion.4 = bf16[6,1024,1024]{2,1,0:T(8,128)(2,1)} fusion(bf16[4,1024,1024]{2,1,0:T(8,128)(2,1)} %get-tuple-element.161), kind=kLoop, calls=%fused_computation.81 | loop fusion | bytes 16777216
  145.2 10.4 %fusion.49 = (bf16[6,512,1024]{2,1,0:T(8,128)(2,1)}, bf16[6,512,1024]{2,1,0:T(8,128)(2,1)}) fusion(bf16[6,1024,1024]{2,1,0:T(8,128)(2,1)} %constant_dynamic-update-slice_fusion.3), kind=kLoop, calls=%fused_computation.128 | loop fusion | bytes 25165824 | tf_op jit(solution)/shard_map/jit(_take)/gather | solution.py:146
  167.8 54.5 %while.25 = (s32[]{:T(128)}, bf16[2,1024,1024]{2,1,0:T(8,128)(2,1)}, bf16[2]{0:T(256)(128)(2,1)S(1)}, s32[2,2,2]{2,1,0:T(2,128)S(1)}, bf16[2,1024,1024]{2,1,0:T(...) while((s32[]{:T(128)}, bf16[2,1024,1024]{2,1,0:T(8,128)(2,1)}, ...), condition=%wide.region_3.4_spmd, body=%wide.region_2.3_spmd.sunk | while | flops 2712668672 | bytes 27871504 | solution.py:155
  168.0 4.9 %multiply_convert_fusion.8 = (bf16[2,128,1024]{2,1,0:T(8,128)(2,1)S(1)}, bf16[2,128,1024]{2,1,0:T(8,128)(2,1)S(1)}) fusion(s32[2,128]{1,0:T(2,128)S(1)} %get-tuple-element.323), kind=kLoop, calls=%fused_computation.42.clone.2 | loop fusion | flops 4718592 | bytes 1049600 | tf_op jit(solution)/shard_map/while/body/eval_jaxpr/convert_element_type | solution.py:48
  250.2 24.6 %dynamic_update_slice.26 = f32[1536,1536]{1,0:T(8,128)} dynamic-update-slice(f32[1536,1536]{1,0:T(8,128)} %broadcast_in_dim.77, f32[1024,1024]{1,0:T(8,128)} %select_bitcast_fusion, s32[]{:T(128)S(6)} %select_n.266, s32[]{:T(128)S(6)} %select_n.267) | dynamic-update-slice | bytes 8388612 | tf_op jit(solution)/shard_map/dynamic_update_slice | solution.py:93
  274.7 6.8 %bitcast_add_fusion.2 = f32[1024,1024]{1,0:T(8,128)} fusion(f32[1536,1536]{1,0:T(8,128)} %dynamic_update_slice.26, s32[]{:T(128)S(6)} %select_n.268, s32[]{:T(128)S(6)} %select_n.269, bf16[2,1024,1024]{2,1,0:T(8,128)(2,1)} %get-tuple-element.162, pred[]{:T(512)} %bitcast.44), kind=kLoop, calls=%fused_computation.68 | loop fusion | flops 3145728 | bytes 10485769 | tf_op jit(solution)/shard_map/add | solution.py:93
  281.5 24.6 %dynamic_update_slice.27 = f32[1536,1536]{1,0:T(8,128)} dynamic-update-slice(f32[1536,1536]{1,0:T(8,128)} %dynamic_update_slice.26, f32[1024,1024]{1,0:T(8,128)} %bitcast_add_fusion.2, s32[]{:T(128)S(6)} %select_n.268, s32[]{:T(128)S(6)} %select_n.269) | dynamic-update-slice | bytes 8388612 | tf_op jit(solution)/shard_map/dynamic_update_slice | solution.py:93
  306.0 6.8 %bitcast_add_fusion.1 = f32[1024,1024]{1,0:T(8,128)} fusion(f32[1536,1536]{1,0:T(8,128)} %dynamic_update_slice.27, s32[]{:T(128)S(6)} %select_n.273, s32[]{:T(128)S(6)} %select_n.274, bf16[2,1024,1024]{2,1,0:T(8,128)(2,1)} %collective-permute-done.10, pred[]{:T(512)} %bitcast.48), kind=kLoop, calls=%fused_computation.67 | loop fusion | flops 3145728 | bytes 10485769 | tf_op jit(solution)/shard_map/add | solution.py:93
  312.8 24.6 %dynamic_update_slice.28 = f32[1536,1536]{1,0:T(8,128)} dynamic-update-slice(f32[1536,1536]{1,0:T(8,128)} %dynamic_update_slice.27, f32[1024,1024]{1,0:T(8,128)} %bitcast_add_fusion.1, s32[]{:T(128)S(6)} %select_n.273, s32[]{:T(128)S(6)} %select_n.274) | dynamic-update-slice | bytes 8388612 | tf_op jit(solution)/shard_map/dynamic_update_slice | solution.py:93
  337.4 6.8 %bitcast_add_fusion = f32[1024,1024]{1,0:T(8,128)} fusion(f32[1536,1536]{1,0:T(8,128)} %dynamic_update_slice.28, s32[]{:T(128)S(6)} %select_n.278, s32[]{:T(128)S(6)} %select_n.279, bf16[2,1024,1024]{2,1,0:T(8,128)(2,1)} %collective-permute-done.10, pred[]{:T(512)} %bitcast.52), kind=kLoop, calls=%fused_computation.66 | loop fusion | flops 3145728 | bytes 10485769 | tf_op jit(solution)/shard_map/add | solution.py:93
  344.1 24.6 %dynamic_update_slice.29 = f32[1536,1536]{1,0:T(8,128)} dynamic-update-slice(f32[1536,1536]{1,0:T(8,128)} %dynamic_update_slice.28, f32[1024,1024]{1,0:T(8,128)} %bitcast_add_fusion, s32[]{:T(128)S(6)} %select_n.278, s32[]{:T(128)S(6)} %select_n.279) | dynamic-update-slice | bytes 8388612 | tf_op jit(solution)/shard_map/dynamic_update_slice | solution.py:93
  377.5 15.5 %collective-permute-done.11 = bf16[1536,512]{1,0:T(8,128)(2,1)S(1)} collective-permute-done((bf16[1536,512]{1,0:T(8,128)(2,1)S(1)}, bf16[1536,512]{1,0:T(8,128)(2,1)S(1)}, u32[]{:S(2)}, u32[]{:S(2)}) %collective-permute-start.11) | collective-permute-done | bytes 1572896 | tf_op jit(solution)/shard_map/ppermute | solution.py:29
  393.0 32.5 %collective-permute-done.12 = bf16[1536,512]{1,0:T(8,128)(2,1)S(1)} collective-permute-done((bf16[1536,512]{1,0:T(8,128)(2,1)S(1)}, bf16[1536,512]{1,0:T(8,128)(2,1)S(1)}, u32[]{:S(2)}, u32[]{:S(2)}) %collective-permute-start.12) | collective-permute-done | bytes 1572896 | tf_op jit(solution)/shard_map/ppermute | solution.py:29
  435.1 5.2 %collective-permute-done.13 = bf16[512,512]{1,0:T(8,128)(2,1)S(1)} collective-permute-done((bf16[512,512]{1,0:T(8,128)(2,1)S(1)}, bf16[512,512]{1,0:T(8,128)(2,1)S(1)}, u32[]{:S(2)}, u32[]{:S(2)}) %collective-permute-start.13) | collective-permute-done | bytes 524320 | tf_op jit(solution)/shard_map/ppermute | solution.py:29
  (135 shorter events, 124.6 us)
Async XLA Ops:
  0.0 16.4 %collective-permute-start.3 = (bf16[512,512]{1,0:T(8,128)(2,1)}, bf16[512,512]{1,0:T(8,128)(2,1)S(1)}, u32[]{:S(2)}, u32[]{:S(2)}) collective-permute-start(bf16[512,512]{1,0:T(8,128)(2,1)} %param.11), channel_id=1, source_target_pairs={{0,32},{32,64},{64,96},{96,128},{128,160},{160,192},{192,224},{1,3... | collective-permute-start | bytes 1572872 | tf_op jit(solution)/shard_map/ppermute | solution.py:14
  3.7 24.3 %collective-permute-start.4 = (bf16[512,512]{1,0:T(8,128)(2,1)}, bf16[512,512]{1,0:T(8,128)(2,1)S(1)}, u32[]{:S(2)}, u32[]{:S(2)}) collective-permute-start(bf16[512,512]{1,0:T(8,128)(2,1)} %param.11), channel_id=1, source_target_pairs={{32,0},{64,32},{96,64},{128,96},{160,128},{192,160},{224,192},{33,... | collective-permute-start | bytes 1572872 | tf_op jit(solution)/shard_map/ppermute | solution.py:17
  28.0 40.1 %collective-permute-start.5 = (bf16[1536,512]{1,0:T(8,128)(2,1)S(1)}, bf16[1536,512]{1,0:T(8,128)(2,1)S(1)}, u32[]{:S(2)}, u32[]{:S(2)}) collective-permute-start(bf16[1536,512]{1,0:T(8,128)(2,1)S(1)} %constant_dynamic-update-slice_fusion), channel_id=1, source_target_pairs={{0,1},{1,2},{2,3},{3,4},{4,5},{5,6},{6,7},{7,8},{8,9},{9,10},{10,1... | collective-permute-start | bytes 4718600 | tf_op jit(solution)/shard_map/ppermute | solution.py:14
  30.0 38.2 %collective-permute-start.6 = (bf16[1536,512]{1,0:T(8,128)(2,1)S(1)}, bf16[1536,512]{1,0:T(8,128)(2,1)}, u32[]{:S(2)}, u32[]{:S(2)}) collective-permute-start(bf16[1536,512]{1,0:T(8,128)(2,1)S(1)} %constant_dynamic-update-slice_fusion), channel_id=1, source_target_pairs={{1,0},{2,1},{3,2},{4,3},{5,4},{6,5},{7,6},{8,7},{9,8},{10,9},{11,1... | collective-permute-start | bytes 4718600 | tf_op jit(solution)/shard_map/ppermute | solution.py:17
  35.2 36.4 %copy-start.2 = (s32[1,1,4,2]{2,3,1,0:T(2,128)S(1)}, s32[1,1,4,2]{2,3,1,0:T(2,128)}, u32[]{:S(2)}) copy-start(s32[1,1,4,2]{2,3,1,0:T(2,128)} %param.13) | copy-start | bytes 100
  35.2 36.4 %copy-start.4 = (bf16[1,1,4]{2,1,0:T(2,128)(2,1)S(1)}, bf16[1,1,4]{2,1,0:T(2,128)(2,1)}, u32[]{:S(2)}) copy-start(bf16[1,1,4]{2,1,0:T(2,128)(2,1)} %param.14) | copy-start | bytes 28
  116.8 5.2 %copy-start.5 = (s32[1,1,4]{2,1,0:T(1,128)S(1)}, s32[1,1,4]{2,1,0:T(1,128)}, u32[]{:S(2)}) copy-start(s32[1,1,4]{2,1,0:T(1,128)} %param.16) | copy-start | bytes 52
  116.8 5.3 %copy-start.1 = (bf16[1,1,4,2,128,128]{5,4,3,2,1,0:T(8,128)(2,1)S(1)}, bf16[1,1,4,2,128,128]{5,4,3,2,1,0:T(8,128)(2,1)}, u32[]{:S(2)}) copy-start(bf16[1,1,4,2,128,128]{5,4,3,2,1,0:T(8,128)(2,1)} %param.17) | copy-start | bytes 786436
  116.8 5.9 %copy-start.3 = (s32[1,1,4,2,2]{2,4,3,1,0:T(2,128)S(1)}, s32[1,1,4,2,2]{2,4,3,1,0:T(2,128)}, u32[]{:S(2)}) copy-start(s32[1,1,4,2,2]{2,4,3,1,0:T(2,128)} %param.15) | copy-start | bytes 196
  121.4 19.1 %collective-permute-start.7 = (bf16[2,1024,1024]{2,1,0:T(8,128)(2,1)}, bf16[2,1024,1024]{2,1,0:T(8,128)(2,1)}, u32[]{:S(2)}, u32[]{:S(2)}) collective-permute-start(bf16[2,1024,1024]{2,1,0:T(8,128)(2,1)} %constant_dynamic-slice_fusion.2), channel_id=1, source_target_pairs={{0,1},{1,0},{2,3},{3,2},{4,5},{5,4},{6,7},{7,6},{8,9},{9,8},{10,11... | collective-permute-start | bytes 12582920 | tf_op jit(solution)/shard_map/ppermute | solution.py:23
  121.4 7.5 %collective-permute-start = (s32[1]{0:T(128)}, s32[1]{0:T(128)}, u32[]{:S(2)}, u32[]{:S(2)}) collective-permute-start(s32[1]{0:T(128)} %bitcast.23), channel_id=1, source_target_pairs={{0,1},{1,0},{2,3},{3,2},{4,5},{5,4},{6,7},{7,6},{8,9},{9,8},{10,11... | collective-permute-start | bytes 20 | tf_op jit(solution)/shard_map/ppermute | solution.py:23
  122.0 8.8 %collective-permute-start.9 = (s32[2]{0:T(128)S(1)}, s32[2]{0:T(128)S(1)}, u32[]{:S(2)}, u32[]{:S(2)}) collective-permute-start(s32[2]{0:T(128)S(1)} %fusion.41), channel_id=1, source_target_pairs={{0,1},{1,0},{2,3},{3,2},{4,5},{5,4},{6,7},{7,6},{8,9},{9,8},{10,11... | collective-permute-start | bytes 32 | tf_op jit(solution)/shard_map/ppermute | solution.py:23
  122.1 10.1 %collective-permute-start.8 = (bf16[2,2,128,128]{3,2,1,0:T(8,128)(2,1)S(1)}, bf16[2,2,128,128]{3,2,1,0:T(8,128)(2,1)S(1)}, u32[]{:S(2)}, u32[]{:S(2)}) collective-permute-start(bf16[2,2,128,128]{3,2,1,0:T(8,128)(2,1)S(1)} %dynamic-slice_bitcast_fusion.1), channel_id=1, source_target_pairs={{0,1},{1,0},{2,3},{3,2},{4,5},{5,4},{6,7},{7,6},{8,9},{9,8},{10,11... | collective-permute-start | bytes 393224 | tf_op jit(solution)/shard_map/ppermute | solution.py:23
  122.8 8.7 %collective-permute-start.2 = (s32[2,2,2]{2,1,0:T(2,128)S(1)}, s32[2,2,2]{2,1,0:T(2,128)S(1)}, u32[]{:S(2)}, u32[]{:S(2)}) collective-permute-start(s32[2,2,2]{2,1,0:T(2,128)S(1)} %bitcast.148), channel_id=1, source_target_pairs={{0,1},{1,0},{2,3},{3,2},{4,5},{5,4},{6,7},{7,6},{8,9},{9,8},{10,11... | collective-permute-start | bytes 104 | tf_op jit(solution)/shard_map/ppermute | solution.py:23
  128.9 1.1 collective-permute-start.1
  184.3 4.6 %copy-start = (bf16[2,1,256,1024]{3,2,1,0:T(8,128)(2,1)S(1)}, bf16[2,1,256,1024]{3,2,1,0:T(8,128)(2,1)}, u32[]{:S(2)}) copy-start(bf16[2,1,256,1024]{3,2,1,0:T(8,128)(2,1)} %get-tuple-element.326) | copy-start | bytes 3145732 | tf_op jit(solution)/shard_map/while
  211.6 4.6 %copy-start = (bf16[2,1,256,1024]{3,2,1,0:T(8,128)(2,1)S(1)}, bf16[2,1,256,1024]{3,2,1,0:T(8,128)(2,1)}, u32[]{:S(2)}) copy-start(bf16[2,1,256,1024]{3,2,1,0:T(8,128)(2,1)} %get-tuple-element.326) | copy-start | bytes 3145732 | tf_op jit(solution)/shard_map/while
  222.3 83.7 %collective-permute-start.10 = (bf16[2,1024,1024]{2,1,0:T(8,128)(2,1)}, bf16[2,1024,1024]{2,1,0:T(8,128)(2,1)}, u32[]{:S(2)}, u32[]{:S(2)}) collective-permute-start(bf16[2,1024,1024]{2,1,0:T(8,128)(2,1)} %get-tuple-element.162), channel_id=1, source_target_pairs={{0,1},{1,0},{2,3},{3,2},{4,5},{5,4},{6,7},{7,6},{8,9},{9,8},{10,11... | collective-permute-start | bytes 12582920 | tf_op jit(solution)/shard_map/ppermute | solution.py:23
  373.2 19.8 %collective-permute-start.11 = (bf16[1536,512]{1,0:T(8,128)(2,1)S(1)}, bf16[1536,512]{1,0:T(8,128)(2,1)S(1)}, u32[]{:S(2)}, u32[]{:S(2)}) collective-permute-start(bf16[1536,512]{1,0:T(8,128)(2,1)S(1)} %get-tuple-element.212), channel_id=1, source_target_pairs={{1,0},{2,1},{3,2},{4,3},{5,4},{6,5},{7,6},{8,7},{9,8},{10,9},{11,1... | collective-permute-start | bytes 4718600 | tf_op jit(solution)/shard_map/ppermute | solution.py:29
  375.1 50.4 %collective-permute-start.12 = (bf16[1536,512]{1,0:T(8,128)(2,1)S(1)}, bf16[1536,512]{1,0:T(8,128)(2,1)S(1)}, u32[]{:S(2)}, u32[]{:S(2)}) collective-permute-start(bf16[1536,512]{1,0:T(8,128)(2,1)S(1)} %get-tuple-element.213), channel_id=1, source_target_pairs={{0,1},{1,2},{2,3},{3,4},{4,5},{5,6},{6,7},{7,8},{8,9},{9,10},{10,1... | collective-permute-start | bytes 4718600 | tf_op jit(solution)/shard_map/ppermute | solution.py:29
  428.4 12.0 %collective-permute-start.13 = (bf16[512,512]{1,0:T(8,128)(2,1)S(1)}, bf16[512,512]{1,0:T(8,128)(2,1)S(1)}, u32[]{:S(2)}, u32[]{:S(2)}) collective-permute-start(bf16[512,512]{1,0:T(8,128)(2,1)S(1)} %get-tuple-element.214), channel_id=1, source_target_pairs={{32,0},{64,32},{96,64},{128,96},{160,128},{192,160},{224,192},{33,... | collective-permute-start | bytes 1572872 | tf_op jit(solution)/shard_map/ppermute | solution.py:29
  430.3 12.3 %collective-permute-start.14 = (bf16[512,512]{1,0:T(8,128)(2,1)S(1)}, bf16[512,512]{1,0:T(8,128)(2,1)S(1)}, u32[]{:S(2)}, u32[]{:S(2)}) collective-permute-start(bf16[512,512]{1,0:T(8,128)(2,1)S(1)} %get-tuple-element.215), channel_id=1, source_target_pairs={{0,32},{32,64},{64,96},{96,128},{128,160},{160,192},{192,224},{1,3... | collective-permute-start | bytes 1572872 | tf_op jit(solution)/shard_map/ppermute | solution.py:29
where the time goes:
time: 452 us; the launch traced here: 444 us
  local copies, waits for them, and re-layouts  155 us (34%)
  waiting for transfers between devices  115 us (25%)
  other arithmetic  93 us (21%)
  starting transfers between devices  25.5 us (6%)
  loops' own time  23.1 us (5%)
  between operations  17.3 us (4%)
  matrix products  14.9 us (3%)
    dynamic_update_slice x4, local copies, waits for them, and re-layouts, add_patch(): lax.dynamic_update_slice(total, current + update, (offset[0], offset[1]))  98.2 us
    ppermute x4, waiting for transfers between devices, shifted(): lax.ppermute(value, axis, [(source, source + steps) for source in range(f...  55.5 us
    ppermute x2, waiting for transfers between devices, padded(): lax.ppermute(lax.slice_in_dim(block, block.shape[dim] - width, None, axis...  43.4 us
    gather x7, local copies, waits for them, and re-layouts, gather_pool(): jnp.take(jnp.concatenate([own_values, got_values], axis=0), pool_index, a...  21.1 us
    another operation x1, loops' own time, shards(): lax.map(lambda item: beam_window(item[0], item[1]), (offsets, widths))  20.4 us
    add x3, other arithmetic, add_patch(): current + update  20.3 us
    dynamic_update_slice x4, other arithmetic, shards(): lax.map(lambda item: beam_window(item[0], item[1]), (offsets, widths))  19.7 us
    ppermute x4, starting transfers between devices, shifted(): lax.ppermute(value, axis, [(source, source + steps) for source in range(f...  11.1 us
  transfers between devices with their start and end apart: 15, of which 9 were waited for; matrix products, arithmetic and copies ran while one was open for 18% of the time, Pallas kernels for 0%

commit v1 on v0

v1 whole, which is shorter than its diff:
```python
import math

import jax
import jax.numpy as jnp
import ml_dtypes
import numpy as np
from jax import lax
from jax.experimental import pallas as pl
from jax.experimental.pallas import tpu as pltpu
from jax.sharding import PartitionSpec as P

TILE = 512
PATCH = 1024
UVB = 128
BLOCKS = 8
SLOTS = 4
ROWS = 64
VMEM_LIMIT = 56 * 1024 * 1024

COUNT, OFFSET, WIDTH, BINS, USED, META = 0, 1, 9, 13, 29, 33

f32 = jnp.float32
bf16 = jnp.bfloat16


def tables():
    phase = np.outer(np.arange(PATCH), np.arange(PATCH)) % PATCH
    angle = phase * (2.0 * math.pi / PATCH)
    factor = 1.0 / math.sqrt(PATCH)
    cos = (np.cos(angle) * factor).reshape(BLOCKS, UVB, PATCH)
    sin = (np.sin(angle) * factor).reshape(BLOCKS, UVB, PATCH)
    stacked = np.concatenate([cos, sin], axis=1)
    flipped = stacked.transpose(0, 2, 1)
    return stacked.astype(ml_dtypes.bfloat16), np.ascontiguousarray(flipped).astype(ml_dtypes.bfloat16)


def falloff(square, width):
    return jnp.exp(square * (-0.5 / (width * width)))


def row_factor(start, rows, oy, width):
    s = lax.broadcasted_iota(jnp.int32, (rows, 128), 0) + start
    m = ((s - oy) & (PATCH - 1)).astype(f32) - (PATCH // 2)
    return falloff(m * m, width), s


def col_factor(shift, width):
    n = lax.broadcasted_iota(jnp.int32, (8, TILE), 1) + shift
    inside = (n >= 0) & (n < PATCH)
    d = n.astype(f32) - (PATCH // 2)
    return jnp.where(inside, falloff(d * d, width), 0.0)[:1]


def twiddle(a, b, oy, shift):
    i = lax.broadcasted_iota(jnp.int32, (UVB, UVB), 0) + a * UVB
    j = lax.broadcasted_iota(jnp.int32, (UVB, UVB), 1) + b * UVB
    p = j * shift - i * oy
    quarter = (p + PATCH // 8) >> 8
    x = (p - (quarter << 8)).astype(f32) * (2.0 * math.pi / PATCH)
    y = x * x
    sin = x * (1.0 + y * (-1.0 / 6 + y * (1.0 / 120 - y * (1.0 / 5040))))
    cos = 1.0 + y * (-0.5 + y * (1.0 / 24 + y * (-1.0 / 720 + y * (1.0 / 40320))))
    odd = (quarter & 1) == 1
    c = jnp.where(odd, sin, cos)
    s = jnp.where(odd, cos, sin)
    c = jnp.where(((quarter + 1) & 2) == 2, -c, c)
    s = jnp.where((quarter & 2) == 2, -s, s)
    return c, s


def column_shift(step, ox):
    return TILE * (1 - step) - ox


def tile_steps(ctl):
    side = ctl[1]
    return 1 - 2 * side, 2 * side - 1


def lanes():
    return [slice(lane * 128, lane * 128 + 128) for lane in range(TILE // 128)]


def forward_body(kinds, ctl, metas, sky, stacked_hbm, flipped_hbm, outs, scratch):
    own, pair, far = sky
    stacked, flipped, window, sems = scratch
    copy_s = pltpu.make_async_copy(stacked_hbm, stacked, sems.at[0])
    copy_f = pltpu.make_async_copy(flipped_hbm.at[:, :TILE, :], flipped, sems.at[1])
    copy_s.start()
    copy_f.start()
    copy_s.wait()
    copy_f.wait()
    low = ctl[0]
    near, outer = tile_steps(ctl)
    steps = {"own": 0, "near": near, "outer": outer}
    for kind, meta, out in zip(kinds, metas, outs):

        def pointing(s, carry, step=steps[kind], meta=meta, out=out):
            oy, ox = meta[OFFSET + 2 * s], meta[OFFSET + 2 * s + 1]
            width = meta[WIDTH + s].astype(f32)
            shift = column_shift(step, ox)
            cols = col_factor(shift, width)

            def beam_rows(i, c):
                at = pl.multiple_of(i * ROWS, ROWS)
                here = pl.ds(at, ROWS)
                g, rows = row_factor(at, ROWS, oy, width)
                mine = jnp.where(rows >= oy, 1, 0) != low
                g2, _ = row_factor(at + TILE, ROWS, oy, width)
                there = pl.ds(pl.multiple_of(at + TILE, ROWS), ROWS)
                for part in lanes():
                    h = cols[:, part]
                    x = jnp.where(mine, own[here, part].astype(f32), far[here, part].astype(f32))
                    window[here, part] = (x * g * h).astype(bf16)
                    window[there, part] = (pair[here, part].astype(f32) * g2 * h).astype(bf16)
                return c

            lax.fori_loop(0, TILE // ROWS, beam_rows, 0)

            def uv(k, c):
                a = meta[BINS + 4 * s + 2 * k]
                b = meta[BINS + 4 * s + 2 * k + 1]
                first = jnp.dot(stacked[a], window[...], preferred_element_type=f32).astype(bf16)
                q = jnp.dot(first, flipped[b], preferred_element_type=f32)
                re = q[:UVB, :UVB] - q[UVB:, UVB:]
                im = q[:UVB, UVB:] + q[UVB:, :UVB]
                cos, sin = twiddle(a, b, oy, shift)
                out[s, k, :, :UVB] = (re * cos - im * sin).astype(bf16)
                out[s, k, :, UVB:] = (im * cos + re * sin).astype(bf16)
                return c

            lax.fori_loop(0, meta[USED + s], uv, 0)
            return carry

        lax.fori_loop(0, meta[COUNT], pointing, 0)


def forward(kinds, ctl, metas, sky, stacked, flipped):
    n = len(kinds)

    def kernel(ctl, *refs):
        metas, rest = refs[:n], refs[n:]
        forward_body(kinds, ctl, metas, rest[:3], rest[3], rest[4], rest[5 : 5 + n], rest[5 + n :])

    smem = pl.BlockSpec(memory_space=pltpu.SMEM)
    vmem = pl.BlockSpec(memory_space=pltpu.VMEM)
    hbm = pl.BlockSpec(memory_space=pl.ANY)
    shape = jax.ShapeDtypeStruct((SLOTS, 2, UVB, 2 * UVB), bf16)
    return pl.pallas_call(
        kernel,
        out_shape=[shape] * n,
        in_specs=[smem] * (1 + n) + [vmem] * 3 + [hbm] * 2,
        out_specs=[vmem] * n,
        scratch_shapes=[
            pltpu.VMEM((BLOCKS, 2 * UVB, PATCH), bf16),
            pltpu.VMEM((BLOCKS, TILE, 2 * UVB), bf16),
            pltpu.VMEM((PATCH, TILE), bf16),
            pltpu.SemaphoreType.DMA((2,)),
        ],
        compiler_params=pltpu.CompilerParams(vmem_limit_bytes=VMEM_LIMIT),
        name="forward_" + "_".join(kinds),
    )(ctl, *metas, *sky, stacked, flipped)


def scale(meta, mine, near, outer, weight):
    def kernel(meta, mine, near, outer, weight, out):
        def pointing(s, carry):
            def uv(k, c):
                w = weight[s, k].astype(f32)
                v = mine[s, k].astype(f32) + near[s, k].astype(f32) + outer[s, k].astype(f32)
                out[s, k, :, :UVB] = (v[:, :UVB] * w).astype(bf16)
                out[s, k, :, UVB:] = (v[:, UVB:] * w).astype(bf16)
                return c

            lax.fori_loop(0, meta[USED + s], uv, 0)
            return carry

        lax.fori_loop(0, meta[COUNT], pointing, 0)

    smem = pl.BlockSpec(memory_space=pltpu.SMEM)
    vmem = pl.BlockSpec(memory_space=pltpu.VMEM)
    return pl.pallas_call(
        kernel,
        out_shape=jax.ShapeDtypeStruct((SLOTS, 2, UVB, 2 * UVB), bf16),
        in_specs=[smem] + [vmem] * 4,
        out_specs=vmem,
        compiler_params=pltpu.CompilerParams(vmem_limit_bytes=VMEM_LIMIT),
        name="scale",
    )(meta, mine, near, outer, weight)


def adjoint_tile(low, step, meta, scaled, stacked, flipped, spread, totals):
    own, pair, far = totals

    def pointing(s, carry):
        oy, ox = meta[OFFSET + 2 * s], meta[OFFSET + 2 * s + 1]
        width = meta[WIDTH + s].astype(f32)
        shift = column_shift(step, ox)
        cols = col_factor(shift, width)
        used = meta[USED + s]

        def uv(k, c):
            a = meta[BINS + 4 * s + 2 * k]
            b = meta[BINS + 4 * s + 2 * k + 1]
            cos, sin = twiddle(a, b, oy, shift)
            re = scaled[s, k, :, :UVB].astype(f32)
            im = scaled[s, k, :, UVB:].astype(f32)
            mr = (re * cos + im * sin).astype(bf16)
            mi = (im * cos - re * sin).astype(bf16)
            both = jnp.concatenate(
                [jnp.concatenate([mr, mi], axis=1), jnp.concatenate([mi, -mr], axis=1)], axis=0
            )
            spread[k] = jnp.dot(both, stacked[b], preferred_element_type=f32).astype(bf16)
            return c

        lax.fori_loop(0, used, uv, 0)

        def add(count):
            blocks = [meta[BINS + 4 * s + 2 * k] for k in range(count)]
            big = 256

            def image(at):
                back = jnp.dot(flipped[blocks[0], pl.ds(at, big), :], spread[0], preferred_element_type=f32)
                for k in range(1, count):
                    back += jnp.dot(
                        flipped[blocks[k], pl.ds(at, big), :], spread[k], preferred_element_type=f32
                    )
                g, rows = row_factor(at, big, oy, width)
                return [back[:, part] * g * cols[:, part] for part in lanes()], rows

            def rows(i, c):
                at = pl.multiple_of(i * big, big)
                here = pl.ds(at, big)
                values, rows = image(at)
                mine = jnp.where(rows >= oy, 1, 0) != low
                for part, v in zip(lanes(), values):
                    own[here, part] = own[here, part] + jnp.where(mine, v, 0.0)
                    far[here, part] = far[here, part] + jnp.where(mine, 0.0, v)
                values, _ = image(pl.multiple_of(at + TILE, big))
                for part, v in zip(lanes(), values):
                    pair[here, part] = pair[here, part] + v
                return c

            lax.fori_loop(0, TILE // big, rows, 0)

        @pl.when(used == 1)
        def _():
            add(1)

        @pl.when(used == 2)
        def _():
            add(2)

        return carry

    lax.fori_loop(0, meta[COUNT], pointing, 0)


def adjoint_scratch(semaphores):
    return [
        pltpu.VMEM((BLOCKS, 2 * UVB, TILE), bf16),
        pltpu.VMEM((BLOCKS, PATCH, 2 * UVB), bf16),
        pltpu.VMEM((2, 2 * UVB, TILE), bf16),
        pltpu.SemaphoreType.DMA((semaphores,)),
    ]


def adjoint_first(ctl, metas, scaled, stacked, flipped):
    def kernel(ctl, meta0, meta1, sc0, sc1, stacked_hbm, flipped_hbm, own, pair, far, stacked, flipped, spread, sems):
        copy_s = pltpu.make_async_copy(stacked_hbm.at[:, :, :TILE], stacked, sems.at[0])
        copy_f = pltpu.make_async_copy(flipped_hbm, flipped, sems.at[1])
        copy_s.start()
        copy_f.start()

        def clear(i, c):
            at = pl.multiple_of(i * ROWS, ROWS)
            for ref in (own, pair, far):
                ref[pl.ds(at, ROWS), :] = jnp.zeros((ROWS, TILE), f32)
            return c

        lax.fori_loop(0, TILE // ROWS, clear, 0)
        copy_s.wait()
        copy_f.wait()
        near, _ = tile_steps(ctl)
        totals = (own, pair, far)
        adjoint_tile(ctl[0], 0, meta0, sc0, stacked, flipped, spread, totals)
        adjoint_tile(ctl[0], near, meta1, sc1, stacked, flipped, spread, totals)

    smem = pl.BlockSpec(memory_space=pltpu.SMEM)
    vmem = pl.BlockSpec(memory_space=pltpu.VMEM)
    hbm = pl.BlockSpec(memory_space=pl.ANY)
    return pl.pallas_call(
        kernel,
        out_shape=[jax.ShapeDtypeStruct((TILE, TILE), f32)] * 3,
        in_specs=[smem] * 3 + [vmem] * 2 + [hbm] * 2,
        out_specs=[vmem] * 3,
        scratch_shapes=adjoint_scratch(2),
        compiler_params=pltpu.CompilerParams(vmem_limit_bytes=VMEM_LIMIT),
        name="adjoint_first",
    )(ctl, *metas, *scaled, stacked, flipped)


def adjoint_last(ctl, meta, scaled, begun, stacked, flipped):
    def kernel(ctl, meta, sc, own0, pair0, far0, stacked_hbm, flipped_hbm, own, pair_out, far_out, *scratch):
        stacked, flipped, spread, sems, pair, far = scratch
        copies = [
            pltpu.make_async_copy(own0, own, sems.at[0]),
            pltpu.make_async_copy(pair0, pair, sems.at[1]),
            pltpu.make_async_copy(far0, far, sems.at[2]),
            pltpu.make_async_copy(stacked_hbm.at[:, :, :TILE], stacked, sems.at[3]),
            pltpu.make_async_copy(flipped_hbm, flipped, sems.at[4]),
        ]
        for copy in copies:
            copy.start()
        for copy in copies:
            copy.wait()
        _, outer = tile_steps(ctl)
        adjoint_tile(ctl[0], outer, meta, sc, stacked, flipped, spread, (own, pair, far))

        def emit(i, c):
            here = pl.ds(pl.multiple_of(i * ROWS, ROWS), ROWS)
            pair_out[here, :] = pair[here, :].astype(bf16)
            far_out[here, :] = far[here, :].astype(bf16)
            return c

        lax.fori_loop(0, TILE // ROWS, emit, 0)

    smem = pl.BlockSpec(memory_space=pltpu.SMEM)
    vmem = pl.BlockSpec(memory_space=pltpu.VMEM)
    hbm = pl.BlockSpec(memory_space=pl.ANY)
    return pl.pallas_call(
        kernel,
        out_shape=[
            jax.ShapeDtypeStruct((TILE, TILE), f32),
            jax.ShapeDtypeStruct((TILE, TILE), bf16),
            jax.ShapeDtypeStruct((TILE, TILE), bf16),
        ],
        in_specs=[smem] * 2 + [vmem] + [hbm] * 5,
        out_specs=[vmem] * 3,
        scratch_shapes=adjoint_scratch(5) + [pltpu.VMEM((TILE, TILE), f32)] * 2,
        compiler_params=pltpu.CompilerParams(vmem_limit_bytes=VMEM_LIMIT),
        name="adjoint_last",
    )(ctl, meta, scaled, *begun, stacked, flipped)


def mesh_moves(rows, cols):
    def pairs(move):
        made = []
        for r in range(rows):
            for c in range(cols):
                r2, c2 = move(r, c)
                if 0 <= r2 < rows and 0 <= c2 < cols:
                    made.append((r * cols + c, r2 * cols + c2))
        return made

    def outer(c):
        return c + 1 if c % 2 else c - 1

    return {
        "row_pair": pairs(lambda r, c: (r ^ 1, c)),
        "row_out": pairs(lambda r, c: (r + 2 if r % 2 else r - 2, c)),
        "row_back": pairs(lambda r, c: (r - 2 if r % 2 else r + 2, c)),
        "near": pairs(lambda r, c: (r, c ^ 1)),
        "outer": pairs(lambda r, c: (r, outer(c))),
        "row_pair_near": pairs(lambda r, c: (r ^ 1, c ^ 1)),
        "row_pair_outer": pairs(lambda r, c: (r ^ 1, outer(c))),
    }


def solution(mesh):
    moves = mesh_moves(mesh.shape["ty"], mesh.shape["tx"])
    stacked_np, flipped_np = tables()

    def send(x, what):
        return lax.ppermute(x, ("ty", "tx"), moves[what])

    def shards(sky, point_count, point_offset, beam_width, uv_bins, uv_count, uv_weight):
        stacked, flipped = jnp.asarray(stacked_np), jnp.asarray(flipped_np)
        ctl = jnp.stack([lax.axis_index("ty") % 2, lax.axis_index("tx") % 2]).astype(jnp.int32)
        meta = jnp.concatenate(
            [
                point_count.reshape(1),
                point_offset.reshape(2 * SLOTS),
                beam_width.reshape(SLOTS).astype(jnp.int32),
                uv_bins.reshape(4 * SLOTS),
                uv_count.reshape(SLOTS),
            ]
        )
        pair_sky = send(sky, "row_pair")
        far_sky = send(sky, "row_out")
        meta_own = send(meta, "row_pair")
        meta_near = send(meta, "row_pair_near")
        meta_outer = send(meta, "row_pair_outer")
        weight = send(uv_weight[0, 0], "row_pair")
        skies = (sky, pair_sky, far_sky)
        (v_outer,) = forward(("outer",), ctl, (meta_outer,), skies, stacked, flipped)
        from_outer = send(v_outer, "outer")
        v_own, v_near = forward(("own", "near"), ctl, (meta_own, meta_near), skies, stacked, flipped)
        from_near = send(v_near, "near")
        scaled = scale(meta_own, v_own, from_near, from_outer, weight)
        scaled_outer = send(scaled, "outer")
        scaled_near = send(scaled, "near")
        begun = adjoint_first(ctl, (meta_own, meta_near), (scaled, scaled_near), stacked, flipped)
        own, pair, far = adjoint_last(ctl, meta_outer, scaled_outer, begun, stacked, flipped)
        return own + send(pair, "row_pair").astype(f32) + send(far, "row_back").astype(f32)

    in_specs = (
        P("ty", "tx"),
        P("ty", "tx"),
        P("ty", "tx", None, None),
        P("ty", "tx", None),
        P("ty", "tx", None, None, None),
        P("ty", "tx", None),
        P("ty", "tx", None, None, None, None),
    )
    return jax.shard_map(shards, mesh=mesh, in_specs=in_specs, out_specs=P("ty", "tx"), check_vma=False)
```

time: 452 us -> 114 us (0.25)
  the two profiles are of different devices: /device:TPU:6 before, /device:TPU:115 now
where the time goes in v1:
time: 114 us; the launch traced here: 113 us
  waiting for transfers between devices  40.9 us (36%)
  Pallas kernels  37.7 us (33%)
  starting transfers between devices  22.4 us (20%)
  local copies, waits for them, and re-layouts  7.18 us (6%)
  other arithmetic  3.72 us (3%)
    ppermute x12, waiting for transfers between devices, send(): return lax.ppermute(x, ('ty', 'tx'), moves[what])  40.9 us
    ppermute x12, starting transfers between devices, send(): return lax.ppermute(x, ('ty', 'tx'), moves[what])  22.4 us
    pallas_call x2, Pallas kernels, forward(): pl.pallas_call(kernel, out_shape=[shape] * n, in_specs=[smem] * (1 + n) +...  17.6 us
    pallas_call x1, Pallas kernels, adjoint_last(): pl.pallas_call(kernel, out_shape=[jax.ShapeDtypeStruct((TILE, TILE), f32)...  9.41 us
    pallas_call x1, Pallas kernels, adjoint_first(): pl.pallas_call(kernel, out_shape=[jax.ShapeDtypeStruct((TILE, TILE), f32)...  8.36 us
    unnamed x24, local copies, waits for them, and re-layouts  6.28 us
    add x1, other arithmetic, shards(): own + send(pair, 'row_pair').astype(f32) + send(far, 'row_back').astype(f32)  2.4 us
    pallas_call x1, Pallas kernels, scale(): pl.pallas_call(kernel, out_shape=jax.ShapeDtypeStruct((SLOTS, 2, UVB, 2 *...  2.37 us
  transfers between devices with their start and end apart: 12, of which 5 were waited for; matrix products, arithmetic and copies ran while one was open for 3% of the time, Pallas kernels for 23%

profile of v1, /device:TPU:115, one launch (start us, length us, event | category | flops | bytes accessed | tf_op | source)
XLA Modules:
  0.0 112.7 jit_solution(701070033533114034)
XLA Ops:
  0.0 2.9 %collective-permute-start.4 = (bf16[512,512]{1,0:T(8,128)(2,1)}, bf16[512,512]{1,0:T(8,128)(2,1)S(1)}, u32[]{:S(2)}, u32[]{:S(2)}) collective-permute-start(bf16[512,512]{1,0:T(8,128)(2,1)} %refs_1_.1), channel_id=1, source_target_pairs={{32,96},{33,97},{34,98},{35,99},{36,100},{37,101},{38,102},{39,103... | collective-permute-start | bytes 1572872 | tf_op jit(solution)/shard_map/ppermute | solution.py:375
  3.7 0.8 copy.12
  4.5 0.8 copy.13
  6.0 0.7 concatenate.3
  6.8 2.6 %collective-permute-start.2 = (s32[33]{0:T(128)S(1)}, s32[33]{0:T(128)S(1)}, u32[]{:S(2)}, u32[]{:S(2)}) collective-permute-start(s32[33]{0:T(128)S(1)} %concatenate.3), channel_id=1, source_target_pairs={{0,33},{1,32},{2,35},{3,34},{4,37},{5,36},{6,39},{7,38},{8,41},{9,... | collective-permute-start | bytes 404 | tf_op jit(solution)/shard_map/ppermute | solution.py:375
  9.3 3.5 %collective-permute-start = (s32[33]{0:T(128)S(1)}, s32[33]{0:T(128)S(1)}, u32[]{:S(2)}, u32[]{:S(2)}) collective-permute-start(s32[33]{0:T(128)S(1)} %concatenate.3), channel_id=1, source_target_pairs={{1,34},{2,33},{3,36},{4,35},{5,38},{6,37},{7,40},{8,39},{9,42},{10... | collective-permute-start | bytes 404 | tf_op jit(solution)/shard_map/ppermute | solution.py:375
  13.5 3.7 %collective-permute-done.2.refs_1_.meta1 = s32[33]{0:T(128)S(1)} collective-permute-done((s32[33]{0:T(128)S(1)}, s32[33]{0:T(128)S(1)}, u32[]{:S(2)}, u32[]{:S(2)}) %collective-permute-start.2) | collective-permute-done | bytes 164 | tf_op jit(solution)/shard_map/ppermute | solution.py:375
  18.0 0.8 copy-done.1
  18.8 8.6 %forward_own_near.1 = (bf16[4,2,128,256]{3,2,1,0:T(8,128)(2,1)}, bf16[4,2,128,256]{3,2,1,0:T(8,128)(2,1)}) custom-call(s32[2]{0:T(128)} %pad_add_fusion.ctl, s32[33]{0:T(128)} %copy-done.7, s32[33]{0:T(128)} %copy-done.9, bf16[512,512]{1,0:T(8,128)(2,1)} %refs_1_.1, bf16[512,512]{1,0:T(8,128)(2,1)} %copy-done.1, bf16[512,512]{1,0:T(8,128)(2,1)} %copy-done, ...), custom_call_target="tpu_custom_call" | custom-call | tf_op jit(solution)/shard_map/forward_own_near/pallas_call | solution.py:149
  28.4 9.0 %forward_outer.1 = bf16[4,2,128,256]{3,2,1,0:T(8,128)(2,1)} custom-call(s32[2]{0:T(128)} %pad_add_fusion.ctl, s32[33]{0:T(128)} %copy-done.8, bf16[512,512]{1,0:T(8,128)(2,1)} %refs_1_.1, bf16[512,512]{1,0:T(8,128)(2,1)} %copy-done.1, bf16[512,512]{1,0:T(8,128)(2,1)} %copy-done, bf16[8,256,1024]{2,1,0:T(8,128)(2,1)} %constant.30.clone.refs_5_.refs_4_.stacked_hbm, ...), custom_call_target="tpu_custom_call" | custom-call | tf_op jit(solution)/shard_map/forward_outer/pallas_call | solution.py:149
  37.4 6.4 %collective-permute-start.6 = (bf16[4,2,128,256]{3,2,1,0:T(8,128)(2,1)}, bf16[4,2,128,256]{3,2,1,0:T(8,128)(2,1)S(1)}, u32[]{:S(2)}, u32[]{:S(2)}) collective-permute-start(bf16[4,2,128,256]{3,2,1,0:T(8,128)(2,1)} %forward_outer.1), channel_id=1, source_target_pairs={{1,2},{2,1},{3,4},{4,3},{5,6},{6,5},{7,8},{8,7},{9,10},{10,9},{11,... | collective-permute-start | bytes 1572872 | tf_op jit(solution)/shard_map/ppermute | solution.py:375
  43.9 17.4 %collective-permute-done.7.weight = bf16[4,2,128,128]{3,2,1,0:T(8,128)(2,1)S(1)} collective-permute-done((bf16[4,2,128,128]{3,2,1,0:T(8,128)(2,1)S(1)}, bf16[4,2,128,128]{3,2,1,0:T(8,128)(2,1)S(1)}, u32[]{:S(2)}, u32[]{:S(2)}) %collective-permute-start.7) | collective-permute-done | bytes 262176 | tf_op jit(solution)/shard_map/ppermute | solution.py:375
  62.4 2.4 %scale.1.sc0 = bf16[4,2,128,256]{3,2,1,0:T(8,128)(2,1)} custom-call(s32[33]{0:T(128)} %copy-done.7, bf16[4,2,128,256]{3,2,1,0:T(8,128)(2,1)} %get-tuple-element.13.mine, bf16[4,2,128,256]{3,2,1,0:T(8,128)(2,1)} %copy-done.2, bf16[4,2,128,256]{3,2,1,0:T(8,128)(2,1)} %copy-done.4, bf16[4,2,128,128]{3,2,1,0:T(8,128)(2,1)} %copy-done.6), custom_call_target="tpu_custom_call" | custom-call | tf_op jit(solution)/shard_map/scale/pallas_call | solution.py:182
  64.8 2.9 %collective-permute-start.8 = (bf16[4,2,128,256]{3,2,1,0:T(8,128)(2,1)}, bf16[4,2,128,256]{3,2,1,0:T(8,128)(2,1)S(1)}, u32[]{:S(2)}, u32[]{:S(2)}) collective-permute-start(bf16[4,2,128,256]{3,2,1,0:T(8,128)(2,1)} %scale.1.sc0), channel_id=1, source_target_pairs={{1,2},{2,1},{3,4},{4,3},{5,6},{6,5},{7,8},{8,7},{9,10},{10,9},{11,... | collective-permute-start | bytes 1572872 | tf_op jit(solution)/shard_map/ppermute | solution.py:375
  67.7 0.8 copy-done.5
  68.5 8.4 %adjoint_first.1 = (f32[512,512]{1,0:T(8,128)}, f32[512,512]{1,0:T(8,128)}, f32[512,512]{1,0:T(8,128)}) custom-call(s32[2]{0:T(128)} %pad_add_fusion.ctl, s32[33]{0:T(128)} %copy-done.7, s32[33]{0:T(128)} %copy-done.9, bf16[4,2,128,256]{3,2,1,0:T(8,128)(2,1)} %scale.1.sc0, bf16[4,2,128,256]{3,2,1,0:T(8,128)(2,1)} %copy-done.5, ...), custom_call_target="tpu_custom_call" | custom-call | tf_op jit(solution)/shard_map/adjoint_first/pallas_call | solution.py:292
  76.8 5.8 %collective-permute-done.8.sc = bf16[4,2,128,256]{3,2,1,0:T(8,128)(2,1)S(1)} collective-permute-done((bf16[4,2,128,256]{3,2,1,0:T(8,128)(2,1)}, bf16[4,2,128,256]{3,2,1,0:T(8,128)(2,1)S(1)}, u32[]{:S(2)}, u32[]{:S(2)}) %collective-permute-start.8) | collective-permute-done | bytes 524320 | tf_op jit(solution)/shard_map/ppermute | solution.py:375
  82.6 0.8 copy-done.3
  83.4 9.4 %adjoint_last.1 = (f32[512,512]{1,0:T(8,128)}, bf16[512,512]{1,0:T(8,128)(2,1)}, bf16[512,512]{1,0:T(8,128)(2,1)}) custom-call(s32[2]{0:T(128)} %pad_add_fusion.ctl, s32[33]{0:T(128)} %copy-done.8, bf16[4,2,128,256]{3,2,1,0:T(8,128)(2,1)} %copy-done.3, f32[512,512]{1,0:T(8,128)} %get-tuple-element.15.own0, f32[512,512]{1,0:T(8,128)} %get-tuple-element.16.pair0, ...), custom_call_target="tpu_custom_call" | custom-call | tf_op jit(solution)/shard_map/adjoint_last/pallas_call | solution.py:331
  92.8 1.6 %collective-permute-start.10 = (bf16[512,512]{1,0:T(8,128)(2,1)}, bf16[512,512]{1,0:T(8,128)(2,1)S(1)}, u32[]{:S(2)}, u32[]{:S(2)}) collective-permute-start(bf16[512,512]{1,0:T(8,128)(2,1)} %get-tuple-element.19), channel_id=1, source_target_pairs={{0,32},{1,33},{2,34},{3,35},{4,36},{5,37},{6,38},{7,39},{8,40},{9,... | collective-permute-start | bytes 1572872 | tf_op jit(solution)/shard_map/ppermute | solution.py:375
  94.4 1.9 %collective-permute-start.11 = (bf16[512,512]{1,0:T(8,128)(2,1)}, bf16[512,512]{1,0:T(8,128)(2,1)S(1)}, u32[]{:S(2)}, u32[]{:S(2)}) collective-permute-start(bf16[512,512]{1,0:T(8,128)(2,1)} %get-tuple-element.20), channel_id=1, source_target_pairs={{0,64},{1,65},{2,66},{3,67},{4,68},{5,69},{6,70},{7,71},{8,72},{9,... | collective-permute-start | bytes 1572872 | tf_op jit(solution)/shard_map/ppermute | solution.py:375
  96.3 10.4 %collective-permute-done.10 = bf16[512,512]{1,0:T(8,128)(2,1)S(1)} collective-permute-done((bf16[512,512]{1,0:T(8,128)(2,1)}, bf16[512,512]{1,0:T(8,128)(2,1)S(1)}, u32[]{:S(2)}, u32[]{:S(2)}) %collective-permute-start.10) | collective-permute-done | bytes 524320 | tf_op jit(solution)/shard_map/ppermute | solution.py:375
  106.6 3.6 %collective-permute-done.11 = bf16[512,512]{1,0:T(8,128)(2,1)S(1)} collective-permute-done((bf16[512,512]{1,0:T(8,128)(2,1)}, bf16[512,512]{1,0:T(8,128)(2,1)S(1)}, u32[]{:S(2)}, u32[]{:S(2)}) %collective-permute-start.11) | collective-permute-done | bytes 524320 | tf_op jit(solution)/shard_map/ppermute | solution.py:375
  110.3 2.4 %convert_add_fusion = f32[512,512]{1,0:T(8,128)} fusion(bf16[512,512]{1,0:T(8,128)(2,1)S(1)} %collective-permute-done.11, f32[512,512]{1,0:T(8,128)} %get-tuple-element.18, bf16[512,512]{1,0:T(8,128)(2,1)S(1)} %collective-permute-done.10), kind=kLoop, calls=%fused_computation | loop fusion | flops 1048576 | bytes 3145728 | tf_op jit(solution)/shard_map/add | solution.py:405
  (35 shorter events, 4.6 us)
Async XLA Ops:
  0.0 17.1 %collective-permute-start.4 = (bf16[512,512]{1,0:T(8,128)(2,1)}, bf16[512,512]{1,0:T(8,128)(2,1)S(1)}, u32[]{:S(2)}, u32[]{:S(2)}) collective-permute-start(bf16[512,512]{1,0:T(8,128)(2,1)} %refs_1_.1), channel_id=1, source_target_pairs={{32,96},{33,97},{34,98},{35,99},{36,100},{37,101},{38,102},{39,103... | collective-permute-start | bytes 1572872 | tf_op jit(solution)/shard_map/ppermute | solution.py:375
  2.9 14.3 %collective-permute-start.3 = (bf16[512,512]{1,0:T(8,128)(2,1)}, bf16[512,512]{1,0:T(8,128)(2,1)S(1)}, u32[]{:S(2)}, u32[]{:S(2)}) collective-permute-start(bf16[512,512]{1,0:T(8,128)(2,1)} %refs_1_.1), channel_id=1, source_target_pairs={{0,32},{1,33},{2,34},{3,35},{4,36},{5,37},{6,38},{7,39},{8,40},{9,... | collective-permute-start | bytes 1572872 | tf_op jit(solution)/shard_map/ppermute | solution.py:375
  6.8 10.4 %collective-permute-start.2 = (s32[33]{0:T(128)S(1)}, s32[33]{0:T(128)S(1)}, u32[]{:S(2)}, u32[]{:S(2)}) collective-permute-start(s32[33]{0:T(128)S(1)} %concatenate.3), channel_id=1, source_target_pairs={{0,33},{1,32},{2,35},{3,34},{4,37},{5,36},{6,39},{7,38},{8,41},{9,... | collective-permute-start | bytes 404 | tf_op jit(solution)/shard_map/ppermute | solution.py:375
  9.3 7.8 %collective-permute-start.1 = (s32[33]{0:T(128)S(1)}, s32[33]{0:T(128)S(1)}, u32[]{:S(2)}, u32[]{:S(2)}) collective-permute-start(s32[33]{0:T(128)S(1)} %concatenate.3), channel_id=1, source_target_pairs={{0,32},{1,33},{2,34},{3,35},{4,36},{5,37},{6,38},{7,39},{8,40},{9,... | collective-permute-start | bytes 404 | tf_op jit(solution)/shard_map/ppermute | solution.py:375
  9.3 18.6 %collective-permute-start = (s32[33]{0:T(128)S(1)}, s32[33]{0:T(128)S(1)}, u32[]{:S(2)}, u32[]{:S(2)}) collective-permute-start(s32[33]{0:T(128)S(1)} %concatenate.3), channel_id=1, source_target_pairs={{1,34},{2,33},{3,36},{4,35},{5,38},{6,37},{7,40},{8,39},{9,42},{10... | collective-permute-start | bytes 404 | tf_op jit(solution)/shard_map/ppermute | solution.py:375
  17.1 0.5 copy-start.9
  17.1 0.5 copy-start.7
  17.2 0.8 copy-start
  18.0 0.8 copy-start.1
  27.3 16.5 %copy-start.10 = (bf16[1,1,4,2,128,128]{5,4,3,2,1,0:T(8,128)(2,1)S(1)}, bf16[1,1,4,2,128,128]{5,4,3,2,1,0:T(8,128)(2,1)}, u32[]{:S(2)}) copy-start(bf16[1,1,4,2,128,128]{5,4,3,2,1,0:T(8,128)(2,1)} %param.15) | copy-start | bytes 786436
  27.3 34.0 %collective-permute-start.5 = (bf16[4,2,128,256]{3,2,1,0:T(8,128)(2,1)}, bf16[4,2,128,256]{3,2,1,0:T(8,128)(2,1)S(1)}, u32[]{:S(2)}, u32[]{:S(2)}) collective-permute-start(bf16[4,2,128,256]{3,2,1,0:T(8,128)(2,1)} %get-tuple-element.14), channel_id=1, source_target_pairs={{0,1},{1,0},{2,3},{3,2},{4,5},{5,4},{6,7},{7,6},{8,9},{9,8},{10,11... | collective-permute-start | bytes 1572872 | tf_op jit(solution)/shard_map/ppermute | solution.py:375
  27.9 0.5 copy-start.8
  37.4 23.9 %collective-permute-start.6 = (bf16[4,2,128,256]{3,2,1,0:T(8,128)(2,1)}, bf16[4,2,128,256]{3,2,1,0:T(8,128)(2,1)S(1)}, u32[]{:S(2)}, u32[]{:S(2)}) collective-permute-start(bf16[4,2,128,256]{3,2,1,0:T(8,128)(2,1)} %forward_outer.1), channel_id=1, source_target_pairs={{1,2},{2,1},{3,4},{4,3},{5,6},{6,5},{7,8},{8,7},{9,10},{10,9},{11,... | collective-permute-start | bytes 1572872 | tf_op jit(solution)/shard_map/ppermute | solution.py:375
  43.8 17.5 %collective-permute-start.7 = (bf16[4,2,128,128]{3,2,1,0:T(8,128)(2,1)S(1)}, bf16[4,2,128,128]{3,2,1,0:T(8,128)(2,1)S(1)}, u32[]{:S(2)}, u32[]{:S(2)}) collective-permute-start(bf16[4,2,128,128]{3,2,1,0:T(8,128)(2,1)S(1)} %bitcast.10), channel_id=1, source_target_pairs={{0,32},{1,33},{2,34},{3,35},{4,36},{5,37},{6,38},{7,39},{8,40},{9,... | collective-permute-start | bytes 786440 | tf_op jit(solution)/shard_map/ppermute | solution.py:375
  61.4 0.7 copy-start.6
  61.4 0.9 copy-start.2
  61.4 1.0 copy-start.4
  64.8 2.9 %collective-permute-start.9 = (bf16[4,2,128,256]{3,2,1,0:T(8,128)(2,1)}, bf16[4,2,128,256]{3,2,1,0:T(8,128)(2,1)S(1)}, u32[]{:S(2)}, u32[]{:S(2)}) collective-permute-start(bf16[4,2,128,256]{3,2,1,0:T(8,128)(2,1)} %scale.1.sc0), channel_id=1, source_target_pairs={{0,1},{1,0},{2,3},{3,2},{4,5},{5,4},{6,7},{7,6},{8,9},{9,8},{10,11... | collective-permute-start | bytes 1572872 | tf_op jit(solution)/shard_map/ppermute | solution.py:375
  64.8 17.8 %collective-permute-start.8 = (bf16[4,2,128,256]{3,2,1,0:T(8,128)(2,1)}, bf16[4,2,128,256]{3,2,1,0:T(8,128)(2,1)S(1)}, u32[]{:S(2)}, u32[]{:S(2)}) collective-permute-start(bf16[4,2,128,256]{3,2,1,0:T(8,128)(2,1)} %scale.1.sc0), channel_id=1, source_target_pairs={{1,2},{2,1},{3,4},{4,3},{5,6},{6,5},{7,8},{8,7},{9,10},{10,9},{11,... | collective-permute-start | bytes 1572872 | tf_op jit(solution)/shard_map/ppermute | solution.py:375
  67.7 0.8 copy-start.5
  82.6 0.8 copy-start.3
  92.8 13.8 %collective-permute-start.10 = (bf16[512,512]{1,0:T(8,128)(2,1)}, bf16[512,512]{1,0:T(8,128)(2,1)S(1)}, u32[]{:S(2)}, u32[]{:S(2)}) collective-permute-start(bf16[512,512]{1,0:T(8,128)(2,1)} %get-tuple-element.19), channel_id=1, source_target_pairs={{0,32},{1,33},{2,34},{3,35},{4,36},{5,37},{6,38},{7,39},{8,40},{9,... | collective-permute-start | bytes 1572872 | tf_op jit(solution)/shard_map/ppermute | solution.py:375
  94.4 15.9 %collective-permute-start.11 = (bf16[512,512]{1,0:T(8,128)(2,1)}, bf16[512,512]{1,0:T(8,128)(2,1)S(1)}, u32[]{:S(2)}, u32[]{:S(2)}) collective-permute-start(bf16[512,512]{1,0:T(8,128)(2,1)} %get-tuple-element.20), channel_id=1, source_target_pairs={{0,64},{1,65},{2,66},{3,67},{4,68},{5,69},{6,70},{7,71},{8,72},{9,... | collective-permute-start | bytes 1572872 | tf_op jit(solution)/shard_map/ppermute | solution.py:375

commit v2 on v1

--- a/solution.py
+++ b/solution.py
@@ -15,9 +15,9 @@
 BLOCKS = 8
 SLOTS = 4
 ROWS = 64
-VMEM_LIMIT = 56 * 1024 * 1024
-
-COUNT, OFFSET, WIDTH, BINS, USED, META = 0, 1, 9, 13, 29, 33
+VMEM_LIMIT = 24 * 1024 * 1024
+
+OFFSET, WIDTH, BINS, USED, COUNT = 0, 2, 3, 7, 8
 
 f32 = jnp.float32
 bf16 = jnp.bfloat16
@@ -32,6 +32,15 @@
     stacked = np.concatenate([cos, sin], axis=1)
     flipped = stacked.transpose(0, 2, 1)
     return stacked.astype(ml_dtypes.bfloat16), np.ascontiguousarray(flipped).astype(ml_dtypes.bfloat16)
+
+
+def near_by(*arrays):
+    return [pltpu.with_memory_space_constraint(x, pltpu.VMEM) for x in arrays]
+
+
+def cost(pointings):
+    once = 2 * 2 * UVB * TILE * (PATCH + 2 * UVB)
+    return pl.CostEstimate(flops=int(1.5 * pointings * once), transcendentals=0, bytes_accessed=1 << 20)
 
 
 def falloff(square, width):
@@ -81,23 +90,39 @@
     return [slice(lane * 128, lane * 128 + 128) for lane in range(TILE // 128)]
 
 
-def forward_body(kinds, ctl, metas, sky, stacked_hbm, flipped_hbm, outs, scratch):
+def stage(sky, stacked, flipped):
+    def kernel(*refs):
+        sems = refs[6]
+        copies = [pltpu.make_async_copy(refs[i], refs[3 + i], sems.at[i]) for i in range(3)]
+        for copy in copies:
+            copy.start()
+        for copy in copies:
+            copy.wait()
+
+    arrays = (sky, stacked, flipped)
+    return pl.pallas_call(
+        kernel,
+        out_shape=[pltpu.VMEM(x.shape, bf16) for x in arrays],
+        in_specs=[pl.BlockSpec(memory_space=pltpu.HBM)] * 3,
+        out_specs=[pl.BlockSpec(memory_space=pltpu.VMEM)] * 3,
+        scratch_shapes=[pltpu.SemaphoreType.DMA((3,))],
+        cost_estimate=pl.CostEstimate(flops=0, transcendentals=0, bytes_accessed=18 << 20),
+        compiler_params=pltpu.CompilerParams(vmem_limit_bytes=VMEM_LIMIT),
+        name="stage",
+    )(*[pltpu.with_memory_space_constraint(x, pltpu.HBM) for x in arrays])
+
+
+def forward_body(kinds, ctl, metas, sky, stacked, flipped, outs, scratch):
     own, pair, far = sky
-    stacked, flipped, window, sems = scratch
-    copy_s = pltpu.make_async_copy(stacked_hbm, stacked, sems.at[0])
-    copy_f = pltpu.make_async_copy(flipped_hbm.at[:, :TILE, :], flipped, sems.at[1])
-    copy_s.start()
-    copy_f.start()
-    copy_s.wait()
-    copy_f.wait()
+    (window,) = scratch
     low = ctl[0]
     near, outer = tile_steps(ctl)
     steps = {"own": 0, "near": near, "outer": outer}
     for kind, meta, out in zip(kinds, metas, outs):
 
         def pointing(s, carry, step=steps[kind], meta=meta, out=out):
-            oy, ox = meta[OFFSET + 2 * s], meta[OFFSET + 2 * s + 1]
-            width = meta[WIDTH + s].astype(f32)
+            oy, ox = meta[OFFSET, s], meta[OFFSET + 1, s]
+            width = meta[WIDTH, s].astype(f32)
             shift = column_shift(step, ox)
             cols = col_factor(shift, width)
 
@@ -118,21 +143,21 @@
             lax.fori_loop(0, TILE // ROWS, beam_rows, 0)
 
             def uv(k, c):
-                a = meta[BINS + 4 * s + 2 * k]
-                b = meta[BINS + 4 * s + 2 * k + 1]
+                a = meta[BINS + 2 * k, s]
+                b = meta[BINS + 2 * k + 1, s]
                 first = jnp.dot(stacked[a], window[...], preferred_element_type=f32).astype(bf16)
-                q = jnp.dot(first, flipped[b], preferred_element_type=f32)
+                q = jnp.dot(first, flipped[b, :TILE, :], preferred_element_type=f32)
                 re = q[:UVB, :UVB] - q[UVB:, UVB:]
                 im = q[:UVB, UVB:] + q[UVB:, :UVB]
                 cos, sin = twiddle(a, b, oy, shift)
-                out[s, k, :, :UVB] = (re * cos - im * sin).astype(bf16)
-                out[s, k, :, UVB:] = (im * cos + re * sin).astype(bf16)
+                out[s, k, :, :UVB] = (re * cos - im * sin).astype(out.dtype)
+                out[s, k, :, UVB:] = (im * cos + re * sin).astype(out.dtype)
                 return c
 
-            lax.fori_loop(0, meta[USED + s], uv, 0)
+            lax.fori_loop(0, meta[USED, s], uv, 0)
             return carry
 
-        lax.fori_loop(0, meta[COUNT], pointing, 0)
+        lax.fori_loop(0, meta[COUNT, 0], pointing, 0)
 
 
 def forward(kinds, ctl, metas, sky, stacked, flipped):
@@ -144,64 +169,85 @@
 
     smem = pl.BlockSpec(memory_space=pltpu.SMEM)
     vmem = pl.BlockSpec(memory_space=pltpu.VMEM)
-    hbm = pl.BlockSpec(memory_space=pl.ANY)
-    shape = jax.ShapeDtypeStruct((SLOTS, 2, UVB, 2 * UVB), bf16)
-    return pl.pallas_call(
-        kernel,
-        out_shape=[shape] * n,
-        in_specs=[smem] * (1 + n) + [vmem] * 3 + [hbm] * 2,
+    return pl.pallas_call(
+        kernel,
+        out_shape=[pltpu.VMEM((SLOTS, 2, UVB, 2 * UVB), f32 if k == "own" else bf16) for k in kinds],
+        in_specs=[smem] * (1 + n) + [vmem] * 5,
         out_specs=[vmem] * n,
-        scratch_shapes=[
-            pltpu.VMEM((BLOCKS, 2 * UVB, PATCH), bf16),
-            pltpu.VMEM((BLOCKS, TILE, 2 * UVB), bf16),
-            pltpu.VMEM((PATCH, TILE), bf16),
-            pltpu.SemaphoreType.DMA((2,)),
-        ],
+        scratch_shapes=[pltpu.VMEM((PATCH, TILE), bf16)],
+        cost_estimate=cost(3 * n - 2),
         compiler_params=pltpu.CompilerParams(vmem_limit_bytes=VMEM_LIMIT),
         name="forward_" + "_".join(kinds),
-    )(ctl, *metas, *sky, stacked, flipped)
-
-
-def scale(meta, mine, near, outer, weight):
-    def kernel(meta, mine, near, outer, weight, out):
-        def pointing(s, carry):
-            def uv(k, c):
-                w = weight[s, k].astype(f32)
-                v = mine[s, k].astype(f32) + near[s, k].astype(f32) + outer[s, k].astype(f32)
-                out[s, k, :, :UVB] = (v[:, :UVB] * w).astype(bf16)
-                out[s, k, :, UVB:] = (v[:, UVB:] * w).astype(bf16)
-                return c
-
-            lax.fori_loop(0, meta[USED + s], uv, 0)
-            return carry
-
-        lax.fori_loop(0, meta[COUNT], pointing, 0)
+    )(ctl, *metas, *near_by(*sky), stacked, flipped)
+
+
+def each_tile(meta, work):
+    def pointing(s, carry):
+        def uv(k, c):
+            work(s, k)
+            return c
+
+        lax.fori_loop(0, meta[USED, s], uv, 0)
+        return carry
+
+    lax.fori_loop(0, meta[COUNT, 0], pointing, 0)
+
+
+def add_partial(meta, mine, other):
+    def kernel(meta, mine, other, out):
+        def work(s, k):
+            out[s, k] = mine[s, k] + other[s, k].astype(f32)
+
+        each_tile(meta, work)
 
     smem = pl.BlockSpec(memory_space=pltpu.SMEM)
     vmem = pl.BlockSpec(memory_space=pltpu.VMEM)
     return pl.pallas_call(
         kernel,
-        out_shape=jax.ShapeDtypeStruct((SLOTS, 2, UVB, 2 * UVB), bf16),
-        in_specs=[smem] + [vmem] * 4,
+        out_shape=pltpu.VMEM((SLOTS, 2, UVB, 2 * UVB), f32),
+        in_specs=[smem] + [vmem] * 2,
         out_specs=vmem,
+        input_output_aliases={1: 0},
+        compiler_params=pltpu.CompilerParams(vmem_limit_bytes=VMEM_LIMIT),
+        name="add_partial",
+    )(meta, *near_by(mine, other))
+
+
+def scale(meta, mine, near, weight):
+    def kernel(meta, mine, near, weight, out):
+        def work(s, k):
+            w = weight[s, k].astype(f32)
+            v = mine[s, k] + near[s, k].astype(f32)
+            out[s, k, :, :UVB] = (v[:, :UVB] * w).astype(bf16)
+            out[s, k, :, UVB:] = (v[:, UVB:] * w).astype(bf16)
+
+        each_tile(meta, work)
+
+    smem = pl.BlockSpec(memory_space=pltpu.SMEM)
+    vmem = pl.BlockSpec(memory_space=pltpu.VMEM)
+    return pl.pallas_call(
+        kernel,
+        out_shape=pltpu.VMEM((SLOTS, 2, UVB, 2 * UVB), bf16),
+        in_specs=[smem] + [vmem] * 3,
+        out_specs=vmem,
         compiler_params=pltpu.CompilerParams(vmem_limit_bytes=VMEM_LIMIT),
         name="scale",
-    )(meta, mine, near, outer, weight)
+    )(meta, *near_by(mine, near, weight))
 
 
 def adjoint_tile(low, step, meta, scaled, stacked, flipped, spread, totals):
     own, pair, far = totals
 
     def pointing(s, carry):
-        oy, ox = meta[OFFSET + 2 * s], meta[OFFSET + 2 * s + 1]
-        width = meta[WIDTH + s].astype(f32)
+        oy, ox = meta[OFFSET, s], meta[OFFSET + 1, s]
+        width = meta[WIDTH, s].astype(f32)
         shift = column_shift(step, ox)
         cols = col_factor(shift, width)
-        used = meta[USED + s]
+        used = meta[USED, s]
 
         def uv(k, c):
-            a = meta[BINS + 4 * s + 2 * k]
-            b = meta[BINS + 4 * s + 2 * k + 1]
+            a = meta[BINS + 2 * k, s]
+            b = meta[BINS + 2 * k + 1, s]
             cos, sin = twiddle(a, b, oy, shift)
             re = scaled[s, k, :, :UVB].astype(f32)
             im = scaled[s, k, :, UVB:].astype(f32)
@@ -210,13 +256,13 @@
             both = jnp.concatenate(
                 [jnp.concatenate([mr, mi], axis=1), jnp.concatenate([mi, -mr], axis=1)], axis=0
             )
-            spread[k] = jnp.dot(both, stacked[b], preferred_element_type=f32).astype(bf16)
+            spread[k] = jnp.dot(both, stacked[b, :, :TILE], preferred_element_type=f32).astype(bf16)
             return c
 
         lax.fori_loop(0, used, uv, 0)
 
         def add(count):
-            blocks = [meta[BINS + 4 * s + 2 * k] for k in range(count)]
+            blocks = [meta[BINS + 2 * k, s] for k in range(count)]
             big = 256
 
             def image(at):
@@ -253,25 +299,11 @@
 
         return carry
 
-    lax.fori_loop(0, meta[COUNT], pointing, 0)
-
-
-def adjoint_scratch(semaphores):
-    return [
-        pltpu.VMEM((BLOCKS, 2 * UVB, TILE), bf16),
-        pltpu.VMEM((BLOCKS, PATCH, 2 * UVB), bf16),
-        pltpu.VMEM((2, 2 * UVB, TILE), bf16),
-        pltpu.SemaphoreType.DMA((semaphores,)),
-    ]
+    lax.fori_loop(0, meta[COUNT, 0], pointing, 0)
 
 
 def adjoint_first(ctl, metas, scaled, stacked, flipped):
-    def kernel(ctl, meta0, meta1, sc0, sc1, stacked_hbm, flipped_hbm, own, pair, far, stacked, flipped, spread, sems):
-        copy_s = pltpu.make_async_copy(stacked_hbm.at[:, :, :TILE], stacked, sems.at[0])
-        copy_f = pltpu.make_async_copy(flipped_hbm, flipped, sems.at[1])
-        copy_s.start()
-        copy_f.start()
-
+    def kernel(ctl, meta0, meta1, sc0, sc1, stacked, flipped, own, pair, far, spread):
         def clear(i, c):
             at = pl.multiple_of(i * ROWS, ROWS)
             for ref in (own, pair, far):
@@ -279,8 +311,6 @@
             return c
 
         lax.fori_loop(0, TILE // ROWS, clear, 0)
-        copy_s.wait()
-        copy_f.wait()
         near, _ = tile_steps(ctl)
         totals = (own, pair, far)
         adjoint_tile(ctl[0], 0, meta0, sc0, stacked, flipped, spread, totals)
@@ -288,32 +318,20 @@
 
     smem = pl.BlockSpec(memory_space=pltpu.SMEM)
     vmem = pl.BlockSpec(memory_space=pltpu.VMEM)
-    hbm = pl.BlockSpec(memory_space=pl.ANY)
-    return pl.pallas_call(
-        kernel,
-        out_shape=[jax.ShapeDtypeStruct((TILE, TILE), f32)] * 3,
-        in_specs=[smem] * 3 + [vmem] * 2 + [hbm] * 2,
+    return pl.pallas_call(
+        kernel,
+        out_shape=[pltpu.VMEM((TILE, TILE), f32)] * 3,
+        in_specs=[smem] * 3 + [vmem] * 4,
         out_specs=[vmem] * 3,
-        scratch_shapes=adjoint_scratch(2),
+        scratch_shapes=[pltpu.VMEM((2, 2 * UVB, TILE), bf16)],
+        cost_estimate=cost(4),
         compiler_params=pltpu.CompilerParams(vmem_limit_bytes=VMEM_LIMIT),
         name="adjoint_first",
-    )(ctl, *metas, *scaled, stacked, flipped)
+    )(ctl, *metas, *near_by(*scaled), stacked, flipped)
 
 
 def adjoint_last(ctl, meta, scaled, begun, stacked, flipped):
-    def kernel(ctl, meta, sc, own0, pair0, far0, stacked_hbm, flipped_hbm, own, pair_out, far_out, *scratch):
-        stacked, flipped, spread, sems, pair, far = scratch
-        copies = [
-            pltpu.make_async_copy(own0, own, sems.at[0]),
-            pltpu.make_async_copy(pair0, pair, sems.at[1]),
-            pltpu.make_async_copy(far0, far, sems.at[2]),
-            pltpu.make_async_copy(stacked_hbm.at[:, :, :TILE], stacked, sems.at[3]),
-            pltpu.make_async_copy(flipped_hbm, flipped, sems.at[4]),
-        ]
-        for copy in copies:
-            copy.start()
-        for copy in copies:
-            copy.wait()
+    def kernel(ctl, meta, sc, own0, pair, far, stacked, flipped, own, pair_out, far_out, spread):
         _, outer = tile_steps(ctl)
         adjoint_tile(ctl[0], outer, meta, sc, stacked, flipped, spread, (own, pair, far))
 
@@ -327,20 +345,21 @@
 
     smem = pl.BlockSpec(memory_space=pltpu.SMEM)
     vmem = pl.BlockSpec(memory_space=pltpu.VMEM)
-    hbm = pl.BlockSpec(memory_space=pl.ANY)
     return pl.pallas_call(
         kernel,
         out_shape=[
-            jax.ShapeDtypeStruct((TILE, TILE), f32),
-            jax.ShapeDtypeStruct((TILE, TILE), bf16),
-            jax.ShapeDtypeStruct((TILE, TILE), bf16),
+            pltpu.VMEM((TILE, TILE), f32),
+            pltpu.VMEM((TILE, TILE), bf16),
+            pltpu.VMEM((TILE, TILE), bf16),
         ],
-        in_specs=[smem] * 2 + [vmem] + [hbm] * 5,
+        in_specs=[smem] * 2 + [vmem] * 6,
         out_specs=[vmem] * 3,
-        scratch_shapes=adjoint_scratch(5) + [pltpu.VMEM((TILE, TILE), f32)] * 2,
+        scratch_shapes=[pltpu.VMEM((2, 2 * UVB, TILE), bf16)],
+        input_output_aliases={3: 0},
+        cost_estimate=cost(1),
         compiler_params=pltpu.CompilerParams(vmem_limit_bytes=VMEM_LIMIT),
         name="adjoint_last",
-    )(ctl, meta, scaled, *begun, stacked, flipped)
+    )(ctl, meta, *near_by(scaled, *begun), stacked, flipped)
 
 
 def mesh_moves(rows, cols):
@@ -375,29 +394,31 @@
         return lax.ppermute(x, ("ty", "tx"), moves[what])
 
     def shards(sky, point_count, point_offset, beam_width, uv_bins, uv_count, uv_weight):
-        stacked, flipped = jnp.asarray(stacked_np), jnp.asarray(flipped_np)
         ctl = jnp.stack([lax.axis_index("ty") % 2, lax.axis_index("tx") % 2]).astype(jnp.int32)
         meta = jnp.concatenate(
             [
-                point_count.reshape(1),
-                point_offset.reshape(2 * SLOTS),
-                beam_width.reshape(SLOTS).astype(jnp.int32),
-                uv_bins.reshape(4 * SLOTS),
-                uv_count.reshape(SLOTS),
+                point_offset[0, 0].T,
+                beam_width[0].astype(jnp.int32),
+                uv_bins[0, 0].transpose(1, 2, 0).reshape(4, SLOTS),
+                uv_count[0],
+                jnp.broadcast_to(point_count, (1, SLOTS)),
             ]
         )
         pair_sky = send(sky, "row_pair")
         far_sky = send(sky, "row_out")
+        meta_outer = send(meta, "row_pair_outer")
         meta_own = send(meta, "row_pair")
-        meta_near = send(meta, "row_pair_near")
-        meta_outer = send(meta, "row_pair_outer")
+        meta_near = send(meta_own, "near")
         weight = send(uv_weight[0, 0], "row_pair")
-        skies = (sky, pair_sky, far_sky)
+        own_sky, stacked, flipped = stage(sky, jnp.asarray(stacked_np), jnp.asarray(flipped_np))
+        skies = (own_sky, pair_sky, far_sky)
         (v_outer,) = forward(("outer",), ctl, (meta_outer,), skies, stacked, flipped)
         from_outer = send(v_outer, "outer")
+        meta_own, meta_near, weight, v_outer = lax.optimization_barrier((meta_own, meta_near, weight, v_outer))
         v_own, v_near = forward(("own", "near"), ctl, (meta_own, meta_near), skies, stacked, flipped)
         from_near = send(v_near, "near")
-        scaled = scale(meta_own, v_own, from_near, from_outer, weight)
+        v_sum = add_partial(meta_own, v_own, from_outer)
+        scaled = scale(meta_own, v_sum, from_near, weight)
         scaled_outer = send(scaled, "outer")
         scaled_near = send(scaled, "near")
         begun = adjoint_first(ctl, (meta_own, meta_near), (scaled, scaled_near), stacked, flipped)

time: 114 us -> 87.7 us (0.77)
  the two profiles are of different devices: /device:TPU:115 before, /device:TPU:6 now
where the time goes in v2:
time: 87.7 us; the launch traced here: 87.1 us
  waiting for transfers between devices  38.8 us (44%)
  starting transfers between devices  23.3 us (27%)
  Pallas kernels  21.6 us (25%)
  other arithmetic  1.92 us (2%)
    ppermute x12, waiting for transfers between devices, send(): return lax.ppermute(x, ('ty', 'tx'), moves[what])  38.8 us
    ppermute x12, starting transfers between devices, send(): return lax.ppermute(x, ('ty', 'tx'), moves[what])  23.3 us
    pallas_call x2, Pallas kernels, forward(): pl.pallas_call(kernel, out_shape=[pltpu.VMEM((SLOTS, 2, UVB, 2 * UVB), f3...  8.85 us
    pallas_call x1, Pallas kernels, adjoint_first(): pl.pallas_call(kernel, out_shape=[pltpu.VMEM((TILE, TILE), f32)] * 3, in_...  5.37 us
    pallas_call x1, Pallas kernels, stage(): pl.pallas_call(kernel, out_shape=[pltpu.VMEM(x.shape, bf16) for x in arra...  3.66 us
    pallas_call x1, Pallas kernels, adjoint_last(): pl.pallas_call(kernel, out_shape=[pltpu.VMEM((TILE, TILE), f32), pltpu.VM...  2.39 us
  transfers between devices with their start and end apart: 12, of which 5 were waited for; matrix products, arithmetic and copies ran while one was open for 2% of the time, Pallas kernels for 21%

profile of v2, /device:TPU:6, one launch (start us, length us, event | category | flops | bytes accessed | tf_op | source)
XLA Modules:
  0.0 87.1 jit_solution(16790604954822148041)
XLA Ops:
  0.0 3.5 %collective-permute-start.5 = (bf16[512,512]{1,0:T(8,128)(2,1)}, bf16[512,512]{1,0:T(8,128)(2,1)S(1)}, u32[]{:S(2)}, u32[]{:S(2)}) collective-permute-start(bf16[512,512]{1,0:T(8,128)(2,1)} %refs_0_.1), channel_id=1, source_target_pairs={{32,96},{33,97},{34,98},{35,99},{36,100},{37,101},{38,102},{39,103... | collective-permute-start | bytes 1572872 | tf_op jit(solution)/shard_map/ppermute | solution.py:394
  3.6 2.0 %collective-permute-start.3 = (bf16[4,2,128,128]{3,2,1,0:T(8,128)(2,1)}, bf16[4,2,128,128]{3,2,1,0:T(8,128)(2,1)S(1)}, u32[]{:S(2)}, u32[]{:S(2)}) collective-permute-start(bf16[4,2,128,128]{3,2,1,0:T(8,128)(2,1)} %bitcast.20), channel_id=1, source_target_pairs={{0,32},{1,33},{2,34},{3,35},{4,36},{5,37},{6,38},{7,39},{8,40},{9,... | collective-permute-start | bytes 786440 | tf_op jit(solution)/shard_map/ppermute | solution.py:394
  5.6 0.7 bitcast_convert_fusion
  6.9 0.7 concatenate.3
  7.7 0.2 collective-permute-start.1
  7.8 2.1 %collective-permute-start = (s32[9,4]{1,0:T(8,128)S(1)}, s32[9,4]{1,0:T(8,128)S(1)}, u32[]{:S(2)}, u32[]{:S(2)}) collective-permute-start(s32[9,4]{1,0:T(8,128)S(1)} %concatenate.3), channel_id=1, source_target_pairs={{1,34},{2,33},{3,36},{4,35},{5,38},{6,37},{7,40},{8,39},{9,42},{10... | collective-permute-start | bytes 440 | tf_op jit(solution)/shard_map/ppermute | solution.py:394
  10.0 3.7 %stage.1 = (bf16[512,512]{1,0:T(8,128)(2,1)S(1)}, bf16[8,256,1024]{2,1,0:T(8,128)(2,1)S(1)}, bf16[8,1024,256]{2,1,0:T(8,128)(2,1)S(1)}) custom-call(bf16[512,512]{1,0:T(8,128)(2,1)} %refs_0_.1, bf16[8,256,1024]{2,1,0:T(8,128)(2,1)} %constant.30.clone.refs_1_, bf16[8,1024,256]{2,1,0:T(8,128)(2,1)} %constant.31.clone.refs_2_), custom_call_target="tpu_custom_call" | custom-call | bytes 18874368 | tf_op jit(solution)/shard_map/stage/pallas_call | solution.py:103
  13.7 9.3 %collective-permute-done.1.refs_0_.meta.meta0 = s32[9,4]{1,0:T(8,128)S(1)} collective-permute-done((s32[9,4]{1,0:T(8,128)S(1)}, s32[9,4]{1,0:T(8,128)S(1)}, u32[]{:S(2)}, u32[]{:S(2)}) %collective-permute-start.1) | collective-permute-done | bytes 176 | tf_op jit(solution)/shard_map/ppermute | solution.py:394
  23.0 2.7 %forward_outer.1 = bf16[4,2,128,256]{3,2,1,0:T(8,128)(2,1)S(1)} custom-call(s32[2]{0:T(128)S(1)} %pad_add_fusion.ctl, s32[9,4]{1,0:T(8,128)S(1)} %collective-permute-done.refs_0_.meta, bf16[512,512]{1,0:T(8,128)(2,1)S(1)} %get-tuple-element.19.refs_1_.refs_2_, bf16[512,512]{1,0:T(8,128)(2,1)S(1)} %collective-permute-done.4.refs_2_.refs_3_, ...), custom_call_target="tpu_custom_call" | custom-call | flops 503316480 | bytes 1048576 | tf_op jit(solution)/shard_map/forward_outer/pallas_call | solution.py:172
  25.7 1.9 %collective-permute-start.6 = (bf16[4,2,128,256]{3,2,1,0:T(8,128)(2,1)S(1)}, bf16[4,2,128,256]{3,2,1,0:T(8,128)(2,1)S(1)}, u32[]{:S(2)}, u32[]{:S(2)}) collective-permute-start(bf16[4,2,128,256]{3,2,1,0:T(8,128)(2,1)S(1)} %forward_outer.1), channel_id=1, source_target_pairs={{1,2},{2,1},{3,4},{4,3},{5,6},{6,5},{7,8},{8,7},{9,10},{10,9},{11,... | collective-permute-start | bytes 1572872 | tf_op jit(solution)/shard_map/ppermute | solution.py:394
  27.6 6.2 %forward_own_near.1 = (f32[4,2,128,256]{3,2,1,0:T(8,128)S(1)}, bf16[4,2,128,256]{3,2,1,0:T(8,128)(2,1)S(1)}) custom-call(s32[2]{0:T(128)S(1)} %pad_add_fusion.ctl, s32[9,4]{1,0:T(8,128)S(1)} %collective-permute-done.1.refs_0_.meta.meta0, s32[9,4]{1,0:T(8,128)S(1)} %collective-permute-done.2.refs_1_.meta1, ...), custom_call_target="tpu_custom_call" | custom-call | flops 2013265920 | bytes 1048576 | tf_op jit(solution)/shard_map/forward_own_near/pallas_call | solution.py:172
  33.8 6.3 %collective-permute-start.7 = (bf16[4,2,128,256]{3,2,1,0:T(8,128)(2,1)S(1)}, bf16[4,2,128,256]{3,2,1,0:T(8,128)(2,1)S(1)}, u32[]{:S(2)}, u32[]{:S(2)}) collective-permute-start(bf16[4,2,128,256]{3,2,1,0:T(8,128)(2,1)S(1)} %get-tuple-element.25), channel_id=1, source_target_pairs={{0,1},{1,0},{2,3},{3,2},{4,5},{5,4},{6,7},{7,6},{8,9},{9,8},{10,11... | collective-permute-start | bytes 1572872 | tf_op jit(solution)/shard_map/ppermute | solution.py:394
  40.1 3.2 %collective-permute-done.6.other = bf16[4,2,128,256]{3,2,1,0:T(8,128)(2,1)S(1)} collective-permute-done((bf16[4,2,128,256]{3,2,1,0:T(8,128)(2,1)S(1)}, bf16[4,2,128,256]{3,2,1,0:T(8,128)(2,1)S(1)}, u32[]{:S(2)}, u32[]{:S(2)}) %collective-permute-start.6) | collective-permute-done | bytes 524320 | tf_op jit(solution)/shard_map/ppermute | solution.py:394
  43.3 0.7 add_partial.1.mine
  44.0 0.7 scale.1.sc0
  44.8 1.9 %collective-permute-start.8 = (bf16[4,2,128,256]{3,2,1,0:T(8,128)(2,1)S(1)}, bf16[4,2,128,256]{3,2,1,0:T(8,128)(2,1)S(1)}, u32[]{:S(2)}, u32[]{:S(2)}) collective-permute-start(bf16[4,2,128,256]{3,2,1,0:T(8,128)(2,1)S(1)} %scale.1.sc0), channel_id=1, source_target_pairs={{1,2},{2,1},{3,4},{4,3},{5,6},{6,5},{7,8},{8,7},{9,10},{10,9},{11,... | collective-permute-start | bytes 1572872 | tf_op jit(solution)/shard_map/ppermute | solution.py:394
  46.7 5.4 %adjoint_first.1 = (f32[512,512]{1,0:T(8,128)S(1)}, f32[512,512]{1,0:T(8,128)S(1)}, f32[512,512]{1,0:T(8,128)S(1)}) custom-call(s32[2]{0:T(128)S(1)} %pad_add_fusion.ctl, s32[9,4]{1,0:T(8,128)S(1)} %collective-permute-done.1.refs_0_.meta.meta0, s32[9,4]{1,0:T(8,128)S(1)} %collective-permute-done.2.refs_1_.meta1, bf16[4,2,128,256]{3,2,1,0:T(8,128)(2,1)S(1)} %scale.1.sc0, ...), custom_call_target="tpu_custom_call" | custom-call | flops 2013265920 | bytes 1048576 | tf_op jit(solution)/shard_map/adjoint_first/pallas_call | solution.py:321
  52.1 13.3 %collective-permute-done.8.sc = bf16[4,2,128,256]{3,2,1,0:T(8,128)(2,1)S(1)} collective-permute-done((bf16[4,2,128,256]{3,2,1,0:T(8,128)(2,1)S(1)}, bf16[4,2,128,256]{3,2,1,0:T(8,128)(2,1)S(1)}, u32[]{:S(2)}, u32[]{:S(2)}) %collective-permute-start.8) | collective-permute-done | bytes 524320 | tf_op jit(solution)/shard_map/ppermute | solution.py:394
  65.4 2.4 %adjoint_last.1 = (f32[512,512]{1,0:T(8,128)S(1)}, bf16[512,512]{1,0:T(8,128)(2,1)S(1)}, bf16[512,512]{1,0:T(8,128)(2,1)S(1)}) custom-call(s32[2]{0:T(128)S(1)} %pad_add_fusion.ctl, s32[9,4]{1,0:T(8,128)S(1)} %collective-permute-done.refs_0_.meta, bf16[4,2,128,256]{3,2,1,0:T(8,128)(2,1)S(1)} %collective-permute-done.8.sc, ...), custom_call_target="tpu_custom_call", output_to_operand_aliasing={{0}: (3, {})} | custom-call | flops 503316480 | bytes 1048576 | tf_op jit(solution)/shard_map/adjoint_last/pallas_call | solution.py:348
  67.8 3.9 %collective-permute-start.10 = (bf16[512,512]{1,0:T(8,128)(2,1)S(1)}, bf16[512,512]{1,0:T(8,128)(2,1)S(1)}, u32[]{:S(2)}, u32[]{:S(2)}) collective-permute-start(bf16[512,512]{1,0:T(8,128)(2,1)S(1)} %get-tuple-element.31), channel_id=1, source_target_pairs={{0,32},{1,33},{2,34},{3,35},{4,36},{5,37},{6,38},{7,39},{8,40},{9,... | collective-permute-start | bytes 1572872 | tf_op jit(solution)/shard_map/ppermute | solution.py:394
  71.7 1.3 %collective-permute-start.11 = (bf16[512,512]{1,0:T(8,128)(2,1)S(1)}, bf16[512,512]{1,0:T(8,128)(2,1)S(1)}, u32[]{:S(2)}, u32[]{:S(2)}) collective-permute-start(bf16[512,512]{1,0:T(8,128)(2,1)S(1)} %get-tuple-element.32), channel_id=1, source_target_pairs={{0,64},{1,65},{2,66},{3,67},{4,68},{5,69},{6,70},{7,71},{8,72},{9,... | collective-permute-start | bytes 1572872 | tf_op jit(solution)/shard_map/ppermute | solution.py:394
  73.0 5.9 %collective-permute-done.10 = bf16[512,512]{1,0:T(8,128)(2,1)S(1)} collective-permute-done((bf16[512,512]{1,0:T(8,128)(2,1)S(1)}, bf16[512,512]{1,0:T(8,128)(2,1)S(1)}, u32[]{:S(2)}, u32[]{:S(2)}) %collective-permute-start.10) | collective-permute-done | bytes 524320 | tf_op jit(solution)/shard_map/ppermute | solution.py:394
  78.9 7.1 %collective-permute-done.11 = bf16[512,512]{1,0:T(8,128)(2,1)S(1)} collective-permute-done((bf16[512,512]{1,0:T(8,128)(2,1)S(1)}, bf16[512,512]{1,0:T(8,128)(2,1)S(1)}, u32[]{:S(2)}, u32[]{:S(2)}) %collective-permute-start.11) | collective-permute-done | bytes 524320 | tf_op jit(solution)/shard_map/ppermute | solution.py:394
  86.0 1.2 %convert_add_fusion = f32[512,512]{1,0:T(8,128)} fusion(bf16[512,512]{1,0:T(8,128)(2,1)S(1)} %collective-permute-done.11, f32[512,512]{1,0:T(8,128)S(1)} %get-tuple-element.30, bf16[512,512]{1,0:T(8,128)(2,1)S(1)} %collective-permute-done.10), kind=kLoop, calls=%fused_computation | loop fusion | flops 1048576 | bytes 3145728 | tf_op jit(solution)/shard_map/add | solution.py:426
  (12 shorter events, 0.3 us)
Async XLA Ops:
  0.0 23.0 %collective-permute-start.5 = (bf16[512,512]{1,0:T(8,128)(2,1)}, bf16[512,512]{1,0:T(8,128)(2,1)S(1)}, u32[]{:S(2)}, u32[]{:S(2)}) collective-permute-start(bf16[512,512]{1,0:T(8,128)(2,1)} %refs_0_.1), channel_id=1, source_target_pairs={{32,96},{33,97},{34,98},{35,99},{36,100},{37,101},{38,102},{39,103... | collective-permute-start | bytes 1572872 | tf_op jit(solution)/shard_map/ppermute | solution.py:394
  3.5 19.5 %collective-permute-start.4 = (bf16[512,512]{1,0:T(8,128)(2,1)}, bf16[512,512]{1,0:T(8,128)(2,1)S(1)}, u32[]{:S(2)}, u32[]{:S(2)}) collective-permute-start(bf16[512,512]{1,0:T(8,128)(2,1)} %refs_0_.1), channel_id=1, source_target_pairs={{0,32},{1,33},{2,34},{3,35},{4,36},{5,37},{6,38},{7,39},{8,40},{9,... | collective-permute-start | bytes 1572872 | tf_op jit(solution)/shard_map/ppermute | solution.py:394
  3.6 24.0 %collective-permute-start.3 = (bf16[4,2,128,128]{3,2,1,0:T(8,128)(2,1)}, bf16[4,2,128,128]{3,2,1,0:T(8,128)(2,1)S(1)}, u32[]{:S(2)}, u32[]{:S(2)}) collective-permute-start(bf16[4,2,128,128]{3,2,1,0:T(8,128)(2,1)} %bitcast.20), channel_id=1, source_target_pairs={{0,32},{1,33},{2,34},{3,35},{4,36},{5,37},{6,38},{7,39},{8,40},{9,... | collective-permute-start | bytes 786440 | tf_op jit(solution)/shard_map/ppermute | solution.py:394
  7.7 15.3 %collective-permute-start.1 = (s32[9,4]{1,0:T(8,128)S(1)}, s32[9,4]{1,0:T(8,128)S(1)}, u32[]{:S(2)}, u32[]{:S(2)}) collective-permute-start(s32[9,4]{1,0:T(8,128)S(1)} %concatenate.3), channel_id=1, source_target_pairs={{0,32},{1,33},{2,34},{3,35},{4,36},{5,37},{6,38},{7,39},{8,40},{9,... | collective-permute-start | bytes 440 | tf_op jit(solution)/shard_map/ppermute | solution.py:394
  7.8 15.1 %collective-permute-start = (s32[9,4]{1,0:T(8,128)S(1)}, s32[9,4]{1,0:T(8,128)S(1)}, u32[]{:S(2)}, u32[]{:S(2)}) collective-permute-start(s32[9,4]{1,0:T(8,128)S(1)} %concatenate.3), channel_id=1, source_target_pairs={{1,34},{2,33},{3,36},{4,35},{5,38},{6,37},{7,40},{8,39},{9,42},{10... | collective-permute-start | bytes 440 | tf_op jit(solution)/shard_map/ppermute | solution.py:394
  23.0 4.6 %collective-permute-start.2 = (s32[9,4]{1,0:T(8,128)S(1)}, s32[9,4]{1,0:T(8,128)S(1)}, u32[]{:S(2)}, u32[]{:S(2)}) collective-permute-start(s32[9,4]{1,0:T(8,128)S(1)} %collective-permute-done.1.refs_0_.meta.meta0), channel_id=1, source_target_pairs={{0,1},{1,0},{2,3},{3,2},{4,5},{5,4},{6,7},{7,6},{8,9},{9,8},{10,11... | collective-permute-start | bytes 440 | tf_op jit(solution)/shard_map/ppermute | solution.py:394
  25.7 17.6 %collective-permute-start.6 = (bf16[4,2,128,256]{3,2,1,0:T(8,128)(2,1)S(1)}, bf16[4,2,128,256]{3,2,1,0:T(8,128)(2,1)S(1)}, u32[]{:S(2)}, u32[]{:S(2)}) collective-permute-start(bf16[4,2,128,256]{3,2,1,0:T(8,128)(2,1)S(1)} %forward_outer.1), channel_id=1, source_target_pairs={{1,2},{2,1},{3,4},{4,3},{5,6},{6,5},{7,8},{8,7},{9,10},{10,9},{11,... | collective-permute-start | bytes 1572872 | tf_op jit(solution)/shard_map/ppermute | solution.py:394
  33.8 10.2 %collective-permute-start.7 = (bf16[4,2,128,256]{3,2,1,0:T(8,128)(2,1)S(1)}, bf16[4,2,128,256]{3,2,1,0:T(8,128)(2,1)S(1)}, u32[]{:S(2)}, u32[]{:S(2)}) collective-permute-start(bf16[4,2,128,256]{3,2,1,0:T(8,128)(2,1)S(1)} %get-tuple-element.25), channel_id=1, source_target_pairs={{0,1},{1,0},{2,3},{3,2},{4,5},{5,4},{6,7},{7,6},{8,9},{9,8},{10,11... | collective-permute-start | bytes 1572872 | tf_op jit(solution)/shard_map/ppermute | solution.py:394
  44.7 2.0 %collective-permute-start.9 = (bf16[4,2,128,256]{3,2,1,0:T(8,128)(2,1)S(1)}, bf16[4,2,128,256]{3,2,1,0:T(8,128)(2,1)S(1)}, u32[]{:S(2)}, u32[]{:S(2)}) collective-permute-start(bf16[4,2,128,256]{3,2,1,0:T(8,128)(2,1)S(1)} %scale.1.sc0), channel_id=1, source_target_pairs={{0,1},{1,0},{2,3},{3,2},{4,5},{5,4},{6,7},{7,6},{8,9},{9,8},{10,11... | collective-permute-start | bytes 1572872 | tf_op jit(solution)/shard_map/ppermute | solution.py:394
  44.8 20.6 %collective-permute-start.8 = (bf16[4,2,128,256]{3,2,1,0:T(8,128)(2,1)S(1)}, bf16[4,2,128,256]{3,2,1,0:T(8,128)(2,1)S(1)}, u32[]{:S(2)}, u32[]{:S(2)}) collective-permute-start(bf16[4,2,128,256]{3,2,1,0:T(8,128)(2,1)S(1)} %scale.1.sc0), channel_id=1, source_target_pairs={{1,2},{2,1},{3,4},{4,3},{5,6},{6,5},{7,8},{8,7},{9,10},{10,9},{11,... | collective-permute-start | bytes 1572872 | tf_op jit(solution)/shard_map/ppermute | solution.py:394
  67.8 11.1 %collective-permute-start.10 = (bf16[512,512]{1,0:T(8,128)(2,1)S(1)}, bf16[512,512]{1,0:T(8,128)(2,1)S(1)}, u32[]{:S(2)}, u32[]{:S(2)}) collective-permute-start(bf16[512,512]{1,0:T(8,128)(2,1)S(1)} %get-tuple-element.31), channel_id=1, source_target_pairs={{0,32},{1,33},{2,34},{3,35},{4,36},{5,37},{6,38},{7,39},{8,40},{9,... | collective-permute-start | bytes 1572872 | tf_op jit(solution)/shard_map/ppermute | solution.py:394
  71.7 14.2 %collective-permute-start.11 = (bf16[512,512]{1,0:T(8,128)(2,1)S(1)}, bf16[512,512]{1,0:T(8,128)(2,1)S(1)}, u32[]{:S(2)}, u32[]{:S(2)}) collective-permute-start(bf16[512,512]{1,0:T(8,128)(2,1)S(1)} %get-tuple-element.32), channel_id=1, source_target_pairs={{0,64},{1,65},{2,66},{3,67},{4,68},{5,69},{6,70},{7,71},{8,72},{9,... | collective-permute-start | bytes 1572872 | tf_op jit(solution)/shard_map/ppermute | solution.py:394

commit v3 on v2

--- a/solution.py
+++ b/solution.py
@@ -14,6 +14,7 @@
 UVB = 128
 BLOCKS = 8
 SLOTS = 4
+BIG = 256
 ROWS = 64
 VMEM_LIMIT = 24 * 1024 * 1024
 
@@ -51,6 +52,12 @@
     s = lax.broadcasted_iota(jnp.int32, (rows, 128), 0) + start
     m = ((s - oy) & (PATCH - 1)).astype(f32) - (PATCH // 2)
     return falloff(m * m, width), s
+
+
+def row_factor_in_lanes(oy, width):
+    s = lax.broadcasted_iota(jnp.int32, (8, PATCH), 1)
+    m = ((s - oy) & (PATCH - 1)).astype(f32) - (PATCH // 2)
+    return falloff(m * m, width)[:1]
 
 
 def col_factor(shift, width):
@@ -114,7 +121,8 @@
 
 def forward_body(kinds, ctl, metas, sky, stacked, flipped, outs, scratch):
     own, pair, far = sky
-    (window,) = scratch
+    folded, lhs = scratch
+    size = 2 * UVB
     low = ctl[0]
     near, outer = tile_steps(ctl)
     steps = {"own": 0, "near": near, "outer": outer}
@@ -124,37 +132,36 @@
             oy, ox = meta[OFFSET, s], meta[OFFSET + 1, s]
             width = meta[WIDTH, s].astype(f32)
             shift = column_shift(step, ox)
-            cols = col_factor(shift, width)
-
-            def beam_rows(i, c):
-                at = pl.multiple_of(i * ROWS, ROWS)
-                here = pl.ds(at, ROWS)
-                g, rows = row_factor(at, ROWS, oy, width)
-                mine = jnp.where(rows >= oy, 1, 0) != low
-                g2, _ = row_factor(at + TILE, ROWS, oy, width)
-                there = pl.ds(pl.multiple_of(at + TILE, ROWS), ROWS)
-                for part in lanes():
-                    h = cols[:, part]
-                    x = jnp.where(mine, own[here, part].astype(f32), far[here, part].astype(f32))
-                    window[here, part] = (x * g * h).astype(bf16)
-                    window[there, part] = (pair[here, part].astype(f32) * g2 * h).astype(bf16)
-                return c
-
-            lax.fori_loop(0, TILE // ROWS, beam_rows, 0)
-
-            def uv(k, c):
-                a = meta[BINS + 2 * k, s]
-                b = meta[BINS + 2 * k + 1, s]
-                first = jnp.dot(stacked[a], window[...], preferred_element_type=f32).astype(bf16)
-                q = jnp.dot(first, flipped[b, :TILE, :], preferred_element_type=f32)
-                re = q[:UVB, :UVB] - q[UVB:, UVB:]
-                im = q[:UVB, UVB:] + q[UVB:, :UVB]
-                cos, sin = twiddle(a, b, oy, shift)
-                out[s, k, :, :UVB] = (re * cos - im * sin).astype(out.dtype)
-                out[s, k, :, UVB:] = (im * cos + re * sin).astype(out.dtype)
-                return c
-
-            lax.fori_loop(0, meta[USED, s], uv, 0)
+
+            def transform(count):
+                bins = [(meta[BINS + 2 * k, s], meta[BINS + 2 * k + 1, s]) for k in range(count)]
+                g = row_factor_in_lanes(oy, width)
+                for k, (a, _) in enumerate(bins):
+                    lhs[k * size : (k + 1) * size, :] = (stacked[a].astype(f32) * g).astype(bf16)
+                first = jnp.dot(lhs[: count * size, TILE:], pair[...], preferred_element_type=f32)
+                for at in range(0, TILE, ROWS):
+                    here = slice(at, at + ROWS)
+                    rows = lax.broadcasted_iota(jnp.int32, (ROWS, TILE), 0) + at
+                    mine = jnp.where(rows >= oy, 1, 0) != low
+                    both = jnp.where(mine, own[here, :].astype(f32), far[here, :].astype(f32))
+                    folded[here, :] = both.astype(bf16)
+                first += jnp.dot(lhs[: count * size, :TILE], folded[...], preferred_element_type=f32)
+                first = (first * col_factor(shift, width)).astype(bf16)
+                for k, (a, b) in enumerate(bins):
+                    rows = first[k * size : (k + 1) * size]
+                    q = jnp.dot(rows, flipped[b, :TILE, :], preferred_element_type=f32)
+                    re = q[:UVB, :UVB] - q[UVB:, UVB:]
+                    im = q[:UVB, UVB:] + q[UVB:, :UVB]
+                    cos, sin = twiddle(a, b, oy, shift)
+                    out[s, k, :, :UVB] = (re * cos - im * sin).astype(out.dtype)
+                    out[s, k, :, UVB:] = (im * cos + re * sin).astype(out.dtype)
+
+            for count in (1, 2):
+
+                @pl.when(meta[USED, s] == count)
+                def _(count=count):
+                    transform(count)
+
             return carry
 
         lax.fori_loop(0, meta[COUNT, 0], pointing, 0)
@@ -174,7 +181,10 @@
         out_shape=[pltpu.VMEM((SLOTS, 2, UVB, 2 * UVB), f32 if k == "own" else bf16) for k in kinds],
         in_specs=[smem] * (1 + n) + [vmem] * 5,
         out_specs=[vmem] * n,
-        scratch_shapes=[pltpu.VMEM((PATCH, TILE), bf16)],
+        scratch_shapes=[
+            pltpu.VMEM((TILE, TILE), bf16),
+            pltpu.VMEM((4 * UVB, PATCH), bf16),
+        ],
         cost_estimate=cost(3 * n - 2),
         compiler_params=pltpu.CompilerParams(vmem_limit_bytes=VMEM_LIMIT),
         name="forward_" + "_".join(kinds),
@@ -242,60 +252,46 @@
         oy, ox = meta[OFFSET, s], meta[OFFSET + 1, s]
         width = meta[WIDTH, s].astype(f32)
         shift = column_shift(step, ox)
-        cols = col_factor(shift, width)
-        used = meta[USED, s]
-
-        def uv(k, c):
-            a = meta[BINS + 2 * k, s]
-            b = meta[BINS + 2 * k + 1, s]
-            cos, sin = twiddle(a, b, oy, shift)
-            re = scaled[s, k, :, :UVB].astype(f32)
-            im = scaled[s, k, :, UVB:].astype(f32)
-            mr = (re * cos + im * sin).astype(bf16)
-            mi = (im * cos - re * sin).astype(bf16)
-            both = jnp.concatenate(
-                [jnp.concatenate([mr, mi], axis=1), jnp.concatenate([mi, -mr], axis=1)], axis=0
-            )
-            spread[k] = jnp.dot(both, stacked[b, :, :TILE], preferred_element_type=f32).astype(bf16)
-            return c
-
-        lax.fori_loop(0, used, uv, 0)
-
-        def add(count):
-            blocks = [meta[BINS + 2 * k, s] for k in range(count)]
-            big = 256
+
+        def transform(count):
+            bins = [(meta[BINS + 2 * k, s], meta[BINS + 2 * k + 1, s]) for k in range(count)]
+            h = col_factor(shift, width)
+            for k, (a, b) in enumerate(bins):
+                cos, sin = twiddle(a, b, oy, shift)
+                re = scaled[s, k, :, :UVB].astype(f32)
+                im = scaled[s, k, :, UVB:].astype(f32)
+                mr = (re * cos + im * sin).astype(bf16)
+                mi = (im * cos - re * sin).astype(bf16)
+                both = jnp.concatenate(
+                    [jnp.concatenate([mr, mi], axis=1), jnp.concatenate([mi, -mr], axis=1)], axis=0
+                )
+                value = jnp.dot(both, stacked[b, :, :TILE], preferred_element_type=f32)
+                spread[k] = (value * h).astype(bf16)
 
             def image(at):
-                back = jnp.dot(flipped[blocks[0], pl.ds(at, big), :], spread[0], preferred_element_type=f32)
+                here = slice(at, at + BIG)
+                back = jnp.dot(flipped[bins[0][0], here, :], spread[0], preferred_element_type=f32)
                 for k in range(1, count):
-                    back += jnp.dot(
-                        flipped[blocks[k], pl.ds(at, big), :], spread[k], preferred_element_type=f32
-                    )
-                g, rows = row_factor(at, big, oy, width)
-                return [back[:, part] * g * cols[:, part] for part in lanes()], rows
-
-            def rows(i, c):
-                at = pl.multiple_of(i * big, big)
-                here = pl.ds(at, big)
+                    back += jnp.dot(flipped[bins[k][0], here, :], spread[k], preferred_element_type=f32)
+                g, rows = row_factor(at, BIG, oy, width)
+                return [back[:, part] * g for part in lanes()], rows
+
+            for at in range(0, TILE, BIG):
+                here = slice(at, at + BIG)
+                values, _ = image(at + TILE)
+                for part, v in zip(lanes(), values):
+                    pair[here, part] = pair[here, part] + v
                 values, rows = image(at)
                 mine = jnp.where(rows >= oy, 1, 0) != low
                 for part, v in zip(lanes(), values):
                     own[here, part] = own[here, part] + jnp.where(mine, v, 0.0)
                     far[here, part] = far[here, part] + jnp.where(mine, 0.0, v)
-                values, _ = image(pl.multiple_of(at + TILE, big))
-                for part, v in zip(lanes(), values):
-                    pair[here, part] = pair[here, part] + v
-                return c
-
-            lax.fori_loop(0, TILE // big, rows, 0)
-
-        @pl.when(used == 1)
-        def _():
-            add(1)
-
-        @pl.when(used == 2)
-        def _():
-            add(2)
+
+        for count in (1, 2):
+
+            @pl.when(meta[USED, s] == count)
+            def _(count=count):
+                transform(count)
 
         return carry
 
@@ -409,7 +405,8 @@
         meta_outer = send(meta, "row_pair_outer")
         meta_own = send(meta, "row_pair")
         meta_near = send(meta_own, "near")
-        weight = send(uv_weight[0, 0], "row_pair")
+        held, meta_outer, meta_own = lax.optimization_barrier((uv_weight[0, 0], meta_outer, meta_own))
+        weight = send(held, "row_pair")
         own_sky, stacked, flipped = stage(sky, jnp.asarray(stacked_np), jnp.asarray(flipped_np))
         skies = (own_sky, pair_sky, far_sky)
         (v_outer,) = forward(("outer",), ctl, (meta_outer,), skies, stacked, flipped)

time: 87.7 us -> 84.4 us (0.962)
  Pallas kernels: 21.6 us -> 14.1 us
  waiting for transfers between devices: 38.8 us -> 42.7 us
    pallas_call x2, Pallas kernels: 8.85 us -> 4.15 us  [forward(): pl.pallas_call(kernel, out_shape=[pltpu.VMEM((SLOTS, 2, UVB, 2 * UVB), f3...]
    ppermute x12, waiting for transfers between devices: 38.8 us -> 42.7 us  [send(): return lax.ppermute(x, ('ty', 'tx'), moves[what])]
    pallas_call x1, Pallas kernels: 5.37 us -> 3.3 us  [adjoint_first(): pl.pallas_call(kernel, out_shape=[pltpu.VMEM((TILE, TILE), f32)] * 3, in_...]
  transfers between devices with their start and end apart: 12 -> 12, of which waited for: 5 -> 5; matrix products, arithmetic and copies ran while one was open for 2% -> 2% of each run, Pallas kernels for 21% -> 14%
where the time goes in v3:
time: 84.4 us; the launch traced here: 83.6 us
  waiting for transfers between devices  42.7 us (51%)
  starting transfers between devices  23.3 us (28%)
  Pallas kernels  14.1 us (17%)
  other arithmetic  1.92 us (2%)
    ppermute x12, waiting for transfers between devices, send(): return lax.ppermute(x, ('ty', 'tx'), moves[what])  42.7 us
    ppermute x12, starting transfers between devices, send(): return lax.ppermute(x, ('ty', 'tx'), moves[what])  23.3 us
    pallas_call x2, Pallas kernels, forward(): pl.pallas_call(kernel, out_shape=[pltpu.VMEM((SLOTS, 2, UVB, 2 * UVB), f3...  4.15 us
    pallas_call x1, Pallas kernels, stage(): pl.pallas_call(kernel, out_shape=[pltpu.VMEM(x.shape, bf16) for x in arra...  3.66 us
    pallas_call x1, Pallas kernels, adjoint_first(): pl.pallas_call(kernel, out_shape=[pltpu.VMEM((TILE, TILE), f32)] * 3, in_...  3.3 us
  transfers between devices with their start and end apart: 12, of which 5 were waited for; matrix products, arithmetic and copies ran while one was open for 2% of the time, Pallas kernels for 14%

profile of v3, /device:TPU:6, one launch (start us, length us, event | category | flops | bytes accessed | tf_op | source)
XLA Modules:
  0.0 83.6 jit_solution(12095574990112037911)
XLA Ops:
  0.0 3.5 %collective-permute-start.5 = (bf16[512,512]{1,0:T(8,128)(2,1)}, bf16[512,512]{1,0:T(8,128)(2,1)S(1)}, u32[]{:S(2)}, u32[]{:S(2)}) collective-permute-start(bf16[512,512]{1,0:T(8,128)(2,1)} %refs_0_.1), channel_id=1, source_target_pairs={{32,96},{33,97},{34,98},{35,99},{36,100},{37,101},{38,102},{39,103... | collective-permute-start | bytes 1572872 | tf_op jit(solution)/shard_map/ppermute | solution.py:390
  4.3 0.7 bitcast_convert_fusion
  4.9 0.7 concatenate.3
  5.6 2.1 %collective-permute-start.1 = (s32[9,4]{1,0:T(8,128)S(1)}, s32[9,4]{1,0:T(8,128)S(1)}, u32[]{:S(2)}, u32[]{:S(2)}) collective-permute-start(s32[9,4]{1,0:T(8,128)S(1)} %concatenate.3), channel_id=1, source_target_pairs={{0,32},{1,33},{2,34},{3,35},{4,36},{5,37},{6,38},{7,39},{8,40},{9,... | collective-permute-start | bytes 440 | tf_op jit(solution)/shard_map/ppermute | solution.py:390
  7.7 1.9 %collective-permute-start = (s32[9,4]{1,0:T(8,128)S(1)}, s32[9,4]{1,0:T(8,128)S(1)}, u32[]{:S(2)}, u32[]{:S(2)}) collective-permute-start(s32[9,4]{1,0:T(8,128)S(1)} %concatenate.3), channel_id=1, source_target_pairs={{1,34},{2,33},{3,36},{4,35},{5,38},{6,37},{7,40},{8,39},{9,42},{10... | collective-permute-start | bytes 440 | tf_op jit(solution)/shard_map/ppermute | solution.py:390
  9.7 7.7 %collective-permute-done.1.refs_0_.meta.meta0 = s32[9,4]{1,0:T(8,128)S(1)} collective-permute-done((s32[9,4]{1,0:T(8,128)S(1)}, s32[9,4]{1,0:T(8,128)S(1)}, u32[]{:S(2)}, u32[]{:S(2)}) %collective-permute-start.1) | collective-permute-done | bytes 176 | tf_op jit(solution)/shard_map/ppermute | solution.py:390
  17.4 0.3 collective-permute-start.3
  17.7 3.7 %stage.1 = (bf16[512,512]{1,0:T(8,128)(2,1)S(1)}, bf16[8,256,1024]{2,1,0:T(8,128)(2,1)S(1)}, bf16[8,1024,256]{2,1,0:T(8,128)(2,1)S(1)}) custom-call(bf16[512,512]{1,0:T(8,128)(2,1)} %refs_0_.1, bf16[8,256,1024]{2,1,0:T(8,128)(2,1)} %constant.30.clone.refs_1_, bf16[8,1024,256]{2,1,0:T(8,128)(2,1)} %constant.31.clone.refs_2_), custom_call_target="tpu_custom_call" | custom-call | bytes 18874368 | tf_op jit(solution)/shard_map/stage/pallas_call | solution.py:110
  21.5 1.5 %forward_outer.1 = bf16[4,2,128,256]{3,2,1,0:T(8,128)(2,1)S(1)} custom-call(s32[2]{0:T(128)S(1)} %pad_add_fusion.ctl, s32[9,4]{1,0:T(8,128)S(1)} %collective-permute-done.refs_0_.meta, bf16[512,512]{1,0:T(8,128)(2,1)S(1)} %get-tuple-element.25.refs_1_.refs_2_, bf16[512,512]{1,0:T(8,128)(2,1)S(1)} %collective-permute-done.4.refs_2_.refs_3_, ...), custom_call_target="tpu_custom_call" | custom-call | flops 503316480 | bytes 1048576 | tf_op jit(solution)/shard_map/forward_outer/pallas_call | solution.py:179
  22.9 2.6 %collective-permute-start.6 = (bf16[4,2,128,256]{3,2,1,0:T(8,128)(2,1)S(1)}, bf16[4,2,128,256]{3,2,1,0:T(8,128)(2,1)S(1)}, u32[]{:S(2)}, u32[]{:S(2)}) collective-permute-start(bf16[4,2,128,256]{3,2,1,0:T(8,128)(2,1)S(1)} %forward_outer.1), channel_id=1, source_target_pairs={{1,2},{2,1},{3,4},{4,3},{5,6},{6,5},{7,8},{8,7},{9,10},{10,9},{11,... | collective-permute-start | bytes 1572872 | tf_op jit(solution)/shard_map/ppermute | solution.py:390
  25.6 2.7 %forward_own_near.1 = (f32[4,2,128,256]{3,2,1,0:T(8,128)S(1)}, bf16[4,2,128,256]{3,2,1,0:T(8,128)(2,1)S(1)}) custom-call(s32[2]{0:T(128)S(1)} %pad_add_fusion.ctl, s32[9,4]{1,0:T(8,128)S(1)} %collective-permute-done.1.refs_0_.meta.meta0, s32[9,4]{1,0:T(8,128)S(1)} %collective-permute-done.2.refs_1_.meta1, ...), custom_call_target="tpu_custom_call" | custom-call | flops 2013265920 | bytes 1048576 | tf_op jit(solution)/shard_map/forward_own_near/pallas_call | solution.py:179
  28.3 3.3 %collective-permute-start.7 = (bf16[4,2,128,256]{3,2,1,0:T(8,128)(2,1)S(1)}, bf16[4,2,128,256]{3,2,1,0:T(8,128)(2,1)S(1)}, u32[]{:S(2)}, u32[]{:S(2)}) collective-permute-start(bf16[4,2,128,256]{3,2,1,0:T(8,128)(2,1)S(1)} %get-tuple-element.31), channel_id=1, source_target_pairs={{0,1},{1,0},{2,3},{3,2},{4,5},{5,4},{6,7},{7,6},{8,9},{9,8},{10,11... | collective-permute-start | bytes 1572872 | tf_op jit(solution)/shard_map/ppermute | solution.py:390
  31.6 9.0 %collective-permute-done.6.other = bf16[4,2,128,256]{3,2,1,0:T(8,128)(2,1)S(1)} collective-permute-done((bf16[4,2,128,256]{3,2,1,0:T(8,128)(2,1)S(1)}, bf16[4,2,128,256]{3,2,1,0:T(8,128)(2,1)S(1)}, u32[]{:S(2)}, u32[]{:S(2)}) %collective-permute-start.6) | collective-permute-done | bytes 524320 | tf_op jit(solution)/shard_map/ppermute | solution.py:390
  40.6 0.7 add_partial.1.mine
  41.2 0.7 scale.1.sc0
  42.0 1.9 %collective-permute-start.8 = (bf16[4,2,128,256]{3,2,1,0:T(8,128)(2,1)S(1)}, bf16[4,2,128,256]{3,2,1,0:T(8,128)(2,1)S(1)}, u32[]{:S(2)}, u32[]{:S(2)}) collective-permute-start(bf16[4,2,128,256]{3,2,1,0:T(8,128)(2,1)S(1)} %scale.1.sc0), channel_id=1, source_target_pairs={{1,2},{2,1},{3,4},{4,3},{5,6},{6,5},{7,8},{8,7},{9,10},{10,9},{11,... | collective-permute-start | bytes 1572872 | tf_op jit(solution)/shard_map/ppermute | solution.py:390
  44.0 3.3 %adjoint_first.1 = (f32[512,512]{1,0:T(8,128)S(1)}, f32[512,512]{1,0:T(8,128)S(1)}, f32[512,512]{1,0:T(8,128)S(1)}) custom-call(s32[2]{0:T(128)S(1)} %pad_add_fusion.ctl, s32[9,4]{1,0:T(8,128)S(1)} %collective-permute-done.1.refs_0_.meta.meta0, s32[9,4]{1,0:T(8,128)S(1)} %collective-permute-done.2.refs_1_.meta1, bf16[4,2,128,256]{3,2,1,0:T(8,128)(2,1)S(1)} %scale.1.sc0, ...), custom_call_target="tpu_custom_call" | custom-call | flops 2013265920 | bytes 1048576 | tf_op jit(solution)/shard_map/adjoint_first/pallas_call | solution.py:317
  47.3 16.3 %collective-permute-done.8.sc = bf16[4,2,128,256]{3,2,1,0:T(8,128)(2,1)S(1)} collective-permute-done((bf16[4,2,128,256]{3,2,1,0:T(8,128)(2,1)S(1)}, bf16[4,2,128,256]{3,2,1,0:T(8,128)(2,1)S(1)}, u32[]{:S(2)}, u32[]{:S(2)}) %collective-permute-start.8) | collective-permute-done | bytes 524320 | tf_op jit(solution)/shard_map/ppermute | solution.py:390
  63.5 1.7 %adjoint_last.1 = (f32[512,512]{1,0:T(8,128)S(1)}, bf16[512,512]{1,0:T(8,128)(2,1)S(1)}, bf16[512,512]{1,0:T(8,128)(2,1)S(1)}) custom-call(s32[2]{0:T(128)S(1)} %pad_add_fusion.ctl, s32[9,4]{1,0:T(8,128)S(1)} %collective-permute-done.refs_0_.meta, bf16[4,2,128,256]{3,2,1,0:T(8,128)(2,1)S(1)} %collective-permute-done.8.sc, ...), custom_call_target="tpu_custom_call", output_to_operand_aliasing={{0}: (3, {})} | custom-call | flops 503316480 | bytes 1048576 | tf_op jit(solution)/shard_map/adjoint_last/pallas_call | solution.py:344
  65.2 6.2 %collective-permute-start.10 = (bf16[512,512]{1,0:T(8,128)(2,1)S(1)}, bf16[512,512]{1,0:T(8,128)(2,1)S(1)}, u32[]{:S(2)}, u32[]{:S(2)}) collective-permute-start(bf16[512,512]{1,0:T(8,128)(2,1)S(1)} %get-tuple-element.37), channel_id=1, source_target_pairs={{0,32},{1,33},{2,34},{3,35},{4,36},{5,37},{6,38},{7,39},{8,40},{9,... | collective-permute-start | bytes 1572872 | tf_op jit(solution)/shard_map/ppermute | solution.py:390
  71.4 1.3 %collective-permute-start.11 = (bf16[512,512]{1,0:T(8,128)(2,1)S(1)}, bf16[512,512]{1,0:T(8,128)(2,1)S(1)}, u32[]{:S(2)}, u32[]{:S(2)}) collective-permute-start(bf16[512,512]{1,0:T(8,128)(2,1)S(1)} %get-tuple-element.38), channel_id=1, source_target_pairs={{0,64},{1,65},{2,66},{3,67},{4,68},{5,69},{6,70},{7,71},{8,72},{9,... | collective-permute-start | bytes 1572872 | tf_op jit(solution)/shard_map/ppermute | solution.py:390
  72.7 5.9 %collective-permute-done.10 = bf16[512,512]{1,0:T(8,128)(2,1)S(1)} collective-permute-done((bf16[512,512]{1,0:T(8,128)(2,1)S(1)}, bf16[512,512]{1,0:T(8,128)(2,1)S(1)}, u32[]{:S(2)}, u32[]{:S(2)}) %collective-permute-start.10) | collective-permute-done | bytes 524320 | tf_op jit(solution)/shard_map/ppermute | solution.py:390
  78.5 3.9 %collective-permute-done.11 = bf16[512,512]{1,0:T(8,128)(2,1)S(1)} collective-permute-done((bf16[512,512]{1,0:T(8,128)(2,1)S(1)}, bf16[512,512]{1,0:T(8,128)(2,1)S(1)}, u32[]{:S(2)}, u32[]{:S(2)}) %collective-permute-start.11) | collective-permute-done | bytes 524320 | tf_op jit(solution)/shard_map/ppermute | solution.py:390
  82.4 1.2 %convert_add_fusion = f32[512,512]{1,0:T(8,128)} fusion(bf16[512,512]{1,0:T(8,128)(2,1)S(1)} %collective-permute-done.11, f32[512,512]{1,0:T(8,128)S(1)} %get-tuple-element.36, bf16[512,512]{1,0:T(8,128)(2,1)S(1)} %collective-permute-done.10), kind=kLoop, calls=%fused_computation | loop fusion | flops 1048576 | bytes 3145728 | tf_op jit(solution)/shard_map/add | solution.py:423
  (12 shorter events, 0.3 us)
Async XLA Ops:
  0.0 21.4 %collective-permute-start.5 = (bf16[512,512]{1,0:T(8,128)(2,1)}, bf16[512,512]{1,0:T(8,128)(2,1)S(1)}, u32[]{:S(2)}, u32[]{:S(2)}) collective-permute-start(bf16[512,512]{1,0:T(8,128)(2,1)} %refs_0_.1), channel_id=1, source_target_pairs={{32,96},{33,97},{34,98},{35,99},{36,100},{37,101},{38,102},{39,103... | collective-permute-start | bytes 1572872 | tf_op jit(solution)/shard_map/ppermute | solution.py:390
  3.5 17.9 %collective-permute-start.4 = (bf16[512,512]{1,0:T(8,128)(2,1)}, bf16[512,512]{1,0:T(8,128)(2,1)S(1)}, u32[]{:S(2)}, u32[]{:S(2)}) collective-permute-start(bf16[512,512]{1,0:T(8,128)(2,1)} %refs_0_.1), channel_id=1, source_target_pairs={{0,32},{1,33},{2,34},{3,35},{4,36},{5,37},{6,38},{7,39},{8,40},{9,... | collective-permute-start | bytes 1572872 | tf_op jit(solution)/shard_map/ppermute | solution.py:390
  5.6 11.7 %collective-permute-start.1 = (s32[9,4]{1,0:T(8,128)S(1)}, s32[9,4]{1,0:T(8,128)S(1)}, u32[]{:S(2)}, u32[]{:S(2)}) collective-permute-start(s32[9,4]{1,0:T(8,128)S(1)} %concatenate.3), channel_id=1, source_target_pairs={{0,32},{1,33},{2,34},{3,35},{4,36},{5,37},{6,38},{7,39},{8,40},{9,... | collective-permute-start | bytes 440 | tf_op jit(solution)/shard_map/ppermute | solution.py:390
  7.7 9.6 %collective-permute-start = (s32[9,4]{1,0:T(8,128)S(1)}, s32[9,4]{1,0:T(8,128)S(1)}, u32[]{:S(2)}, u32[]{:S(2)}) collective-permute-start(s32[9,4]{1,0:T(8,128)S(1)} %concatenate.3), channel_id=1, source_target_pairs={{1,34},{2,33},{3,36},{4,35},{5,38},{6,37},{7,40},{8,39},{9,42},{10... | collective-permute-start | bytes 440 | tf_op jit(solution)/shard_map/ppermute | solution.py:390
  17.4 8.2 %collective-permute-start.3 = (bf16[4,2,128,128]{3,2,1,0:T(8,128)(2,1)}, bf16[4,2,128,128]{3,2,1,0:T(8,128)(2,1)S(1)}, u32[]{:S(2)}, u32[]{:S(2)}) collective-permute-start(bf16[4,2,128,128]{3,2,1,0:T(8,128)(2,1)} %bitcast.20), channel_id=1, source_target_pairs={{0,32},{1,33},{2,34},{3,35},{4,36},{5,37},{6,38},{7,39},{8,40},{9,... | collective-permute-start | bytes 786440 | tf_op jit(solution)/shard_map/ppermute | solution.py:390
  21.4 4.2 %collective-permute-start.2 = (s32[9,4]{1,0:T(8,128)S(1)}, s32[9,4]{1,0:T(8,128)S(1)}, u32[]{:S(2)}, u32[]{:S(2)}) collective-permute-start(s32[9,4]{1,0:T(8,128)S(1)} %collective-permute-done.1.refs_0_.meta.meta0), channel_id=1, source_target_pairs={{0,1},{1,0},{2,3},{3,2},{4,5},{5,4},{6,7},{7,6},{8,9},{9,8},{10,11... | collective-permute-start | bytes 440 | tf_op jit(solution)/shard_map/ppermute | solution.py:390
  22.9 17.6 %collective-permute-start.6 = (bf16[4,2,128,256]{3,2,1,0:T(8,128)(2,1)S(1)}, bf16[4,2,128,256]{3,2,1,0:T(8,128)(2,1)S(1)}, u32[]{:S(2)}, u32[]{:S(2)}) collective-permute-start(bf16[4,2,128,256]{3,2,1,0:T(8,128)(2,1)S(1)} %forward_outer.1), channel_id=1, source_target_pairs={{1,2},{2,1},{3,4},{4,3},{5,6},{6,5},{7,8},{8,7},{9,10},{10,9},{11,... | collective-permute-start | bytes 1572872 | tf_op jit(solution)/shard_map/ppermute | solution.py:390
  28.3 13.0 %collective-permute-start.7 = (bf16[4,2,128,256]{3,2,1,0:T(8,128)(2,1)S(1)}, bf16[4,2,128,256]{3,2,1,0:T(8,128)(2,1)S(1)}, u32[]{:S(2)}, u32[]{:S(2)}) collective-permute-start(bf16[4,2,128,256]{3,2,1,0:T(8,128)(2,1)S(1)} %get-tuple-element.31), channel_id=1, source_target_pairs={{0,1},{1,0},{2,3},{3,2},{4,5},{5,4},{6,7},{7,6},{8,9},{9,8},{10,11... | collective-permute-start | bytes 1572872 | tf_op jit(solution)/shard_map/ppermute | solution.py:390
  41.9 2.0 %collective-permute-start.9 = (bf16[4,2,128,256]{3,2,1,0:T(8,128)(2,1)S(1)}, bf16[4,2,128,256]{3,2,1,0:T(8,128)(2,1)S(1)}, u32[]{:S(2)}, u32[]{:S(2)}) collective-permute-start(bf16[4,2,128,256]{3,2,1,0:T(8,128)(2,1)S(1)} %scale.1.sc0), channel_id=1, source_target_pairs={{0,1},{1,0},{2,3},{3,2},{4,5},{5,4},{6,7},{7,6},{8,9},{9,8},{10,11... | collective-permute-start | bytes 1572872 | tf_op jit(solution)/shard_map/ppermute | solution.py:390
  42.0 21.5 %collective-permute-start.8 = (bf16[4,2,128,256]{3,2,1,0:T(8,128)(2,1)S(1)}, bf16[4,2,128,256]{3,2,1,0:T(8,128)(2,1)S(1)}, u32[]{:S(2)}, u32[]{:S(2)}) collective-permute-start(bf16[4,2,128,256]{3,2,1,0:T(8,128)(2,1)S(1)} %scale.1.sc0), channel_id=1, source_target_pairs={{1,2},{2,1},{3,4},{4,3},{5,6},{6,5},{7,8},{8,7},{9,10},{10,9},{11,... | collective-permute-start | bytes 1572872 | tf_op jit(solution)/shard_map/ppermute | solution.py:390
  65.2 13.3 %collective-permute-start.10 = (bf16[512,512]{1,0:T(8,128)(2,1)S(1)}, bf16[512,512]{1,0:T(8,128)(2,1)S(1)}, u32[]{:S(2)}, u32[]{:S(2)}) collective-permute-start(bf16[512,512]{1,0:T(8,128)(2,1)S(1)} %get-tuple-element.37), channel_id=1, source_target_pairs={{0,32},{1,33},{2,34},{3,35},{4,36},{5,37},{6,38},{7,39},{8,40},{9,... | collective-permute-start | bytes 1572872 | tf_op jit(solution)/shard_map/ppermute | solution.py:390
  71.4 11.1 %collective-permute-start.11 = (bf16[512,512]{1,0:T(8,128)(2,1)S(1)}, bf16[512,512]{1,0:T(8,128)(2,1)S(1)}, u32[]{:S(2)}, u32[]{:S(2)}) collective-permute-start(bf16[512,512]{1,0:T(8,128)(2,1)S(1)} %get-tuple-element.38), channel_id=1, source_target_pairs={{0,64},{1,65},{2,66},{3,67},{4,68},{5,69},{6,70},{7,71},{8,72},{9,... | collective-permute-start | bytes 1572872 | tf_op jit(solution)/shard_map/ppermute | solution.py:390

commit v4 on v3

--- a/solution.py
+++ b/solution.py
@@ -31,6 +31,7 @@
     cos = (np.cos(angle) * factor).reshape(BLOCKS, UVB, PATCH)
     sin = (np.sin(angle) * factor).reshape(BLOCKS, UVB, PATCH)
     stacked = np.concatenate([cos, sin], axis=1)
+    stacked = stacked[:, :, :TILE]
     flipped = stacked.transpose(0, 2, 1)
     return stacked.astype(ml_dtypes.bfloat16), np.ascontiguousarray(flipped).astype(ml_dtypes.bfloat16)
 
@@ -57,14 +58,23 @@
 def row_factor_in_lanes(oy, width):
     s = lax.broadcasted_iota(jnp.int32, (8, PATCH), 1)
     m = ((s - oy) & (PATCH - 1)).astype(f32) - (PATCH // 2)
-    return falloff(m * m, width)[:1]
+    return falloff(m * m, width)
+
+
+def alternating():
+    i = lax.broadcasted_iota(jnp.int32, (8, TILE), 0)
+    return jnp.where((i & 1) == 1, -1.0, 1.0).astype(f32)
+
+
+def times_rows(x, factor):
+    return (x.reshape(x.shape[0] // 8, 8, x.shape[1]) * factor[None]).reshape(x.shape)
 
 
 def col_factor(shift, width):
     n = lax.broadcasted_iota(jnp.int32, (8, TILE), 1) + shift
     inside = (n >= 0) & (n < PATCH)
     d = n.astype(f32) - (PATCH // 2)
-    return jnp.where(inside, falloff(d * d, width), 0.0)[:1]
+    return jnp.where(inside, falloff(d * d, width), 0.0)
 
 
 def twiddle(a, b, oy, shift):
@@ -137,7 +147,10 @@
                 bins = [(meta[BINS + 2 * k, s], meta[BINS + 2 * k + 1, s]) for k in range(count)]
                 g = row_factor_in_lanes(oy, width)
                 for k, (a, _) in enumerate(bins):
-                    lhs[k * size : (k + 1) * size, :] = (stacked[a].astype(f32) * g).astype(bf16)
+                    rows = slice(k * size, (k + 1) * size)
+                    table = stacked[a].astype(f32)
+                    lhs[rows, TILE:] = times_rows(table, g[:, TILE:] * alternating()).astype(bf16)
+                    lhs[rows, :TILE] = times_rows(table, g[:, :TILE]).astype(bf16)
                 first = jnp.dot(lhs[: count * size, TILE:], pair[...], preferred_element_type=f32)
                 for at in range(0, TILE, ROWS):
                     here = slice(at, at + ROWS)
@@ -146,10 +159,10 @@
                     both = jnp.where(mine, own[here, :].astype(f32), far[here, :].astype(f32))
                     folded[here, :] = both.astype(bf16)
                 first += jnp.dot(lhs[: count * size, :TILE], folded[...], preferred_element_type=f32)
-                first = (first * col_factor(shift, width)).astype(bf16)
+                first = times_rows(first, col_factor(shift, width)).astype(bf16)
                 for k, (a, b) in enumerate(bins):
                     rows = first[k * size : (k + 1) * size]
-                    q = jnp.dot(rows, flipped[b, :TILE, :], preferred_element_type=f32)
+                    q = jnp.dot(rows, flipped[b], preferred_element_type=f32)
                     re = q[:UVB, :UVB] - q[UVB:, UVB:]
                     im = q[:UVB, UVB:] + q[UVB:, :UVB]
                     cos, sin = twiddle(a, b, oy, shift)
@@ -265,23 +278,24 @@
                 both = jnp.concatenate(
                     [jnp.concatenate([mr, mi], axis=1), jnp.concatenate([mi, -mr], axis=1)], axis=0
                 )
-                value = jnp.dot(both, stacked[b, :, :TILE], preferred_element_type=f32)
-                spread[k] = (value * h).astype(bf16)
-
-            def image(at):
+                value = jnp.dot(both, stacked[b], preferred_element_type=f32)
+                spread[0, k] = times_rows(value, h).astype(bf16)
+                spread[1, k] = times_rows(value, h * alternating()).astype(bf16)
+
+            def image(at, upper):
                 here = slice(at, at + BIG)
-                back = jnp.dot(flipped[bins[0][0], here, :], spread[0], preferred_element_type=f32)
+                back = jnp.dot(flipped[bins[0][0], here, :], spread[upper, 0], preferred_element_type=f32)
                 for k in range(1, count):
-                    back += jnp.dot(flipped[bins[k][0], here, :], spread[k], preferred_element_type=f32)
-                g, rows = row_factor(at, BIG, oy, width)
+                    back += jnp.dot(flipped[bins[k][0], here, :], spread[upper, k], preferred_element_type=f32)
+                g, rows = row_factor(at + upper * TILE, BIG, oy, width)
                 return [back[:, part] * g for part in lanes()], rows
 
             for at in range(0, TILE, BIG):
                 here = slice(at, at + BIG)
-                values, _ = image(at + TILE)
+                values, _ = image(at, 1)
                 for part, v in zip(lanes(), values):
                     pair[here, part] = pair[here, part] + v
-                values, rows = image(at)
+                values, rows = image(at, 0)
                 mine = jnp.where(rows >= oy, 1, 0) != low
                 for part, v in zip(lanes(), values):
                     own[here, part] = own[here, part] + jnp.where(mine, v, 0.0)
@@ -298,8 +312,8 @@
     lax.fori_loop(0, meta[COUNT, 0], pointing, 0)
 
 
-def adjoint_first(ctl, metas, scaled, stacked, flipped):
-    def kernel(ctl, meta0, meta1, sc0, sc1, stacked, flipped, own, pair, far, spread):
+def adjoint_own(ctl, meta, scaled, stacked, flipped):
+    def kernel(ctl, meta, sc, stacked, flipped, own, pair, far, spread):
         def clear(i, c):
             at = pl.multiple_of(i * ROWS, ROWS)
             for ref in (own, pair, far):
@@ -307,23 +321,40 @@
             return c
 
         lax.fori_loop(0, TILE // ROWS, clear, 0)
+        adjoint_tile(ctl[0], 0, meta, sc, stacked, flipped, spread, (own, pair, far))
+
+    smem = pl.BlockSpec(memory_space=pltpu.SMEM)
+    vmem = pl.BlockSpec(memory_space=pltpu.VMEM)
+    return pl.pallas_call(
+        kernel,
+        out_shape=[pltpu.VMEM((TILE, TILE), f32)] * 3,
+        in_specs=[smem] * 2 + [vmem] * 3,
+        out_specs=[vmem] * 3,
+        scratch_shapes=[pltpu.VMEM((2, 2, 2 * UVB, TILE), bf16)],
+        cost_estimate=cost(2),
+        compiler_params=pltpu.CompilerParams(vmem_limit_bytes=VMEM_LIMIT),
+        name="adjoint_own",
+    )(ctl, meta, *near_by(scaled), stacked, flipped)
+
+
+def adjoint_near(ctl, meta, scaled, begun, stacked, flipped):
+    def kernel(ctl, meta, sc, own0, pair0, far0, stacked, flipped, own, pair, far, spread):
         near, _ = tile_steps(ctl)
-        totals = (own, pair, far)
-        adjoint_tile(ctl[0], 0, meta0, sc0, stacked, flipped, spread, totals)
-        adjoint_tile(ctl[0], near, meta1, sc1, stacked, flipped, spread, totals)
+        adjoint_tile(ctl[0], near, meta, sc, stacked, flipped, spread, (own, pair, far))
 
     smem = pl.BlockSpec(memory_space=pltpu.SMEM)
     vmem = pl.BlockSpec(memory_space=pltpu.VMEM)
     return pl.pallas_call(
         kernel,
         out_shape=[pltpu.VMEM((TILE, TILE), f32)] * 3,
-        in_specs=[smem] * 3 + [vmem] * 4,
+        in_specs=[smem] * 2 + [vmem] * 6,
         out_specs=[vmem] * 3,
-        scratch_shapes=[pltpu.VMEM((2, 2 * UVB, TILE), bf16)],
-        cost_estimate=cost(4),
-        compiler_params=pltpu.CompilerParams(vmem_limit_bytes=VMEM_LIMIT),
-        name="adjoint_first",
-    )(ctl, *metas, *near_by(*scaled), stacked, flipped)
+        scratch_shapes=[pltpu.VMEM((2, 2, 2 * UVB, TILE), bf16)],
+        input_output_aliases={3: 0, 4: 1, 5: 2},
+        cost_estimate=cost(2),
+        compiler_params=pltpu.CompilerParams(vmem_limit_bytes=VMEM_LIMIT),
+        name="adjoint_near",
+    )(ctl, meta, *near_by(scaled, *begun), stacked, flipped)
 
 
 def adjoint_last(ctl, meta, scaled, begun, stacked, flipped):
@@ -350,7 +381,7 @@
         ],
         in_specs=[smem] * 2 + [vmem] * 6,
         out_specs=[vmem] * 3,
-        scratch_shapes=[pltpu.VMEM((2, 2 * UVB, TILE), bf16)],
+        scratch_shapes=[pltpu.VMEM((2, 2, 2 * UVB, TILE), bf16)],
         input_output_aliases={3: 0},
         cost_estimate=cost(1),
         compiler_params=pltpu.CompilerParams(vmem_limit_bytes=VMEM_LIMIT),
@@ -391,23 +422,21 @@
 
     def shards(sky, point_count, point_offset, beam_width, uv_bins, uv_count, uv_weight):
         ctl = jnp.stack([lax.axis_index("ty") % 2, lax.axis_index("tx") % 2]).astype(jnp.int32)
-        meta = jnp.concatenate(
-            [
-                point_offset[0, 0].T,
-                beam_width[0].astype(jnp.int32),
-                uv_bins[0, 0].transpose(1, 2, 0).reshape(4, SLOTS),
-                uv_count[0],
-                jnp.broadcast_to(point_count, (1, SLOTS)),
-            ]
+        rows = (
+            (OFFSET, point_offset[0, 0].T),
+            (WIDTH, beam_width[0].astype(jnp.int32)),
+            (BINS, uv_bins[0, 0].transpose(1, 2, 0).reshape(4, SLOTS)),
+            (USED, uv_count[0]),
+            (COUNT, jnp.broadcast_to(point_count, (1, SLOTS))),
         )
+        meta = sum(jnp.pad(x, ((at, COUNT + 1 - at - x.shape[0]), (0, 0))) for at, x in rows)
         pair_sky = send(sky, "row_pair")
         far_sky = send(sky, "row_out")
         meta_outer = send(meta, "row_pair_outer")
         meta_own = send(meta, "row_pair")
-        meta_near = send(meta_own, "near")
-        held, meta_outer, meta_own = lax.optimization_barrier((uv_weight[0, 0], meta_outer, meta_own))
-        weight = send(held, "row_pair")
+        meta_near = send(meta, "row_pair_near")
         own_sky, stacked, flipped = stage(sky, jnp.asarray(stacked_np), jnp.asarray(flipped_np))
+        weight = send(uv_weight[0, 0], "row_pair")
         skies = (own_sky, pair_sky, far_sky)
         (v_outer,) = forward(("outer",), ctl, (meta_outer,), skies, stacked, flipped)
         from_outer = send(v_outer, "outer")
@@ -418,7 +447,8 @@
         scaled = scale(meta_own, v_sum, from_near, weight)
         scaled_outer = send(scaled, "outer")
         scaled_near = send(scaled, "near")
-        begun = adjoint_first(ctl, (meta_own, meta_near), (scaled, scaled_near), stacked, flipped)
+        begun = adjoint_own(ctl, meta_own, scaled, stacked, flipped)
+        begun = adjoint_near(ctl, meta_near, scaled_near, begun, stacked, flipped)
         own, pair, far = adjoint_last(ctl, meta_outer, scaled_outer, begun, stacked, flipped)
         return own + send(pair, "row_pair").astype(f32) + send(far, "row_back").astype(f32)
 

time: 84.4 us -> 79.5 us (0.942)
  starting transfers between devices: 23.3 us -> 16.2 us
  Pallas kernels: 14.1 us -> 18.8 us
  waiting for transfers between devices: 42.7 us -> 40.3 us
    ppermute x12, starting transfers between devices: 23.3 us -> 16.2 us  [send(): return lax.ppermute(x, ('ty', 'tx'), moves[what])]
    pallas_call x1, Pallas kernels: 1.66 us -> 4.46 us  [adjoint_last(): pl.pallas_call(kernel, out_shape=[pltpu.VMEM((TILE, TILE), f32), pltpu.VM...]
    pallas_call x2, Pallas kernels: 4.15 us -> 6.62 us  [forward(): pl.pallas_call(kernel, out_shape=[pltpu.VMEM((SLOTS, 2, UVB, 2 * UVB), f3...]
    ppermute x12, waiting for transfers between devices: 42.7 us -> 40.3 us  [send(): return lax.ppermute(x, ('ty', 'tx'), moves[what])]
    pallas_call x1, Pallas kernels: 3.66 us -> 2.42 us  [stage(): pl.pallas_call(kernel, out_shape=[pltpu.VMEM(x.shape, bf16) for x in arra...]
    pallas_call x1 -> x2, Pallas kernels: 3.3 us -> 3.8 us  [the longest x1 2.94 us: adjoint_own(): pl.pallas_call(kernel, out_shape=[pltpu.VMEM((TILE, TILE), f32)] * 3, in_...]
  transfers between devices with their start and end apart: 12 -> 12, of which waited for: 5 -> 7; matrix products, arithmetic and copies ran while one was open for 2% -> 1% of each run, Pallas kernels for 14% -> 17%
where the time goes in v4:
time: 79.5 us; the launch traced here: 78.3 us
  waiting for transfers between devices  40.3 us (51%)
  Pallas kernels  18.8 us (24%)
  starting transfers between devices  16.2 us (20%)
  other arithmetic  2.04 us (3%)
  between operations  0.86 us (1%)
    ppermute x12, waiting for transfers between devices, send(): return lax.ppermute(x, ('ty', 'tx'), moves[what])  40.3 us
    ppermute x12, starting transfers between devices, send(): return lax.ppermute(x, ('ty', 'tx'), moves[what])  16.2 us
    pallas_call x2, Pallas kernels, forward(): pl.pallas_call(kernel, out_shape=[pltpu.VMEM((SLOTS, 2, UVB, 2 * UVB), f3...  6.62 us
    pallas_call x1, Pallas kernels, adjoint_last(): pl.pallas_call(kernel, out_shape=[pltpu.VMEM((TILE, TILE), f32), pltpu.VM...  4.46 us
    pallas_call x1, Pallas kernels, adjoint_own(): pl.pallas_call(kernel, out_shape=[pltpu.VMEM((TILE, TILE), f32)] * 3, in_...  2.94 us
    pallas_call x1, Pallas kernels, stage(): pl.pallas_call(kernel, out_shape=[pltpu.VMEM(x.shape, bf16) for x in arra...  2.42 us
  transfers between devices with their start and end apart: 12, of which 7 were waited for; matrix products, arithmetic and copies ran while one was open for 1% of the time, Pallas kernels for 17%

profile of v4, /device:TPU:6, one launch (start us, length us, event | category | flops | bytes accessed | tf_op | source)
XLA Modules:
  0.0 78.3 jit_solution(14644585851773327028)
XLA Ops:
  0.0 3.5 %collective-permute-start.5 = (bf16[512,512]{1,0:T(8,128)(2,1)}, bf16[512,512]{1,0:T(8,128)(2,1)S(1)}, u32[]{:S(2)}, u32[]{:S(2)}) collective-permute-start(bf16[512,512]{1,0:T(8,128)(2,1)} %refs_0_.1), channel_id=1, source_target_pairs={{32,96},{33,97},{34,98},{35,99},{36,100},{37,101},{38,102},{39,103... | collective-permute-start | bytes 1572872 | tf_op jit(solution)/shard_map/ppermute | solution.py:421
  3.5 0.1 collective-permute-start.4
  3.6 2.0 %collective-permute-start.3 = (bf16[4,2,128,128]{3,2,1,0:T(8,128)(2,1)}, bf16[4,2,128,128]{3,2,1,0:T(8,128)(2,1)S(1)}, u32[]{:S(2)}, u32[]{:S(2)}) collective-permute-start(bf16[4,2,128,128]{3,2,1,0:T(8,128)(2,1)} %bitcast.19), channel_id=1, source_target_pairs={{0,32},{1,33},{2,34},{3,35},{4,36},{5,37},{6,38},{7,39},{8,40},{9,... | collective-permute-start | bytes 786440 | tf_op jit(solution)/shard_map/ppermute | solution.py:421
  6.4 0.8 %add_add_fusion = s32[9,4]{1,0:T(8,128)S(1)} fusion(s32[1,4]{1,0:T(1,128)} %bitcast.17, s32[4,4]{1,0:T(4,128)} %bitcast.15, s32[2,4]{1,0:T(2,128)} %bitcast.16, s32[9]{0:T(128)S(1)} %pad.30, bf16[1,4]{1,0:T(2,128)(2,1)} %bitcast.18), kind=kLoop, calls=%fused_computation.1 | loop fusion | flops 180 | bytes 300 | tf_op jit(solution)/shard_map/add | solution.py:432
  7.2 3.6 %collective-permute-start = (s32[9,4]{1,0:T(8,128)S(1)}, s32[9,4]{1,0:T(8,128)S(1)}, u32[]{:S(2)}, u32[]{:S(2)}) collective-permute-start(s32[9,4]{1,0:T(8,128)S(1)} %add_add_fusion), channel_id=1, source_target_pairs={{1,34},{2,33},{3,36},{4,35},{5,38},{6,37},{7,40},{8,39},{9,42},{10... | collective-permute-start | bytes 440 | tf_op jit(solution)/shard_map/ppermute | solution.py:421
  10.9 2.4 %stage.1 = (bf16[512,512]{1,0:T(8,128)(2,1)S(1)}, bf16[8,256,512]{2,1,0:T(8,128)(2,1)S(1)}, bf16[8,512,256]{2,1,0:T(8,128)(2,1)S(1)}) custom-call(bf16[512,512]{1,0:T(8,128)(2,1)} %refs_0_.1, bf16[8,256,512]{2,1,0:T(8,128)(2,1)} %constant.33.clone.refs_1_, bf16[8,512,256]{2,1,0:T(8,128)(2,1)} %constant.34.clone.refs_2_), custom_call_target="tpu_custom_call" | custom-call | bytes 18874368 | tf_op jit(solution)/shard_map/stage/pallas_call | solution.py:120
  13.4 1.6 %collective-permute-done.5.refs_3_.refs_4_ = bf16[512,512]{1,0:T(8,128)(2,1)S(1)} collective-permute-done((bf16[512,512]{1,0:T(8,128)(2,1)}, bf16[512,512]{1,0:T(8,128)(2,1)S(1)}, u32[]{:S(2)}, u32[]{:S(2)}) %collective-permute-start.5) | collective-permute-done | bytes 524320 | tf_op jit(solution)/shard_map/ppermute | solution.py:421
  15.0 3.7 %collective-permute-done.4.refs_2_.refs_3_ = bf16[512,512]{1,0:T(8,128)(2,1)S(1)} collective-permute-done((bf16[512,512]{1,0:T(8,128)(2,1)}, bf16[512,512]{1,0:T(8,128)(2,1)S(1)}, u32[]{:S(2)}, u32[]{:S(2)}) %collective-permute-start.4) | collective-permute-done | bytes 524320 | tf_op jit(solution)/shard_map/ppermute | solution.py:421
  18.7 3.9 %forward_outer.1 = bf16[4,2,128,256]{3,2,1,0:T(8,128)(2,1)S(1)} custom-call(s32[2]{0:T(128)S(1)} %pad_add_fusion.ctl, s32[9,4]{1,0:T(8,128)S(1)} %collective-permute-done.refs_0_.meta, bf16[512,512]{1,0:T(8,128)(2,1)S(1)} %get-tuple-element.22.refs_1_.refs_2_, bf16[512,512]{1,0:T(8,128)(2,1)S(1)} %collective-permute-done.4.refs_2_.refs_3_, ...), custom_call_target="tpu_custom_call" | custom-call | flops 503316480 | bytes 1048576 | tf_op jit(solution)/shard_map/forward_outer/pallas_call | solution.py:192
  22.6 1.9 %collective-permute-start.6 = (bf16[4,2,128,256]{3,2,1,0:T(8,128)(2,1)S(1)}, bf16[4,2,128,256]{3,2,1,0:T(8,128)(2,1)S(1)}, u32[]{:S(2)}, u32[]{:S(2)}) collective-permute-start(bf16[4,2,128,256]{3,2,1,0:T(8,128)(2,1)S(1)} %forward_outer.1), channel_id=1, source_target_pairs={{1,2},{2,1},{3,4},{4,3},{5,6},{6,5},{7,8},{8,7},{9,10},{10,9},{11,... | collective-permute-start | bytes 1572872 | tf_op jit(solution)/shard_map/ppermute | solution.py:421
  24.6 2.7 %forward_own_near.1 = (f32[4,2,128,256]{3,2,1,0:T(8,128)S(1)}, bf16[4,2,128,256]{3,2,1,0:T(8,128)(2,1)S(1)}) custom-call(s32[2]{0:T(128)S(1)} %pad_add_fusion.ctl, s32[9,4]{1,0:T(8,128)S(1)} %collective-permute-done.1.refs_0_.meta, s32[9,4]{1,0:T(8,128)S(1)} %collective-permute-done.2.refs_1_.meta, bf16[512,512]{1,0:T(8,128)(2,1)S(1)} %get-tuple-element.22.refs_1_.refs_2_, ...), custom_call_target="tpu_custom_call" | custom-call | flops 2013265920 | bytes 1048576 | tf_op jit(solution)/shard_map/forward_own_near/pallas_call | solution.py:192
  27.4 9.4 %collective-permute-done.6.other = bf16[4,2,128,256]{3,2,1,0:T(8,128)(2,1)S(1)} collective-permute-done((bf16[4,2,128,256]{3,2,1,0:T(8,128)(2,1)S(1)}, bf16[4,2,128,256]{3,2,1,0:T(8,128)(2,1)S(1)}, u32[]{:S(2)}, u32[]{:S(2)}) %collective-permute-start.6) | collective-permute-done | bytes 524320 | tf_op jit(solution)/shard_map/ppermute | solution.py:421
  36.8 0.8 add_partial.1.mine
  37.6 0.8 scale.1.sc
  38.4 1.9 %collective-permute-start.8 = (bf16[4,2,128,256]{3,2,1,0:T(8,128)(2,1)S(1)}, bf16[4,2,128,256]{3,2,1,0:T(8,128)(2,1)S(1)}, u32[]{:S(2)}, u32[]{:S(2)}) collective-permute-start(bf16[4,2,128,256]{3,2,1,0:T(8,128)(2,1)S(1)} %scale.1.sc), channel_id=1, source_target_pairs={{1,2},{2,1},{3,4},{4,3},{5,6},{6,5},{7,8},{8,7},{9,10},{10,9},{11,... | collective-permute-start | bytes 1572872 | tf_op jit(solution)/shard_map/ppermute | solution.py:421
  40.4 2.9 %adjoint_own.1 = (f32[512,512]{1,0:T(8,128)S(1)}, f32[512,512]{1,0:T(8,128)S(1)}, f32[512,512]{1,0:T(8,128)S(1)}) custom-call(s32[2]{0:T(128)S(1)} %pad_add_fusion.ctl, s32[9,4]{1,0:T(8,128)S(1)} %collective-permute-done.1.refs_0_.meta, bf16[4,2,128,256]{3,2,1,0:T(8,128)(2,1)S(1)} %scale.1.sc, ...), custom_call_target="tpu_custom_call" | custom-call | flops 1006632960 | bytes 1048576 | tf_op jit(solution)/shard_map/adjoint_own/pallas_call | solution.py:328
  43.3 0.9 %adjoint_near.1 = (f32[512,512]{1,0:T(8,128)S(1)}, f32[512,512]{1,0:T(8,128)S(1)}, f32[512,512]{1,0:T(8,128)S(1)}) custom-call(s32[2]{0:T(128)S(1)} %pad_add_fusion.ctl, s32[9,4]{1,0:T(8,128)S(1)} %collective-permute-done.2.refs_1_.meta, ...), custom_call_target="tpu_custom_call", output_to_operand_aliasing={{0}: (3, {}), {1}: (4, {}), {2}: (5, {})} | custom-call | flops 1006632960 | bytes 1048576 | tf_op jit(solution)/shard_map/adjoint_near/pallas_call | solution.py:347
  44.2 15.8 %collective-permute-done.8.sc = bf16[4,2,128,256]{3,2,1,0:T(8,128)(2,1)S(1)} collective-permute-done((bf16[4,2,128,256]{3,2,1,0:T(8,128)(2,1)S(1)}, bf16[4,2,128,256]{3,2,1,0:T(8,128)(2,1)S(1)}, u32[]{:S(2)}, u32[]{:S(2)}) %collective-permute-start.8) | collective-permute-done | bytes 524320 | tf_op jit(solution)/shard_map/ppermute | solution.py:421
  60.0 4.5 %adjoint_last.1 = (f32[512,512]{1,0:T(8,128)S(1)}, bf16[512,512]{1,0:T(8,128)(2,1)S(1)}, bf16[512,512]{1,0:T(8,128)(2,1)S(1)}) custom-call(s32[2]{0:T(128)S(1)} %pad_add_fusion.ctl, s32[9,4]{1,0:T(8,128)S(1)} %collective-permute-done.refs_0_.meta, bf16[4,2,128,256]{3,2,1,0:T(8,128)(2,1)S(1)} %collective-permute-done.8.sc, ...), custom_call_target="tpu_custom_call", output_to_operand_aliasing={{0}: (3, {})} | custom-call | flops 503316480 | bytes 1048576 | tf_op jit(solution)/shard_map/adjoint_last/pallas_call | solution.py:375
  64.4 1.7 %collective-permute-start.10 = (bf16[512,512]{1,0:T(8,128)(2,1)S(1)}, bf16[512,512]{1,0:T(8,128)(2,1)S(1)}, u32[]{:S(2)}, u32[]{:S(2)}) collective-permute-start(bf16[512,512]{1,0:T(8,128)(2,1)S(1)} %get-tuple-element.37), channel_id=1, source_target_pairs={{0,32},{1,33},{2,34},{3,35},{4,36},{5,37},{6,38},{7,39},{8,40},{9,... | collective-permute-start | bytes 1572872 | tf_op jit(solution)/shard_map/ppermute | solution.py:421
  66.1 1.3 %collective-permute-start.11 = (bf16[512,512]{1,0:T(8,128)(2,1)S(1)}, bf16[512,512]{1,0:T(8,128)(2,1)S(1)}, u32[]{:S(2)}, u32[]{:S(2)}) collective-permute-start(bf16[512,512]{1,0:T(8,128)(2,1)S(1)} %get-tuple-element.38), channel_id=1, source_target_pairs={{0,64},{1,65},{2,66},{3,67},{4,68},{5,69},{6,70},{7,71},{8,72},{9,... | collective-permute-start | bytes 1572872 | tf_op jit(solution)/shard_map/ppermute | solution.py:421
  67.4 6.3 %collective-permute-done.10 = bf16[512,512]{1,0:T(8,128)(2,1)S(1)} collective-permute-done((bf16[512,512]{1,0:T(8,128)(2,1)S(1)}, bf16[512,512]{1,0:T(8,128)(2,1)S(1)}, u32[]{:S(2)}, u32[]{:S(2)}) %collective-permute-start.10) | collective-permute-done | bytes 524320 | tf_op jit(solution)/shard_map/ppermute | solution.py:421
  73.7 3.5 %collective-permute-done.11 = bf16[512,512]{1,0:T(8,128)(2,1)S(1)} collective-permute-done((bf16[512,512]{1,0:T(8,128)(2,1)S(1)}, bf16[512,512]{1,0:T(8,128)(2,1)S(1)}, u32[]{:S(2)}, u32[]{:S(2)}) %collective-permute-start.11) | collective-permute-done | bytes 524320 | tf_op jit(solution)/shard_map/ppermute | solution.py:421
  77.2 1.2 %convert_add_fusion = f32[512,512]{1,0:T(8,128)} fusion(bf16[512,512]{1,0:T(8,128)(2,1)S(1)} %collective-permute-done.11, f32[512,512]{1,0:T(8,128)S(1)} %get-tuple-element.36, bf16[512,512]{1,0:T(8,128)(2,1)S(1)} %collective-permute-done.10), kind=kLoop, calls=%fused_computation | loop fusion | flops 1048576 | bytes 3145728 | tf_op jit(solution)/shard_map/add | solution.py:453
  (12 shorter events, 0.5 us)
Async XLA Ops:
  0.0 15.0 %collective-permute-start.5 = (bf16[512,512]{1,0:T(8,128)(2,1)}, bf16[512,512]{1,0:T(8,128)(2,1)S(1)}, u32[]{:S(2)}, u32[]{:S(2)}) collective-permute-start(bf16[512,512]{1,0:T(8,128)(2,1)} %refs_0_.1), channel_id=1, source_target_pairs={{32,96},{33,97},{34,98},{35,99},{36,100},{37,101},{38,102},{39,103... | collective-permute-start | bytes 1572872 | tf_op jit(solution)/shard_map/ppermute | solution.py:421
  3.5 15.1 %collective-permute-start.4 = (bf16[512,512]{1,0:T(8,128)(2,1)}, bf16[512,512]{1,0:T(8,128)(2,1)S(1)}, u32[]{:S(2)}, u32[]{:S(2)}) collective-permute-start(bf16[512,512]{1,0:T(8,128)(2,1)} %refs_0_.1), channel_id=1, source_target_pairs={{0,32},{1,33},{2,34},{3,35},{4,36},{5,37},{6,38},{7,39},{8,40},{9,... | collective-permute-start | bytes 1572872 | tf_op jit(solution)/shard_map/ppermute | solution.py:421
  3.6 21.0 %collective-permute-start.3 = (bf16[4,2,128,128]{3,2,1,0:T(8,128)(2,1)}, bf16[4,2,128,128]{3,2,1,0:T(8,128)(2,1)S(1)}, u32[]{:S(2)}, u32[]{:S(2)}) collective-permute-start(bf16[4,2,128,128]{3,2,1,0:T(8,128)(2,1)} %bitcast.19), channel_id=1, source_target_pairs={{0,32},{1,33},{2,34},{3,35},{4,36},{5,37},{6,38},{7,39},{8,40},{9,... | collective-permute-start | bytes 786440 | tf_op jit(solution)/shard_map/ppermute | solution.py:421
  7.1 17.4 %collective-permute-start.2 = (s32[9,4]{1,0:T(8,128)S(1)}, s32[9,4]{1,0:T(8,128)S(1)}, u32[]{:S(2)}, u32[]{:S(2)}) collective-permute-start(s32[9,4]{1,0:T(8,128)S(1)} %add_add_fusion), channel_id=1, source_target_pairs={{0,33},{1,32},{2,35},{3,34},{4,37},{5,36},{6,39},{7,38},{8,41},{9,... | collective-permute-start | bytes 440 | tf_op jit(solution)/shard_map/ppermute | solution.py:421
  7.2 6.2 %collective-permute-start = (s32[9,4]{1,0:T(8,128)S(1)}, s32[9,4]{1,0:T(8,128)S(1)}, u32[]{:S(2)}, u32[]{:S(2)}) collective-permute-start(s32[9,4]{1,0:T(8,128)S(1)} %add_add_fusion), channel_id=1, source_target_pairs={{1,34},{2,33},{3,36},{4,35},{5,38},{6,37},{7,40},{8,39},{9,42},{10... | collective-permute-start | bytes 440 | tf_op jit(solution)/shard_map/ppermute | solution.py:421
  13.4 11.2 %collective-permute-start.1 = (s32[9,4]{1,0:T(8,128)S(1)}, s32[9,4]{1,0:T(8,128)S(1)}, u32[]{:S(2)}, u32[]{:S(2)}) collective-permute-start(s32[9,4]{1,0:T(8,128)S(1)} %add_add_fusion), channel_id=1, source_target_pairs={{0,32},{1,33},{2,34},{3,35},{4,36},{5,37},{6,38},{7,39},{8,40},{9,... | collective-permute-start | bytes 440 | tf_op jit(solution)/shard_map/ppermute | solution.py:421
  22.6 14.2 %collective-permute-start.6 = (bf16[4,2,128,256]{3,2,1,0:T(8,128)(2,1)S(1)}, bf16[4,2,128,256]{3,2,1,0:T(8,128)(2,1)S(1)}, u32[]{:S(2)}, u32[]{:S(2)}) collective-permute-start(bf16[4,2,128,256]{3,2,1,0:T(8,128)(2,1)S(1)} %forward_outer.1), channel_id=1, source_target_pairs={{1,2},{2,1},{3,4},{4,3},{5,6},{6,5},{7,8},{8,7},{9,10},{10,9},{11,... | collective-permute-start | bytes 1572872 | tf_op jit(solution)/shard_map/ppermute | solution.py:421
  27.3 10.3 %collective-permute-start.7 = (bf16[4,2,128,256]{3,2,1,0:T(8,128)(2,1)S(1)}, bf16[4,2,128,256]{3,2,1,0:T(8,128)(2,1)S(1)}, u32[]{:S(2)}, u32[]{:S(2)}) collective-permute-start(bf16[4,2,128,256]{3,2,1,0:T(8,128)(2,1)S(1)} %get-tuple-element.28), channel_id=1, source_target_pairs={{0,1},{1,0},{2,3},{3,2},{4,5},{5,4},{6,7},{7,6},{8,9},{9,8},{10,11... | collective-permute-start | bytes 1572872 | tf_op jit(solution)/shard_map/ppermute | solution.py:421
  38.3 5.0 %collective-permute-start.9 = (bf16[4,2,128,256]{3,2,1,0:T(8,128)(2,1)S(1)}, bf16[4,2,128,256]{3,2,1,0:T(8,128)(2,1)S(1)}, u32[]{:S(2)}, u32[]{:S(2)}) collective-permute-start(bf16[4,2,128,256]{3,2,1,0:T(8,128)(2,1)S(1)} %scale.1.sc), channel_id=1, source_target_pairs={{0,1},{1,0},{2,3},{3,2},{4,5},{5,4},{6,7},{7,6},{8,9},{9,8},{10,11... | collective-permute-start | bytes 1572872 | tf_op jit(solution)/shard_map/ppermute | solution.py:421
  38.4 21.5 %collective-permute-start.8 = (bf16[4,2,128,256]{3,2,1,0:T(8,128)(2,1)S(1)}, bf16[4,2,128,256]{3,2,1,0:T(8,128)(2,1)S(1)}, u32[]{:S(2)}, u32[]{:S(2)}) collective-permute-start(bf16[4,2,128,256]{3,2,1,0:T(8,128)(2,1)S(1)} %scale.1.sc), channel_id=1, source_target_pairs={{1,2},{2,1},{3,4},{4,3},{5,6},{6,5},{7,8},{8,7},{9,10},{10,9},{11,... | collective-permute-start | bytes 1572872 | tf_op jit(solution)/shard_map/ppermute | solution.py:421
  64.4 9.3 %collective-permute-start.10 = (bf16[512,512]{1,0:T(8,128)(2,1)S(1)}, bf16[512,512]{1,0:T(8,128)(2,1)S(1)}, u32[]{:S(2)}, u32[]{:S(2)}) collective-permute-start(bf16[512,512]{1,0:T(8,128)(2,1)S(1)} %get-tuple-element.37), channel_id=1, source_target_pairs={{0,32},{1,33},{2,34},{3,35},{4,36},{5,37},{6,38},{7,39},{8,40},{9,... | collective-permute-start | bytes 1572872 | tf_op jit(solution)/shard_map/ppermute | solution.py:421
  66.1 11.1 %collective-permute-start.11 = (bf16[512,512]{1,0:T(8,128)(2,1)S(1)}, bf16[512,512]{1,0:T(8,128)(2,1)S(1)}, u32[]{:S(2)}, u32[]{:S(2)}) collective-permute-start(bf16[512,512]{1,0:T(8,128)(2,1)S(1)} %get-tuple-element.38), channel_id=1, source_target_pairs={{0,64},{1,65},{2,66},{3,67},{4,68},{5,69},{6,70},{7,71},{8,72},{9,... | collective-permute-start | bytes 1572872 | tf_op jit(solution)/shard_map/ppermute | solution.py:421

commit v5 on v4

--- a/solution.py
+++ b/solution.py
@@ -14,6 +14,7 @@
 UVB = 128
 BLOCKS = 8
 SLOTS = 4
+CHUNK = 2
 BIG = 256
 ROWS = 64
 VMEM_LIMIT = 24 * 1024 * 1024
@@ -129,28 +130,25 @@
     )(*[pltpu.with_memory_space_constraint(x, pltpu.HBM) for x in arrays])
 
 
-def forward_body(kinds, ctl, metas, sky, stacked, flipped, outs, scratch):
-    own, pair, far = sky
-    folded, lhs = scratch
+def forward_body(low, blocks, slots, meta, stacked, flipped, out, folded, lhs):
     size = 2 * UVB
-    low = ctl[0]
-    near, outer = tile_steps(ctl)
-    steps = {"own": 0, "near": near, "outer": outer}
-    for kind, meta, out in zip(kinds, metas, outs):
-
-        def pointing(s, carry, step=steps[kind], meta=meta, out=out):
-            oy, ox = meta[OFFSET, s], meta[OFFSET + 1, s]
-            width = meta[WIDTH, s].astype(f32)
-            shift = column_shift(step, ox)
-
-            def transform(count):
-                bins = [(meta[BINS + 2 * k, s], meta[BINS + 2 * k + 1, s]) for k in range(count)]
-                g = row_factor_in_lanes(oy, width)
-                for k, (a, _) in enumerate(bins):
-                    rows = slice(k * size, (k + 1) * size)
-                    table = stacked[a].astype(f32)
-                    lhs[rows, TILE:] = times_rows(table, g[:, TILE:] * alternating()).astype(bf16)
-                    lhs[rows, :TILE] = times_rows(table, g[:, :TILE]).astype(bf16)
+    begin, end = slots
+
+    def pointing(s, carry):
+        oy, ox = meta[OFFSET, s], meta[OFFSET + 1, s]
+        width = meta[WIDTH, s].astype(f32)
+
+        def transform(count):
+            bins = [(meta[BINS + 2 * k, s], meta[BINS + 2 * k + 1, s]) for k in range(count)]
+            g = row_factor_in_lanes(oy, width)
+            for k, (a, _) in enumerate(bins):
+                rows = slice(k * size, (k + 1) * size)
+                table = stacked[a].astype(f32)
+                lhs[rows, TILE:] = times_rows(table, g[:, TILE:] * alternating()).astype(bf16)
+                lhs[rows, :TILE] = times_rows(table, g[:, :TILE]).astype(bf16)
+            parts = [[] for _ in bins]
+            for step, (own, pair, far) in blocks:
+                shift = column_shift(step, ox)
                 first = jnp.dot(lhs[: count * size, TILE:], pair[...], preferred_element_type=f32)
                 for at in range(0, TILE, ROWS):
                     here = slice(at, at + ROWS)
@@ -166,99 +164,78 @@
                     re = q[:UVB, :UVB] - q[UVB:, UVB:]
                     im = q[:UVB, UVB:] + q[UVB:, :UVB]
                     cos, sin = twiddle(a, b, oy, shift)
-                    out[s, k, :, :UVB] = (re * cos - im * sin).astype(out.dtype)
-                    out[s, k, :, UVB:] = (im * cos + re * sin).astype(out.dtype)
-
-            for count in (1, 2):
-
-                @pl.when(meta[USED, s] == count)
-                def _(count=count):
-                    transform(count)
-
+                    parts[k].append((re * cos - im * sin, im * cos + re * sin))
+            for k, values in enumerate(parts):
+                out[s - begin, k, :, :UVB] = sum(re for re, _ in values).astype(out.dtype)
+                out[s - begin, k, :, UVB:] = sum(im for _, im in values).astype(out.dtype)
+
+        for count in (1, 2):
+
+            @pl.when(meta[USED, s] == count)
+            def _(count=count):
+                transform(count)
+
+        return carry
+
+    lax.fori_loop(begin, jnp.minimum(meta[COUNT, 0], end), pointing, 0)
+
+
+def forward(kind, slots, ctl, meta, skies, stacked, flipped):
+    n = len(skies)
+
+    def kernel(ctl, meta, *refs):
+        tiles, (stacked, flipped, out, folded, lhs) = refs[: 3 * n], refs[3 * n :]
+        near, outer = tile_steps(ctl)
+        steps = {"own": (0, -near), "outer": (outer,)}[kind]
+        blocks = [(step, tiles[3 * i : 3 * i + 3]) for i, step in enumerate(steps)]
+        forward_body(ctl[0], blocks, slots, meta, stacked, flipped, out, folded, lhs)
+
+    smem = pl.BlockSpec(memory_space=pltpu.SMEM)
+    vmem = pl.BlockSpec(memory_space=pltpu.VMEM)
+    shape = (slots[1] - slots[0], 2, UVB, 2 * UVB)
+    return pl.pallas_call(
+        kernel,
+        out_shape=pltpu.VMEM(shape, f32 if kind == "own" else bf16),
+        in_specs=[smem] * 2 + [vmem] * (3 * n + 2),
+        out_specs=vmem,
+        scratch_shapes=[
+            pltpu.VMEM((TILE, TILE), bf16),
+            pltpu.VMEM((4 * UVB, PATCH), bf16),
+        ],
+        cost_estimate=cost(2 * n),
+        compiler_params=pltpu.CompilerParams(vmem_limit_bytes=VMEM_LIMIT),
+        name="forward_" + kind + str(slots[0]),
+    )(ctl, meta, *near_by(*[x for tiles in skies for x in tiles]), stacked, flipped)
+
+
+def scale(begin, meta, mine, outer, weight):
+    def kernel(meta, mine, outer, weight, out):
+        def pointing(s, carry):
+            def uv(k, c):
+                w = weight[s, k].astype(f32)
+                v = mine[s, k] + outer[s - begin, k].astype(f32)
+                out[s - begin, k, :, :UVB] = (v[:, :UVB] * w).astype(bf16)
+                out[s - begin, k, :, UVB:] = (v[:, UVB:] * w).astype(bf16)
+                return c
+
+            lax.fori_loop(0, meta[USED, s], uv, 0)
             return carry
 
-        lax.fori_loop(0, meta[COUNT, 0], pointing, 0)
-
-
-def forward(kinds, ctl, metas, sky, stacked, flipped):
-    n = len(kinds)
-
-    def kernel(ctl, *refs):
-        metas, rest = refs[:n], refs[n:]
-        forward_body(kinds, ctl, metas, rest[:3], rest[3], rest[4], rest[5 : 5 + n], rest[5 + n :])
+        lax.fori_loop(begin, jnp.minimum(meta[COUNT, 0], begin + CHUNK), pointing, 0)
 
     smem = pl.BlockSpec(memory_space=pltpu.SMEM)
     vmem = pl.BlockSpec(memory_space=pltpu.VMEM)
     return pl.pallas_call(
         kernel,
-        out_shape=[pltpu.VMEM((SLOTS, 2, UVB, 2 * UVB), f32 if k == "own" else bf16) for k in kinds],
-        in_specs=[smem] * (1 + n) + [vmem] * 5,
-        out_specs=[vmem] * n,
-        scratch_shapes=[
-            pltpu.VMEM((TILE, TILE), bf16),
-            pltpu.VMEM((4 * UVB, PATCH), bf16),
-        ],
-        cost_estimate=cost(3 * n - 2),
-        compiler_params=pltpu.CompilerParams(vmem_limit_bytes=VMEM_LIMIT),
-        name="forward_" + "_".join(kinds),
-    )(ctl, *metas, *near_by(*sky), stacked, flipped)
-
-
-def each_tile(meta, work):
-    def pointing(s, carry):
-        def uv(k, c):
-            work(s, k)
-            return c
-
-        lax.fori_loop(0, meta[USED, s], uv, 0)
-        return carry
-
-    lax.fori_loop(0, meta[COUNT, 0], pointing, 0)
-
-
-def add_partial(meta, mine, other):
-    def kernel(meta, mine, other, out):
-        def work(s, k):
-            out[s, k] = mine[s, k] + other[s, k].astype(f32)
-
-        each_tile(meta, work)
-
-    smem = pl.BlockSpec(memory_space=pltpu.SMEM)
-    vmem = pl.BlockSpec(memory_space=pltpu.VMEM)
-    return pl.pallas_call(
-        kernel,
-        out_shape=pltpu.VMEM((SLOTS, 2, UVB, 2 * UVB), f32),
-        in_specs=[smem] + [vmem] * 2,
-        out_specs=vmem,
-        input_output_aliases={1: 0},
-        compiler_params=pltpu.CompilerParams(vmem_limit_bytes=VMEM_LIMIT),
-        name="add_partial",
-    )(meta, *near_by(mine, other))
-
-
-def scale(meta, mine, near, weight):
-    def kernel(meta, mine, near, weight, out):
-        def work(s, k):
-            w = weight[s, k].astype(f32)
-            v = mine[s, k] + near[s, k].astype(f32)
-            out[s, k, :, :UVB] = (v[:, :UVB] * w).astype(bf16)
-            out[s, k, :, UVB:] = (v[:, UVB:] * w).astype(bf16)
-
-        each_tile(meta, work)
-
-    smem = pl.BlockSpec(memory_space=pltpu.SMEM)
-    vmem = pl.BlockSpec(memory_space=pltpu.VMEM)
-    return pl.pallas_call(
-        kernel,
-        out_shape=pltpu.VMEM((SLOTS, 2, UVB, 2 * UVB), bf16),
+        out_shape=pltpu.VMEM((CHUNK, 2, UVB, 2 * UVB), bf16),
         in_specs=[smem] + [vmem] * 3,
         out_specs=vmem,
         compiler_params=pltpu.CompilerParams(vmem_limit_bytes=VMEM_LIMIT),
-        name="scale",
-    )(meta, *near_by(mine, near, weight))
-
-
-def adjoint_tile(low, step, meta, scaled, stacked, flipped, spread, totals):
+        name="scale" + str(begin),
+    )(meta, *near_by(mine, outer, weight))
+
+
+def adjoint_tile(low, step, begin, meta, scaled, stacked, flipped, spread, totals):
     own, pair, far = totals
 
     def pointing(s, carry):
@@ -271,8 +248,8 @@
             h = col_factor(shift, width)
             for k, (a, b) in enumerate(bins):
                 cos, sin = twiddle(a, b, oy, shift)
-                re = scaled[s, k, :, :UVB].astype(f32)
-                im = scaled[s, k, :, UVB:].astype(f32)
+                re = scaled[s - begin, k, :, :UVB].astype(f32)
+                im = scaled[s - begin, k, :, UVB:].astype(f32)
                 mr = (re * cos + im * sin).astype(bf16)
                 mi = (im * cos - re * sin).astype(bf16)
                 both = jnp.concatenate(
@@ -309,84 +286,60 @@
 
         return carry
 
-    lax.fori_loop(0, meta[COUNT, 0], pointing, 0)
-
-
-def adjoint_own(ctl, meta, scaled, stacked, flipped):
-    def kernel(ctl, meta, sc, stacked, flipped, own, pair, far, spread):
-        def clear(i, c):
-            at = pl.multiple_of(i * ROWS, ROWS)
-            for ref in (own, pair, far):
-                ref[pl.ds(at, ROWS), :] = jnp.zeros((ROWS, TILE), f32)
-            return c
-
-        lax.fori_loop(0, TILE // ROWS, clear, 0)
-        adjoint_tile(ctl[0], 0, meta, sc, stacked, flipped, spread, (own, pair, far))
+    lax.fori_loop(begin, jnp.minimum(meta[COUNT, 0], begin + CHUNK), pointing, 0)
+
+
+def adjoint(kind, chunks, ctl, meta, scaled, begun, last, stacked, flipped):
+    n = len(scaled)
+    started = begun is not None
+
+    def kernel(ctl, meta, *refs):
+        scaled, refs = refs[:n], refs[n:]
+        totals, refs = (refs[:3], refs[3:]) if started else (None, refs)
+        stacked, flipped, *outs, spread = refs
+        near, outer = tile_steps(ctl)
+        step = {"own": 0, "near": near, "outer": outer}[kind]
+        if last:
+            totals = (outs[0],) + totals[1:]
+        else:
+            totals = outs
+        if not started:
+
+            def clear(i, c):
+                at = pl.multiple_of(i * ROWS, ROWS)
+                for ref in totals:
+                    ref[pl.ds(at, ROWS), :] = jnp.zeros((ROWS, TILE), f32)
+                return c
+
+            lax.fori_loop(0, TILE // ROWS, clear, 0)
+        for begin, sc in zip(chunks, scaled):
+            adjoint_tile(ctl[0], step, begin, meta, sc, stacked, flipped, spread, totals)
+        if last:
+
+            def emit(i, c):
+                here = pl.ds(pl.multiple_of(i * ROWS, ROWS), ROWS)
+                for total, out in zip(totals[1:], outs[1:]):
+                    out[here, :] = total[here, :].astype(bf16)
+                return c
+
+            lax.fori_loop(0, TILE // ROWS, emit, 0)
 
     smem = pl.BlockSpec(memory_space=pltpu.SMEM)
     vmem = pl.BlockSpec(memory_space=pltpu.VMEM)
+    first = 2 + n
+    aliases = {first: 0} if last else {first + i: i for i in range(3)}
+    rest = bf16 if last else f32
     return pl.pallas_call(
         kernel,
-        out_shape=[pltpu.VMEM((TILE, TILE), f32)] * 3,
-        in_specs=[smem] * 2 + [vmem] * 3,
+        out_shape=[pltpu.VMEM((TILE, TILE), kept) for kept in (f32, rest, rest)],
+        in_specs=[smem] * 2 + [vmem] * (n + 2 + (3 if started else 0)),
         out_specs=[vmem] * 3,
         scratch_shapes=[pltpu.VMEM((2, 2, 2 * UVB, TILE), bf16)],
-        cost_estimate=cost(2),
+        input_output_aliases=aliases if started else {},
+        cost_estimate=cost(2 * n),
         compiler_params=pltpu.CompilerParams(vmem_limit_bytes=VMEM_LIMIT),
-        name="adjoint_own",
-    )(ctl, meta, *near_by(scaled), stacked, flipped)
-
-
-def adjoint_near(ctl, meta, scaled, begun, stacked, flipped):
-    def kernel(ctl, meta, sc, own0, pair0, far0, stacked, flipped, own, pair, far, spread):
-        near, _ = tile_steps(ctl)
-        adjoint_tile(ctl[0], near, meta, sc, stacked, flipped, spread, (own, pair, far))
-
-    smem = pl.BlockSpec(memory_space=pltpu.SMEM)
-    vmem = pl.BlockSpec(memory_space=pltpu.VMEM)
-    return pl.pallas_call(
-        kernel,
-        out_shape=[pltpu.VMEM((TILE, TILE), f32)] * 3,
-        in_specs=[smem] * 2 + [vmem] * 6,
-        out_specs=[vmem] * 3,
-        scratch_shapes=[pltpu.VMEM((2, 2, 2 * UVB, TILE), bf16)],
-        input_output_aliases={3: 0, 4: 1, 5: 2},
-        cost_estimate=cost(2),
-        compiler_params=pltpu.CompilerParams(vmem_limit_bytes=VMEM_LIMIT),
-        name="adjoint_near",
-    )(ctl, meta, *near_by(scaled, *begun), stacked, flipped)
-
-
-def adjoint_last(ctl, meta, scaled, begun, stacked, flipped):
-    def kernel(ctl, meta, sc, own0, pair, far, stacked, flipped, own, pair_out, far_out, spread):
-        _, outer = tile_steps(ctl)
-        adjoint_tile(ctl[0], outer, meta, sc, stacked, flipped, spread, (own, pair, far))
-
-        def emit(i, c):
-            here = pl.ds(pl.multiple_of(i * ROWS, ROWS), ROWS)
-            pair_out[here, :] = pair[here, :].astype(bf16)
-            far_out[here, :] = far[here, :].astype(bf16)
-            return c
-
-        lax.fori_loop(0, TILE // ROWS, emit, 0)
-
-    smem = pl.BlockSpec(memory_space=pltpu.SMEM)
-    vmem = pl.BlockSpec(memory_space=pltpu.VMEM)
-    return pl.pallas_call(
-        kernel,
-        out_shape=[
-            pltpu.VMEM((TILE, TILE), f32),
-            pltpu.VMEM((TILE, TILE), bf16),
-            pltpu.VMEM((TILE, TILE), bf16),
-        ],
-        in_specs=[smem] * 2 + [vmem] * 6,
-        out_specs=[vmem] * 3,
-        scratch_shapes=[pltpu.VMEM((2, 2, 2 * UVB, TILE), bf16)],
-        input_output_aliases={3: 0},
-        cost_estimate=cost(1),
-        compiler_params=pltpu.CompilerParams(vmem_limit_bytes=VMEM_LIMIT),
-        name="adjoint_last",
-    )(ctl, meta, *near_by(scaled, *begun), stacked, flipped)
+        name="adjoint_" + kind + str(chunks[0]),
+    )(ctl, meta, *near_by(*scaled, *(begun or ())), stacked, flipped)
 
 
 def mesh_moves(rows, cols):
@@ -434,22 +387,32 @@
         far_sky = send(sky, "row_out")
         meta_outer = send(meta, "row_pair_outer")
         meta_own = send(meta, "row_pair")
-        meta_near = send(meta, "row_pair_near")
         own_sky, stacked, flipped = stage(sky, jnp.asarray(stacked_np), jnp.asarray(flipped_np))
         weight = send(uv_weight[0, 0], "row_pair")
         skies = (own_sky, pair_sky, far_sky)
-        (v_outer,) = forward(("outer",), ctl, (meta_outer,), skies, stacked, flipped)
-        from_outer = send(v_outer, "outer")
-        meta_own, meta_near, weight, v_outer = lax.optimization_barrier((meta_own, meta_near, weight, v_outer))
-        v_own, v_near = forward(("own", "near"), ctl, (meta_own, meta_near), skies, stacked, flipped)
-        from_near = send(v_near, "near")
-        v_sum = add_partial(meta_own, v_own, from_outer)
-        scaled = scale(meta_own, v_sum, from_near, weight)
-        scaled_outer = send(scaled, "outer")
-        scaled_near = send(scaled, "near")
-        begun = adjoint_own(ctl, meta_own, scaled, stacked, flipped)
-        begun = adjoint_near(ctl, meta_near, scaled_near, begun, stacked, flipped)
-        own, pair, far = adjoint_last(ctl, meta_outer, scaled_outer, begun, stacked, flipped)
+        chunks = tuple(range(0, SLOTS, CHUNK))
+        from_outer = []
+        for begin in chunks:
+            v_outer = forward("outer", (begin, begin + CHUNK), ctl, meta_outer, [skies], stacked, flipped)
+            from_outer.append(send(v_outer, "outer"))
+            meta_outer, v_outer = lax.optimization_barrier((meta_outer, v_outer))
+        pair_sky, far_sky, meta_own, weight, meta_outer = lax.optimization_barrier(
+            (pair_sky, far_sky, meta_own, weight, meta_outer)
+        )
+        near_skies = [send(x, "near") for x in (sky, pair_sky, far_sky)]
+        meta_near = send(meta_own, "near")
+        v_own = forward("own", (0, SLOTS), ctl, meta_own, [skies, near_skies], stacked, flipped)
+        scaled = []
+        for begin, part in zip(chunks, from_outer):
+            scaled.append(scale(begin, meta_own, v_own, part, weight))
+            meta_own, _ = lax.optimization_barrier((meta_own, scaled[-1]))
+        scaled_outer = [send(x, "outer") for x in scaled]
+        scaled_near = [send(x, "near") for x in scaled]
+        total = adjoint("own", chunks, ctl, meta_own, scaled, None, False, stacked, flipped)
+        total = adjoint("outer", chunks[:1], ctl, meta_outer, scaled_outer[:1], total, False, stacked, flipped)
+        total = adjoint("near", chunks, ctl, meta_near, scaled_near, total, False, stacked, flipped)
+        total = adjoint("outer", chunks[1:], ctl, meta_outer, scaled_outer[1:], total, True, stacked, flipped)
+        own, pair, far = total
         return own + send(pair, "row_pair").astype(f32) + send(far, "row_back").astype(f32)
 
     in_specs = (

time: 79.5 us -> 77.3 us (0.972)
  the two profiles are of different devices: /device:TPU:6 before, /device:TPU:57 now
where the time goes in v5:
time: 77.3 us; the launch traced here: 78.3 us
  starting transfers between devices  34.2 us (44%)
  waiting for transfers between devices  22.8 us (29%)
  Pallas kernels  18.2 us (24%)
  other arithmetic  2.04 us (3%)
  between operations  0.89 us (1%)
    ppermute x17, starting transfers between devices, send(): return lax.ppermute(x, ('ty', 'tx'), moves[what])  34.2 us
    ppermute x17, waiting for transfers between devices, send(): return lax.ppermute(x, ('ty', 'tx'), moves[what])  22.8 us
    pallas_call x4, Pallas kernels, adjoint(): pl.pallas_call(kernel, out_shape=[pltpu.VMEM((TILE, TILE), kept) for kept...  8.21 us
    pallas_call x3, Pallas kernels, forward(): pl.pallas_call(kernel, out_shape=pltpu.VMEM(shape, f32 if kind == 'own' e...  6.06 us
    pallas_call x1, Pallas kernels, stage(): pl.pallas_call(kernel, out_shape=[pltpu.VMEM(x.shape, bf16) for x in arra...  2.46 us
  transfers between devices with their start and end apart: 17, of which 6 were waited for; matrix products, arithmetic and copies ran while one was open for 1% of the time, Pallas kernels for 22%

profile of v5, /device:TPU:57, one launch (start us, length us, event | category | flops | bytes accessed | tf_op | source)
XLA Modules:
  0.0 78.3 jit_solution(18369083170060872033)
XLA Ops:
  0.0 1.2 %collective-permute-start = (bf16[512,512]{1,0:T(8,128)(2,1)}, bf16[512,512]{1,0:T(8,128)(2,1)S(1)}, u32[]{:S(2)}, u32[]{:S(2)}) collective-permute-start(bf16[512,512]{1,0:T(8,128)(2,1)} %refs_0_.1), channel_id=1, source_target_pairs={{0,32},{1,33},{2,34},{3,35},{4,36},{5,37},{6,38},{7,39},{8,40},{9,... | collective-permute-start | bytes 1572872 | tf_op jit(solution)/shard_map/ppermute | solution.py:374
  1.2 2.4 %collective-permute-start.1 = (bf16[512,512]{1,0:T(8,128)(2,1)}, bf16[512,512]{1,0:T(8,128)(2,1)S(1)}, u32[]{:S(2)}, u32[]{:S(2)}) collective-permute-start(bf16[512,512]{1,0:T(8,128)(2,1)} %refs_0_.1), channel_id=1, source_target_pairs={{32,96},{33,97},{34,98},{35,99},{36,100},{37,101},{38,102},{39,103... | collective-permute-start | bytes 1572872 | tf_op jit(solution)/shard_map/ppermute | solution.py:374
  5.1 3.4 %collective-permute-start.4 = (s32[9,4]{1,0:T(8,128)S(1)}, s32[9,4]{1,0:T(8,128)S(1)}, u32[]{:S(2)}, u32[]{:S(2)}) collective-permute-start(s32[9,4]{1,0:T(8,128)S(1)} %add_add_fusion), channel_id=1, source_target_pairs={{1,34},{2,33},{3,36},{4,35},{5,38},{6,37},{7,40},{8,39},{9,42},{10... | collective-permute-start | bytes 440 | tf_op jit(solution)/shard_map/ppermute | solution.py:374
  8.6 1.8 %collective-permute-start.2 = (s32[9,4]{1,0:T(8,128)S(1)}, s32[9,4]{1,0:T(8,128)S(1)}, u32[]{:S(2)}, u32[]{:S(2)}) collective-permute-start(s32[9,4]{1,0:T(8,128)S(1)} %add_add_fusion), channel_id=1, source_target_pairs={{0,32},{1,33},{2,34},{3,35},{4,36},{5,37},{6,38},{7,39},{8,40},{9,... | collective-permute-start | bytes 440 | tf_op jit(solution)/shard_map/ppermute | solution.py:374
  10.5 2.5 %stage.1 = (bf16[512,512]{1,0:T(8,128)(2,1)S(1)}, bf16[8,256,512]{2,1,0:T(8,128)(2,1)S(1)}, bf16[8,512,256]{2,1,0:T(8,128)(2,1)S(1)}) custom-call(bf16[512,512]{1,0:T(8,128)(2,1)} %refs_0_.1, bf16[8,256,512]{2,1,0:T(8,128)(2,1)} %constant.33.clone.refs_1_, bf16[8,512,256]{2,1,0:T(8,128)(2,1)} %constant.34.clone.refs_2_), custom_call_target="tpu_custom_call" | custom-call | bytes 18874368 | tf_op jit(solution)/shard_map/stage/pallas_call | solution.py:121
  14.1 1.5 %forward_outer0.1 = bf16[2,2,128,256]{3,2,1,0:T(8,128)(2,1)S(1)} custom-call(s32[2]{0:T(128)S(1)} %pad_add_fusion.ctl, s32[9,4]{1,0:T(8,128)S(1)} %collective-permute-done.4.meta, bf16[512,512]{1,0:T(8,128)(2,1)S(1)} %get-tuple-element.29.refs_0_, bf16[512,512]{1,0:T(8,128)(2,1)S(1)} %collective-permute-done.refs_1_, ...), custom_call_target="tpu_custom_call" | custom-call | flops 1006632960 | bytes 1048576 | tf_op jit(solution)/shard_map/forward_outer0/pallas_call | solution.py:196
  16.3 2.6 %collective-permute-done.3.weight = bf16[4,2,128,128]{3,2,1,0:T(8,128)(2,1)S(1)} collective-permute-done((bf16[4,2,128,128]{3,2,1,0:T(8,128)(2,1)}, bf16[4,2,128,128]{3,2,1,0:T(8,128)(2,1)S(1)}, u32[]{:S(2)}, u32[]{:S(2)}) %collective-permute-start.3) | collective-permute-done | bytes 262176 | tf_op jit(solution)/shard_map/ppermute | solution.py:374
  19.0 1.4 %collective-permute-start.6 = (bf16[512,512]{1,0:T(8,128)(2,1)S(1)}, bf16[512,512]{1,0:T(8,128)(2,1)S(1)}, u32[]{:S(2)}, u32[]{:S(2)}) collective-permute-start(bf16[512,512]{1,0:T(8,128)(2,1)S(1)} %collective-permute-done.refs_1_), channel_id=1, source_target_pairs={{0,1},{1,0},{2,3},{3,2},{4,5},{5,4},{6,7},{7,6},{8,9},{9,8},{10,11... | collective-permute-start | bytes 1572872 | tf_op jit(solution)/shard_map/ppermute | solution.py:374
  20.3 5.0 %collective-permute-start.8 = (bf16[2,2,128,256]{3,2,1,0:T(8,128)(2,1)S(1)}, bf16[2,2,128,256]{3,2,1,0:T(8,128)(2,1)S(1)}, u32[]{:S(2)}, u32[]{:S(2)}) collective-permute-start(bf16[2,2,128,256]{3,2,1,0:T(8,128)(2,1)S(1)} %forward_outer0.1), channel_id=1, source_target_pairs={{1,2},{2,1},{3,4},{4,3},{5,6},{6,5},{7,8},{8,7},{9,10},{10,9},{11,... | collective-permute-start | bytes 786440 | tf_op jit(solution)/shard_map/ppermute | solution.py:374
  25.4 2.0 %collective-permute-start.9 = (bf16[2,2,128,256]{3,2,1,0:T(8,128)(2,1)S(1)}, bf16[2,2,128,256]{3,2,1,0:T(8,128)(2,1)S(1)}, u32[]{:S(2)}, u32[]{:S(2)}) collective-permute-start(bf16[2,2,128,256]{3,2,1,0:T(8,128)(2,1)S(1)} %forward_outer2.1), channel_id=1, source_target_pairs={{1,2},{2,1},{3,4},{4,3},{5,6},{6,5},{7,8},{8,7},{9,10},{10,9},{11,... | collective-permute-start | bytes 786440 | tf_op jit(solution)/shard_map/ppermute | solution.py:374
  27.4 3.9 %forward_own0.1.mine = f32[4,2,128,256]{3,2,1,0:T(8,128)S(1)} custom-call(s32[2]{0:T(128)S(1)} %pad_add_fusion.ctl, s32[9,4]{1,0:T(8,128)S(1)} %collective-permute-done.2.meta, bf16[512,512]{1,0:T(8,128)(2,1)S(1)} %get-tuple-element.29.refs_0_, bf16[512,512]{1,0:T(8,128)(2,1)S(1)} %collective-permute-done.refs_1_, ...), custom_call_target="tpu_custom_call" | custom-call | flops 2013265920 | bytes 1048576 | tf_op jit(solution)/shard_map/forward_own0/pallas_call | solution.py:196
  31.4 3.8 %collective-permute-done.8.outer = bf16[2,2,128,256]{3,2,1,0:T(8,128)(2,1)S(1)} collective-permute-done((bf16[2,2,128,256]{3,2,1,0:T(8,128)(2,1)S(1)}, bf16[2,2,128,256]{3,2,1,0:T(8,128)(2,1)S(1)}, u32[]{:S(2)}, u32[]{:S(2)}) %collective-permute-start.8) | collective-permute-done | bytes 262176 | tf_op jit(solution)/shard_map/ppermute | solution.py:374
  35.9 5.0 %collective-permute-start.14 = (bf16[2,2,128,256]{3,2,1,0:T(8,128)(2,1)S(1)}, bf16[2,2,128,256]{3,2,1,0:T(8,128)(2,1)S(1)}, u32[]{:S(2)}, u32[]{:S(2)}) collective-permute-start(bf16[2,2,128,256]{3,2,1,0:T(8,128)(2,1)S(1)} %scale0.1.refs_0_), channel_id=1, source_target_pairs={{1,2},{2,1},{3,4},{4,3},{5,6},{6,5},{7,8},{8,7},{9,10},{10,9},{11,... | collective-permute-start | bytes 786440 | tf_op jit(solution)/shard_map/ppermute | solution.py:374
  42.4 2.3 %collective-permute-start.10 = (bf16[2,2,128,256]{3,2,1,0:T(8,128)(2,1)S(1)}, bf16[2,2,128,256]{3,2,1,0:T(8,128)(2,1)S(1)}, u32[]{:S(2)}, u32[]{:S(2)}) collective-permute-start(bf16[2,2,128,256]{3,2,1,0:T(8,128)(2,1)S(1)} %scale2.1.refs_1_), channel_id=1, source_target_pairs={{1,2},{2,1},{3,4},{4,3},{5,6},{6,5},{7,8},{8,7},{9,10},{10,9},{11,... | collective-permute-start | bytes 786440 | tf_op jit(solution)/shard_map/ppermute | solution.py:374
  44.7 3.1 %adjoint_own0.1 = (f32[512,512]{1,0:T(8,128)S(1)}, f32[512,512]{1,0:T(8,128)S(1)}, f32[512,512]{1,0:T(8,128)S(1)}) custom-call(s32[2]{0:T(128)S(1)} %pad_add_fusion.ctl, s32[9,4]{1,0:T(8,128)S(1)} %collective-permute-done.2.meta, bf16[2,2,128,256]{3,2,1,0:T(8,128)(2,1)S(1)} %scale0.1.refs_0_, bf16[2,2,128,256]{3,2,1,0:T(8,128)(2,1)S(1)} %scale2.1.refs_1_, ...), custom_call_target="tpu_custom_call" | custom-call | flops 2013265920 | bytes 1048576 | tf_op jit(solution)/shard_map/adjoint_own0/pallas_call | solution.py:332
  47.8 1.5 %adjoint_outer0.1 = (f32[512,512]{1,0:T(8,128)S(1)}, f32[512,512]{1,0:T(8,128)S(1)}, f32[512,512]{1,0:T(8,128)S(1)}) custom-call(s32[2]{0:T(128)S(1)} %pad_add_fusion.ctl, s32[9,4]{1,0:T(8,128)S(1)} %collective-permute-done.4.meta, ...), custom_call_target="tpu_custom_call", output_to_operand_aliasing={{0}: (3, {}), {1}: (4, {}), {2}: (5, {})} | custom-call | flops 1006632960 | bytes 1048576 | tf_op jit(solution)/shard_map/adjoint_outer0/pallas_call | solution.py:332
  49.4 2.7 %adjoint_near0.1 = (f32[512,512]{1,0:T(8,128)S(1)}, f32[512,512]{1,0:T(8,128)S(1)}, f32[512,512]{1,0:T(8,128)S(1)}) custom-call(s32[2]{0:T(128)S(1)} %pad_add_fusion.ctl, s32[9,4]{1,0:T(8,128)S(1)} %collective-permute-done.11.meta, ...), custom_call_target="tpu_custom_call", output_to_operand_aliasing={{0}: (4, {}), {1}: (5, {}), {2}: (6, {})} | custom-call | flops 2013265920 | bytes 1048576 | tf_op jit(solution)/shard_map/adjoint_near0/pallas_call | solution.py:332
  52.1 2.2 %collective-permute-done.10.refs_0_ = bf16[2,2,128,256]{3,2,1,0:T(8,128)(2,1)S(1)} collective-permute-done((bf16[2,2,128,256]{3,2,1,0:T(8,128)(2,1)S(1)}, bf16[2,2,128,256]{3,2,1,0:T(8,128)(2,1)S(1)}, u32[]{:S(2)}, u32[]{:S(2)}) %collective-permute-start.10) | collective-permute-done | bytes 262176 | tf_op jit(solution)/shard_map/ppermute | solution.py:374
  54.4 0.8 %adjoint_outer2.1 = (f32[512,512]{1,0:T(8,128)S(1)}, bf16[512,512]{1,0:T(8,128)(2,1)S(1)}, bf16[512,512]{1,0:T(8,128)(2,1)S(1)}) custom-call(s32[2]{0:T(128)S(1)} %pad_add_fusion.ctl, s32[9,4]{1,0:T(8,128)S(1)} %collective-permute-done.4.meta, bf16[2,2,128,256]{3,2,1,0:T(8,128)(2,1)S(1)} %collective-permute-done.10.refs_0_, ...), custom_call_target="tpu_custom_call", output_to_operand_aliasing={{0}: (3, {})} | custom-call | flops 1006632960 | bytes 1048576 | tf_op jit(solution)/shard_map/adjoint_outer2/pallas_call | solution.py:332
  55.2 7.1 %collective-permute-start.15 = (bf16[512,512]{1,0:T(8,128)(2,1)S(1)}, bf16[512,512]{1,0:T(8,128)(2,1)S(1)}, u32[]{:S(2)}, u32[]{:S(2)}) collective-permute-start(bf16[512,512]{1,0:T(8,128)(2,1)S(1)} %get-tuple-element.51), channel_id=1, source_target_pairs={{0,32},{1,33},{2,34},{3,35},{4,36},{5,37},{6,38},{7,39},{8,40},{9,... | collective-permute-start | bytes 1572872 | tf_op jit(solution)/shard_map/ppermute | solution.py:374
  62.4 1.3 %collective-permute-start.16 = (bf16[512,512]{1,0:T(8,128)(2,1)S(1)}, bf16[512,512]{1,0:T(8,128)(2,1)S(1)}, u32[]{:S(2)}, u32[]{:S(2)}) collective-permute-start(bf16[512,512]{1,0:T(8,128)(2,1)S(1)} %get-tuple-element.52), channel_id=1, source_target_pairs={{0,64},{1,65},{2,66},{3,67},{4,68},{5,69},{6,70},{7,71},{8,72},{9,... | collective-permute-start | bytes 1572872 | tf_op jit(solution)/shard_map/ppermute | solution.py:374
  63.6 9.8 %collective-permute-done.15 = bf16[512,512]{1,0:T(8,128)(2,1)S(1)} collective-permute-done((bf16[512,512]{1,0:T(8,128)(2,1)S(1)}, bf16[512,512]{1,0:T(8,128)(2,1)S(1)}, u32[]{:S(2)}, u32[]{:S(2)}) %collective-permute-start.15) | collective-permute-done | bytes 524320 | tf_op jit(solution)/shard_map/ppermute | solution.py:374
  73.5 3.6 %collective-permute-done.16 = bf16[512,512]{1,0:T(8,128)(2,1)S(1)} collective-permute-done((bf16[512,512]{1,0:T(8,128)(2,1)S(1)}, bf16[512,512]{1,0:T(8,128)(2,1)S(1)}, u32[]{:S(2)}, u32[]{:S(2)}) %collective-permute-start.16) | collective-permute-done | bytes 524320 | tf_op jit(solution)/shard_map/ppermute | solution.py:374
  77.1 1.2 %convert_add_fusion = f32[512,512]{1,0:T(8,128)} fusion(bf16[512,512]{1,0:T(8,128)(2,1)S(1)} %collective-permute-done.16, f32[512,512]{1,0:T(8,128)S(1)} %get-tuple-element.50, bf16[512,512]{1,0:T(8,128)(2,1)S(1)} %collective-permute-done.15), kind=kLoop, calls=%fused_computation | loop fusion | flops 1048576 | bytes 3145728 | tf_op jit(solution)/shard_map/add | solution.py:416
  (26 shorter events, 5.1 us)
Async XLA Ops:
  0.0 13.4 %collective-permute-start = (bf16[512,512]{1,0:T(8,128)(2,1)}, bf16[512,512]{1,0:T(8,128)(2,1)S(1)}, u32[]{:S(2)}, u32[]{:S(2)}) collective-permute-start(bf16[512,512]{1,0:T(8,128)(2,1)} %refs_0_.1), channel_id=1, source_target_pairs={{0,32},{1,33},{2,34},{3,35},{4,36},{5,37},{6,38},{7,39},{8,40},{9,... | collective-permute-start | bytes 1572872 | tf_op jit(solution)/shard_map/ppermute | solution.py:374
  1.2 12.9 %collective-permute-start.1 = (bf16[512,512]{1,0:T(8,128)(2,1)}, bf16[512,512]{1,0:T(8,128)(2,1)S(1)}, u32[]{:S(2)}, u32[]{:S(2)}) collective-permute-start(bf16[512,512]{1,0:T(8,128)(2,1)} %refs_0_.1), channel_id=1, source_target_pairs={{32,96},{33,97},{34,98},{35,99},{36,100},{37,101},{38,102},{39,103... | collective-permute-start | bytes 1572872 | tf_op jit(solution)/shard_map/ppermute | solution.py:374
  5.1 7.9 %collective-permute-start.4 = (s32[9,4]{1,0:T(8,128)S(1)}, s32[9,4]{1,0:T(8,128)S(1)}, u32[]{:S(2)}, u32[]{:S(2)}) collective-permute-start(s32[9,4]{1,0:T(8,128)S(1)} %add_add_fusion), channel_id=1, source_target_pairs={{1,34},{2,33},{3,36},{4,35},{5,38},{6,37},{7,40},{8,39},{9,42},{10... | collective-permute-start | bytes 440 | tf_op jit(solution)/shard_map/ppermute | solution.py:374
  8.6 7.7 %collective-permute-start.2 = (s32[9,4]{1,0:T(8,128)S(1)}, s32[9,4]{1,0:T(8,128)S(1)}, u32[]{:S(2)}, u32[]{:S(2)}) collective-permute-start(s32[9,4]{1,0:T(8,128)S(1)} %add_add_fusion), channel_id=1, source_target_pairs={{0,32},{1,33},{2,34},{3,35},{4,36},{5,37},{6,38},{7,39},{8,40},{9,... | collective-permute-start | bytes 440 | tf_op jit(solution)/shard_map/ppermute | solution.py:374
  10.4 8.6 %collective-permute-start.3 = (bf16[4,2,128,128]{3,2,1,0:T(8,128)(2,1)}, bf16[4,2,128,128]{3,2,1,0:T(8,128)(2,1)S(1)}, u32[]{:S(2)}, u32[]{:S(2)}) collective-permute-start(bf16[4,2,128,128]{3,2,1,0:T(8,128)(2,1)} %bitcast.19), channel_id=1, source_target_pairs={{0,32},{1,33},{2,34},{3,35},{4,36},{5,37},{6,38},{7,39},{8,40},{9,... | collective-permute-start | bytes 786440 | tf_op jit(solution)/shard_map/ppermute | solution.py:374
  10.5 2.5 %copy-start = (bf16[512,512]{1,0:T(8,128)(2,1)S(1)}, bf16[512,512]{1,0:T(8,128)(2,1)}, u32[]{:S(2)}) copy-start(bf16[512,512]{1,0:T(8,128)(2,1)} %refs_0_.1) | copy-start | bytes 1572868
  13.0 14.4 %collective-permute-start.5 = (bf16[512,512]{1,0:T(8,128)(2,1)S(1)}, bf16[512,512]{1,0:T(8,128)(2,1)S(1)}, u32[]{:S(2)}, u32[]{:S(2)}) collective-permute-start(bf16[512,512]{1,0:T(8,128)(2,1)S(1)} %copy-done), channel_id=1, source_target_pairs={{0,1},{1,0},{2,3},{3,2},{4,5},{5,4},{6,7},{7,6},{8,9},{9,8},{10,11... | collective-permute-start | bytes 1572872 | tf_op jit(solution)/shard_map/ppermute | solution.py:374
  19.0 8.5 %collective-permute-start.6 = (bf16[512,512]{1,0:T(8,128)(2,1)S(1)}, bf16[512,512]{1,0:T(8,128)(2,1)S(1)}, u32[]{:S(2)}, u32[]{:S(2)}) collective-permute-start(bf16[512,512]{1,0:T(8,128)(2,1)S(1)} %collective-permute-done.refs_1_), channel_id=1, source_target_pairs={{0,1},{1,0},{2,3},{3,2},{4,5},{5,4},{6,7},{7,6},{8,9},{9,8},{10,11... | collective-permute-start | bytes 1572872 | tf_op jit(solution)/shard_map/ppermute | solution.py:374
  20.3 7.1 %collective-permute-start.7 = (bf16[512,512]{1,0:T(8,128)(2,1)S(1)}, bf16[512,512]{1,0:T(8,128)(2,1)S(1)}, u32[]{:S(2)}, u32[]{:S(2)}) collective-permute-start(bf16[512,512]{1,0:T(8,128)(2,1)S(1)} %collective-permute-done.1.refs_2_), channel_id=1, source_target_pairs={{0,1},{1,0},{2,3},{3,2},{4,5},{5,4},{6,7},{7,6},{8,9},{9,8},{10,11... | collective-permute-start | bytes 1572872 | tf_op jit(solution)/shard_map/ppermute | solution.py:374
  20.3 14.8 %collective-permute-start.8 = (bf16[2,2,128,256]{3,2,1,0:T(8,128)(2,1)S(1)}, bf16[2,2,128,256]{3,2,1,0:T(8,128)(2,1)S(1)}, u32[]{:S(2)}, u32[]{:S(2)}) collective-permute-start(bf16[2,2,128,256]{3,2,1,0:T(8,128)(2,1)S(1)} %forward_outer0.1), channel_id=1, source_target_pairs={{1,2},{2,1},{3,4},{4,3},{5,6},{6,5},{7,8},{8,7},{9,10},{10,9},{11,... | collective-permute-start | bytes 786440 | tf_op jit(solution)/shard_map/ppermute | solution.py:374
  25.4 15.6 %collective-permute-start.9 = (bf16[2,2,128,256]{3,2,1,0:T(8,128)(2,1)S(1)}, bf16[2,2,128,256]{3,2,1,0:T(8,128)(2,1)S(1)}, u32[]{:S(2)}, u32[]{:S(2)}) collective-permute-start(bf16[2,2,128,256]{3,2,1,0:T(8,128)(2,1)S(1)} %forward_outer2.1), channel_id=1, source_target_pairs={{1,2},{2,1},{3,4},{4,3},{5,6},{6,5},{7,8},{8,7},{9,10},{10,9},{11,... | collective-permute-start | bytes 786440 | tf_op jit(solution)/shard_map/ppermute | solution.py:374
  35.9 11.9 %collective-permute-start.14 = (bf16[2,2,128,256]{3,2,1,0:T(8,128)(2,1)S(1)}, bf16[2,2,128,256]{3,2,1,0:T(8,128)(2,1)S(1)}, u32[]{:S(2)}, u32[]{:S(2)}) collective-permute-start(bf16[2,2,128,256]{3,2,1,0:T(8,128)(2,1)S(1)} %scale0.1.refs_0_), channel_id=1, source_target_pairs={{1,2},{2,1},{3,4},{4,3},{5,6},{6,5},{7,8},{8,7},{9,10},{10,9},{11,... | collective-permute-start | bytes 786440 | tf_op jit(solution)/shard_map/ppermute | solution.py:374
  40.9 8.4 %collective-permute-start.11 = (s32[9,4]{1,0:T(8,128)S(1)}, s32[9,4]{1,0:T(8,128)S(1)}, u32[]{:S(2)}, u32[]{:S(2)}) collective-permute-start(s32[9,4]{1,0:T(8,128)S(1)} %collective-permute-done.2.meta), channel_id=1, source_target_pairs={{0,1},{1,0},{2,3},{3,2},{4,5},{5,4},{6,7},{7,6},{8,9},{9,8},{10,11... | collective-permute-start | bytes 440 | tf_op jit(solution)/shard_map/ppermute | solution.py:374
  41.7 7.7 %collective-permute-start.13 = (bf16[2,2,128,256]{3,2,1,0:T(8,128)(2,1)S(1)}, bf16[2,2,128,256]{3,2,1,0:T(8,128)(2,1)S(1)}, u32[]{:S(2)}, u32[]{:S(2)}) collective-permute-start(bf16[2,2,128,256]{3,2,1,0:T(8,128)(2,1)S(1)} %scale2.1.refs_1_), channel_id=1, source_target_pairs={{0,1},{1,0},{2,3},{3,2},{4,5},{5,4},{6,7},{7,6},{8,9},{9,8},{10,11... | collective-permute-start | bytes 786440 | tf_op jit(solution)/shard_map/ppermute | solution.py:374
  42.3 7.1 %collective-permute-start.12 = (bf16[2,2,128,256]{3,2,1,0:T(8,128)(2,1)S(1)}, bf16[2,2,128,256]{3,2,1,0:T(8,128)(2,1)S(1)}, u32[]{:S(2)}, u32[]{:S(2)}) collective-permute-start(bf16[2,2,128,256]{3,2,1,0:T(8,128)(2,1)S(1)} %scale0.1.refs_0_), channel_id=1, source_target_pairs={{0,1},{1,0},{2,3},{3,2},{4,5},{5,4},{6,7},{7,6},{8,9},{9,8},{10,11... | collective-permute-start | bytes 786440 | tf_op jit(solution)/shard_map/ppermute | solution.py:374
  42.4 12.0 %collective-permute-start.10 = (bf16[2,2,128,256]{3,2,1,0:T(8,128)(2,1)S(1)}, bf16[2,2,128,256]{3,2,1,0:T(8,128)(2,1)S(1)}, u32[]{:S(2)}, u32[]{:S(2)}) collective-permute-start(bf16[2,2,128,256]{3,2,1,0:T(8,128)(2,1)S(1)} %scale2.1.refs_1_), channel_id=1, source_target_pairs={{1,2},{2,1},{3,4},{4,3},{5,6},{6,5},{7,8},{8,7},{9,10},{10,9},{11,... | collective-permute-start | bytes 786440 | tf_op jit(solution)/shard_map/ppermute | solution.py:374
  55.2 18.3 %collective-permute-start.15 = (bf16[512,512]{1,0:T(8,128)(2,1)S(1)}, bf16[512,512]{1,0:T(8,128)(2,1)S(1)}, u32[]{:S(2)}, u32[]{:S(2)}) collective-permute-start(bf16[512,512]{1,0:T(8,128)(2,1)S(1)} %get-tuple-element.51), channel_id=1, source_target_pairs={{0,32},{1,33},{2,34},{3,35},{4,36},{5,37},{6,38},{7,39},{8,40},{9,... | collective-permute-start | bytes 1572872 | tf_op jit(solution)/shard_map/ppermute | solution.py:374
  62.4 14.7 %collective-permute-start.16 = (bf16[512,512]{1,0:T(8,128)(2,1)S(1)}, bf16[512,512]{1,0:T(8,128)(2,1)S(1)}, u32[]{:S(2)}, u32[]{:S(2)}) collective-permute-start(bf16[512,512]{1,0:T(8,128)(2,1)S(1)} %get-tuple-element.52), channel_id=1, source_target_pairs={{0,64},{1,65},{2,66},{3,67},{4,68},{5,69},{6,70},{7,71},{8,72},{9,... | collective-permute-start | bytes 1572872 | tf_op jit(solution)/shard_map/ppermute | solution.py:374

commit v6 on v5

--- a/solution.py
+++ b/solution.py
@@ -16,6 +16,7 @@
 SLOTS = 4
 CHUNK = 2
 BIG = 256
+HALF = 256
 ROWS = 64
 VMEM_LIMIT = 24 * 1024 * 1024
 
@@ -71,8 +72,25 @@
     return (x.reshape(x.shape[0] // 8, 8, x.shape[1]) * factor[None]).reshape(x.shape)
 
 
-def col_factor(shift, width):
-    n = lax.broadcasted_iota(jnp.int32, (8, TILE), 1) + shift
+def half_in_window(step, ox):
+    half = ((step == -1) & (ox <= HALF)) | ((step == 1) & (ox >= HALF))
+    return half, pl.multiple_of(jnp.where(step == 1, HALF, 0), HALF)
+
+
+def variants(used, half):
+    def run(body):
+        for count in (1, 2):
+            for narrow in (False, True):
+
+                @pl.when((used == count) & (half == narrow))
+                def _(count=count, narrow=narrow):
+                    body(count, narrow)
+
+    return run
+
+
+def col_factor(shift, width, columns):
+    n = lax.broadcasted_iota(jnp.int32, (8, columns), 1) + shift
     inside = (n >= 0) & (n < PATCH)
     d = n.astype(f32) - (PATCH // 2)
     return jnp.where(inside, falloff(d * d, width), 0.0)
@@ -104,10 +122,6 @@
     return 1 - 2 * side, 2 * side - 1
 
 
-def lanes():
-    return [slice(lane * 128, lane * 128 + 128) for lane in range(TILE // 128)]
-
-
 def stage(sky, stacked, flipped):
     def kernel(*refs):
         sems = refs[6]
@@ -138,7 +152,10 @@
         oy, ox = meta[OFFSET, s], meta[OFFSET + 1, s]
         width = meta[WIDTH, s].astype(f32)
 
-        def transform(count):
+        half, start = half_in_window(blocks[-1][0], ox)
+
+        @variants(meta[USED, s], half)
+        def transform(count, narrow):
             bins = [(meta[BINS + 2 * k, s], meta[BINS + 2 * k + 1, s]) for k in range(count)]
             g = row_factor_in_lanes(oy, width)
             for k, (a, _) in enumerate(bins):
@@ -147,20 +164,24 @@
                 lhs[rows, TILE:] = times_rows(table, g[:, TILE:] * alternating()).astype(bf16)
                 lhs[rows, :TILE] = times_rows(table, g[:, :TILE]).astype(bf16)
             parts = [[] for _ in bins]
-            for step, (own, pair, far) in blocks:
+            for i, (step, (own, pair, far)) in enumerate(blocks):
+                cut = narrow and i == len(blocks) - 1
+                columns = HALF if cut else TILE
+                part = pl.ds(start, HALF) if cut else slice(0, TILE)
                 shift = column_shift(step, ox)
-                first = jnp.dot(lhs[: count * size, TILE:], pair[...], preferred_element_type=f32)
+                first = jnp.dot(lhs[: count * size, TILE:], pair[:, part], preferred_element_type=f32)
                 for at in range(0, TILE, ROWS):
                     here = slice(at, at + ROWS)
-                    rows = lax.broadcasted_iota(jnp.int32, (ROWS, TILE), 0) + at
+                    rows = lax.broadcasted_iota(jnp.int32, (ROWS, columns), 0) + at
                     mine = jnp.where(rows >= oy, 1, 0) != low
-                    both = jnp.where(mine, own[here, :].astype(f32), far[here, :].astype(f32))
-                    folded[here, :] = both.astype(bf16)
-                first += jnp.dot(lhs[: count * size, :TILE], folded[...], preferred_element_type=f32)
-                first = times_rows(first, col_factor(shift, width)).astype(bf16)
+                    both = jnp.where(mine, own[here, part].astype(f32), far[here, part].astype(f32))
+                    folded[here, :columns] = both.astype(bf16)
+                first += jnp.dot(lhs[: count * size, :TILE], folded[:, :columns], preferred_element_type=f32)
+                h = col_factor(shift + (start if cut else 0), width, columns)
+                first = times_rows(first, h).astype(bf16)
                 for k, (a, b) in enumerate(bins):
                     rows = first[k * size : (k + 1) * size]
-                    q = jnp.dot(rows, flipped[b], preferred_element_type=f32)
+                    q = jnp.dot(rows, flipped[b, part, :], preferred_element_type=f32)
                     re = q[:UVB, :UVB] - q[UVB:, UVB:]
                     im = q[:UVB, UVB:] + q[UVB:, :UVB]
                     cos, sin = twiddle(a, b, oy, shift)
@@ -168,12 +189,6 @@
             for k, values in enumerate(parts):
                 out[s - begin, k, :, :UVB] = sum(re for re, _ in values).astype(out.dtype)
                 out[s - begin, k, :, UVB:] = sum(im for _, im in values).astype(out.dtype)
-
-        for count in (1, 2):
-
-            @pl.when(meta[USED, s] == count)
-            def _(count=count):
-                transform(count)
 
         return carry
 
@@ -243,9 +258,14 @@
         width = meta[WIDTH, s].astype(f32)
         shift = column_shift(step, ox)
 
-        def transform(count):
+        half, start = half_in_window(step, ox)
+
+        @variants(meta[USED, s], half)
+        def transform(count, narrow):
             bins = [(meta[BINS + 2 * k, s], meta[BINS + 2 * k + 1, s]) for k in range(count)]
-            h = col_factor(shift, width)
+            columns = HALF if narrow else TILE
+            left = start if narrow else 0
+            h = col_factor(shift + left, width, columns)
             for k, (a, b) in enumerate(bins):
                 cos, sin = twiddle(a, b, oy, shift)
                 re = scaled[s - begin, k, :, :UVB].astype(f32)
@@ -255,34 +275,33 @@
                 both = jnp.concatenate(
                     [jnp.concatenate([mr, mi], axis=1), jnp.concatenate([mi, -mr], axis=1)], axis=0
                 )
-                value = jnp.dot(both, stacked[b], preferred_element_type=f32)
-                spread[0, k] = times_rows(value, h).astype(bf16)
-                spread[1, k] = times_rows(value, h * alternating()).astype(bf16)
+                value = jnp.dot(both, stacked[b, :, pl.ds(left, columns)], preferred_element_type=f32)
+                spread[0, k, :, :columns] = times_rows(value, h).astype(bf16)
+                spread[1, k, :, :columns] = times_rows(value, h * alternating()[:, :columns]).astype(bf16)
 
             def image(at, upper):
                 here = slice(at, at + BIG)
-                back = jnp.dot(flipped[bins[0][0], here, :], spread[upper, 0], preferred_element_type=f32)
-                for k in range(1, count):
-                    back += jnp.dot(flipped[bins[k][0], here, :], spread[upper, k], preferred_element_type=f32)
+                back = None
+                for k in range(count):
+                    part = jnp.dot(
+                        flipped[bins[k][0], here, :], spread[upper, k, :, :columns], preferred_element_type=f32
+                    )
+                    back = part if back is None else back + part
                 g, rows = row_factor(at + upper * TILE, BIG, oy, width)
-                return [back[:, part] * g for part in lanes()], rows
-
+                values = [back[:, lane : lane + 128] * g for lane in range(0, columns, 128)]
+                return values, rows
+
+            places = [pl.ds(pl.multiple_of(left + lane, 128), 128) for lane in range(0, columns, 128)]
             for at in range(0, TILE, BIG):
                 here = slice(at, at + BIG)
                 values, _ = image(at, 1)
-                for part, v in zip(lanes(), values):
+                for part, v in zip(places, values):
                     pair[here, part] = pair[here, part] + v
                 values, rows = image(at, 0)
                 mine = jnp.where(rows >= oy, 1, 0) != low
-                for part, v in zip(lanes(), values):
+                for part, v in zip(places, values):
                     own[here, part] = own[here, part] + jnp.where(mine, v, 0.0)
                     far[here, part] = far[here, part] + jnp.where(mine, 0.0, v)
-
-        for count in (1, 2):
-
-            @pl.when(meta[USED, s] == count)
-            def _(count=count):
-                transform(count)
 
         return carry
 
@@ -390,17 +409,17 @@
         own_sky, stacked, flipped = stage(sky, jnp.asarray(stacked_np), jnp.asarray(flipped_np))
         weight = send(uv_weight[0, 0], "row_pair")
         skies = (own_sky, pair_sky, far_sky)
+        meta_near = send(meta, "row_pair_near")
         chunks = tuple(range(0, SLOTS, CHUNK))
         from_outer = []
         for begin in chunks:
             v_outer = forward("outer", (begin, begin + CHUNK), ctl, meta_outer, [skies], stacked, flipped)
             from_outer.append(send(v_outer, "outer"))
             meta_outer, v_outer = lax.optimization_barrier((meta_outer, v_outer))
-        pair_sky, far_sky, meta_own, weight, meta_outer = lax.optimization_barrier(
-            (pair_sky, far_sky, meta_own, weight, meta_outer)
+        pair_sky, far_sky, meta_own, meta_near, weight, meta_outer = lax.optimization_barrier(
+            (pair_sky, far_sky, meta_own, meta_near, weight, meta_outer)
         )
         near_skies = [send(x, "near") for x in (sky, pair_sky, far_sky)]
-        meta_near = send(meta_own, "near")
         v_own = forward("own", (0, SLOTS), ctl, meta_own, [skies, near_skies], stacked, flipped)
         scaled = []
         for begin, part in zip(chunks, from_outer):

time: 77.3 us -> 76.9 us (level)
  the two profiles are of different devices: /device:TPU:57 before, /device:TPU:124 now
where the time goes in v6:
time: 76.9 us; the launch traced here: 76.7 us
  starting transfers between devices  34 us (44%)
  Pallas kernels  21.8 us (28%)
  waiting for transfers between devices  17.9 us (23%)
  other arithmetic  2.04 us (3%)
  between operations  0.87 us (1%)
    ppermute x17, starting transfers between devices, send(): return lax.ppermute(x, ('ty', 'tx'), moves[what])  34 us
    ppermute x17, waiting for transfers between devices, send(): return lax.ppermute(x, ('ty', 'tx'), moves[what])  17.9 us
    pallas_call x3, Pallas kernels, forward(): pl.pallas_call(kernel, out_shape=pltpu.VMEM(shape, f32 if kind == 'own' e...  9.35 us
    pallas_call x4, Pallas kernels, adjoint(): pl.pallas_call(kernel, out_shape=[pltpu.VMEM((TILE, TILE), kept) for kept...  8.45 us
    pallas_call x1, Pallas kernels, stage(): pl.pallas_call(kernel, out_shape=[pltpu.VMEM(x.shape, bf16) for x in arra...  2.46 us
  transfers between devices with their start and end apart: 17, of which 4 were waited for; matrix products, arithmetic and copies ran while one was open for 1% of the time, Pallas kernels for 27%

profile of v6, /device:TPU:124, one launch (start us, length us, event | category | flops | bytes accessed | tf_op | source)
XLA Modules:
  0.0 76.7 jit_solution(15852911041995328601)
XLA Ops:
  0.0 1.2 %collective-permute-start = (bf16[512,512]{1,0:T(8,128)(2,1)}, bf16[512,512]{1,0:T(8,128)(2,1)S(1)}, u32[]{:S(2)}, u32[]{:S(2)}) collective-permute-start(bf16[512,512]{1,0:T(8,128)(2,1)} %refs_0_.1), channel_id=1, source_target_pairs={{0,32},{1,33},{2,34},{3,35},{4,36},{5,37},{6,38},{7,39},{8,40},{9,... | collective-permute-start | bytes 1572872 | tf_op jit(solution)/shard_map/ppermute | solution.py:393
  1.2 2.7 %collective-permute-start.1 = (bf16[512,512]{1,0:T(8,128)(2,1)}, bf16[512,512]{1,0:T(8,128)(2,1)S(1)}, u32[]{:S(2)}, u32[]{:S(2)}) collective-permute-start(bf16[512,512]{1,0:T(8,128)(2,1)} %refs_0_.1), channel_id=1, source_target_pairs={{32,96},{33,97},{34,98},{35,99},{36,100},{37,101},{38,102},{39,103... | collective-permute-start | bytes 1572872 | tf_op jit(solution)/shard_map/ppermute | solution.py:393
  5.4 1.9 %collective-permute-start.5 = (s32[9,4]{1,0:T(8,128)S(1)}, s32[9,4]{1,0:T(8,128)S(1)}, u32[]{:S(2)}, u32[]{:S(2)}) collective-permute-start(s32[9,4]{1,0:T(8,128)S(1)} %add_add_fusion), channel_id=1, source_target_pairs={{1,34},{2,33},{3,36},{4,35},{5,38},{6,37},{7,40},{8,39},{9,42},{10... | collective-permute-start | bytes 440 | tf_op jit(solution)/shard_map/ppermute | solution.py:393
  7.3 0.9 %collective-permute-start.2 = (s32[9,4]{1,0:T(8,128)S(1)}, s32[9,4]{1,0:T(8,128)S(1)}, u32[]{:S(2)}, u32[]{:S(2)}) collective-permute-start(s32[9,4]{1,0:T(8,128)S(1)} %add_add_fusion), channel_id=1, source_target_pairs={{0,32},{1,33},{2,34},{3,35},{4,36},{5,37},{6,38},{7,39},{8,40},{9,... | collective-permute-start | bytes 440 | tf_op jit(solution)/shard_map/ppermute | solution.py:393
  8.2 1.2 %collective-permute-start.4 = (bf16[4,2,128,128]{3,2,1,0:T(8,128)(2,1)}, bf16[4,2,128,128]{3,2,1,0:T(8,128)(2,1)S(1)}, u32[]{:S(2)}, u32[]{:S(2)}) collective-permute-start(bf16[4,2,128,128]{3,2,1,0:T(8,128)(2,1)} %bitcast.19), channel_id=1, source_target_pairs={{0,32},{1,33},{2,34},{3,35},{4,36},{5,37},{6,38},{7,39},{8,40},{9,... | collective-permute-start | bytes 786440 | tf_op jit(solution)/shard_map/ppermute | solution.py:393
  9.5 2.5 %stage.1 = (bf16[512,512]{1,0:T(8,128)(2,1)S(1)}, bf16[8,256,512]{2,1,0:T(8,128)(2,1)S(1)}, bf16[8,512,256]{2,1,0:T(8,128)(2,1)S(1)}) custom-call(bf16[512,512]{1,0:T(8,128)(2,1)} %refs_0_.1, bf16[8,256,512]{2,1,0:T(8,128)(2,1)} %constant.33.clone.refs_1_, bf16[8,512,256]{2,1,0:T(8,128)(2,1)} %constant.34.clone.refs_2_), custom_call_target="tpu_custom_call" | custom-call | bytes 18874368 | tf_op jit(solution)/shard_map/stage/pallas_call | solution.py:135
  12.0 3.8 %collective-permute-start.3 = (s32[9,4]{1,0:T(8,128)S(1)}, s32[9,4]{1,0:T(8,128)S(1)}, u32[]{:S(2)}, u32[]{:S(2)}) collective-permute-start(s32[9,4]{1,0:T(8,128)S(1)} %add_add_fusion), channel_id=1, source_target_pairs={{0,33},{1,32},{2,35},{3,34},{4,37},{5,36},{6,39},{7,38},{8,41},{9,... | collective-permute-start | bytes 440 | tf_op jit(solution)/shard_map/ppermute | solution.py:393
  15.8 1.8 %forward_outer0.1 = bf16[2,2,128,256]{3,2,1,0:T(8,128)(2,1)S(1)} custom-call(s32[2]{0:T(128)S(1)} %pad_add_fusion.ctl, s32[9,4]{1,0:T(8,128)S(1)} %collective-permute-done.5.meta, bf16[512,512]{1,0:T(8,128)(2,1)S(1)} %get-tuple-element.30.refs_0_, bf16[512,512]{1,0:T(8,128)(2,1)S(1)} %collective-permute-done.refs_1_, ...), custom_call_target="tpu_custom_call" | custom-call | flops 1006632960 | bytes 1048576 | tf_op jit(solution)/shard_map/forward_outer0/pallas_call | solution.py:211
  18.3 1.6 %collective-permute-done.3.meta = s32[9,4]{1,0:T(8,128)S(1)} collective-permute-done((s32[9,4]{1,0:T(8,128)S(1)}, s32[9,4]{1,0:T(8,128)S(1)}, u32[]{:S(2)}, u32[]{:S(2)}) %collective-permute-start.3) | collective-permute-done | bytes 176 | tf_op jit(solution)/shard_map/ppermute | solution.py:393
  20.4 2.0 %collective-permute-start.9 = (bf16[2,2,128,256]{3,2,1,0:T(8,128)(2,1)S(1)}, bf16[2,2,128,256]{3,2,1,0:T(8,128)(2,1)S(1)}, u32[]{:S(2)}, u32[]{:S(2)}) collective-permute-start(bf16[2,2,128,256]{3,2,1,0:T(8,128)(2,1)S(1)} %forward_outer0.1), channel_id=1, source_target_pairs={{1,2},{2,1},{3,4},{4,3},{5,6},{6,5},{7,8},{8,7},{9,10},{10,9},{11,... | collective-permute-start | bytes 786440 | tf_op jit(solution)/shard_map/ppermute | solution.py:393
  22.4 5.0 %collective-permute-start.10 = (bf16[2,2,128,256]{3,2,1,0:T(8,128)(2,1)S(1)}, bf16[2,2,128,256]{3,2,1,0:T(8,128)(2,1)S(1)}, u32[]{:S(2)}, u32[]{:S(2)}) collective-permute-start(bf16[2,2,128,256]{3,2,1,0:T(8,128)(2,1)S(1)} %forward_outer2.1), channel_id=1, source_target_pairs={{1,2},{2,1},{3,4},{4,3},{5,6},{6,5},{7,8},{8,7},{9,10},{10,9},{11,... | collective-permute-start | bytes 786440 | tf_op jit(solution)/shard_map/ppermute | solution.py:393
  27.5 6.9 %forward_own0.1.mine = f32[4,2,128,256]{3,2,1,0:T(8,128)S(1)} custom-call(s32[2]{0:T(128)S(1)} %pad_add_fusion.ctl, s32[9,4]{1,0:T(8,128)S(1)} %collective-permute-done.2.meta, bf16[512,512]{1,0:T(8,128)(2,1)S(1)} %get-tuple-element.30.refs_0_, bf16[512,512]{1,0:T(8,128)(2,1)S(1)} %collective-permute-done.refs_1_, ...), custom_call_target="tpu_custom_call" | custom-call | flops 2013265920 | bytes 1048576 | tf_op jit(solution)/shard_map/forward_own0/pallas_call | solution.py:211
  35.1 2.8 %collective-permute-start.14 = (bf16[2,2,128,256]{3,2,1,0:T(8,128)(2,1)S(1)}, bf16[2,2,128,256]{3,2,1,0:T(8,128)(2,1)S(1)}, u32[]{:S(2)}, u32[]{:S(2)}) collective-permute-start(bf16[2,2,128,256]{3,2,1,0:T(8,128)(2,1)S(1)} %scale0.1.refs_0_), channel_id=1, source_target_pairs={{1,2},{2,1},{3,4},{4,3},{5,6},{6,5},{7,8},{8,7},{9,10},{10,9},{11,... | collective-permute-start | bytes 786440 | tf_op jit(solution)/shard_map/ppermute | solution.py:393
  38.8 1.4 %collective-permute-start.13 = (bf16[2,2,128,256]{3,2,1,0:T(8,128)(2,1)S(1)}, bf16[2,2,128,256]{3,2,1,0:T(8,128)(2,1)S(1)}, u32[]{:S(2)}, u32[]{:S(2)}) collective-permute-start(bf16[2,2,128,256]{3,2,1,0:T(8,128)(2,1)S(1)} %scale2.1.refs_1_), channel_id=1, source_target_pairs={{0,1},{1,0},{2,3},{3,2},{4,5},{5,4},{6,7},{7,6},{8,9},{9,8},{10,11... | collective-permute-start | bytes 786440 | tf_op jit(solution)/shard_map/ppermute | solution.py:393
  40.2 3.2 %collective-permute-start.11 = (bf16[2,2,128,256]{3,2,1,0:T(8,128)(2,1)S(1)}, bf16[2,2,128,256]{3,2,1,0:T(8,128)(2,1)S(1)}, u32[]{:S(2)}, u32[]{:S(2)}) collective-permute-start(bf16[2,2,128,256]{3,2,1,0:T(8,128)(2,1)S(1)} %scale2.1.refs_1_), channel_id=1, source_target_pairs={{1,2},{2,1},{3,4},{4,3},{5,6},{6,5},{7,8},{8,7},{9,10},{10,9},{11,... | collective-permute-start | bytes 786440 | tf_op jit(solution)/shard_map/ppermute | solution.py:393
  43.5 4.6 %adjoint_own0.1 = (f32[512,512]{1,0:T(8,128)S(1)}, f32[512,512]{1,0:T(8,128)S(1)}, f32[512,512]{1,0:T(8,128)S(1)}) custom-call(s32[2]{0:T(128)S(1)} %pad_add_fusion.ctl, s32[9,4]{1,0:T(8,128)S(1)} %collective-permute-done.2.meta, bf16[2,2,128,256]{3,2,1,0:T(8,128)(2,1)S(1)} %scale0.1.refs_0_, bf16[2,2,128,256]{3,2,1,0:T(8,128)(2,1)S(1)} %scale2.1.refs_1_, ...), custom_call_target="tpu_custom_call" | custom-call | flops 2013265920 | bytes 1048576 | tf_op jit(solution)/shard_map/adjoint_own0/pallas_call | solution.py:351
  48.1 2.1 %adjoint_outer0.1 = (f32[512,512]{1,0:T(8,128)S(1)}, f32[512,512]{1,0:T(8,128)S(1)}, f32[512,512]{1,0:T(8,128)S(1)}) custom-call(s32[2]{0:T(128)S(1)} %pad_add_fusion.ctl, s32[9,4]{1,0:T(8,128)S(1)} %collective-permute-done.5.meta, ...), custom_call_target="tpu_custom_call", output_to_operand_aliasing={{0}: (3, {}), {1}: (4, {}), {2}: (5, {})} | custom-call | flops 1006632960 | bytes 1048576 | tf_op jit(solution)/shard_map/adjoint_outer0/pallas_call | solution.py:351
  50.9 1.4 %collective-permute-done.11.refs_0_ = bf16[2,2,128,256]{3,2,1,0:T(8,128)(2,1)S(1)} collective-permute-done((bf16[2,2,128,256]{3,2,1,0:T(8,128)(2,1)S(1)}, bf16[2,2,128,256]{3,2,1,0:T(8,128)(2,1)S(1)}, u32[]{:S(2)}, u32[]{:S(2)}) %collective-permute-start.11) | collective-permute-done | bytes 262176 | tf_op jit(solution)/shard_map/ppermute | solution.py:393
  52.4 1.1 %adjoint_outer2.1 = (f32[512,512]{1,0:T(8,128)S(1)}, bf16[512,512]{1,0:T(8,128)(2,1)S(1)}, bf16[512,512]{1,0:T(8,128)(2,1)S(1)}) custom-call(s32[2]{0:T(128)S(1)} %pad_add_fusion.ctl, s32[9,4]{1,0:T(8,128)S(1)} %collective-permute-done.5.meta, bf16[2,2,128,256]{3,2,1,0:T(8,128)(2,1)S(1)} %collective-permute-done.11.refs_0_, ...), custom_call_target="tpu_custom_call", output_to_operand_aliasing={{0}: (3, {})} | custom-call | flops 1006632960 | bytes 1048576 | tf_op jit(solution)/shard_map/adjoint_outer2/pallas_call | solution.py:351
  53.4 5.9 %collective-permute-start.15 = (bf16[512,512]{1,0:T(8,128)(2,1)S(1)}, bf16[512,512]{1,0:T(8,128)(2,1)S(1)}, u32[]{:S(2)}, u32[]{:S(2)}) collective-permute-start(bf16[512,512]{1,0:T(8,128)(2,1)S(1)} %get-tuple-element.53), channel_id=1, source_target_pairs={{0,32},{1,33},{2,34},{3,35},{4,36},{5,37},{6,38},{7,39},{8,40},{9,... | collective-permute-start | bytes 1572872 | tf_op jit(solution)/shard_map/ppermute | solution.py:393
  59.4 1.3 %collective-permute-start.16 = (bf16[512,512]{1,0:T(8,128)(2,1)S(1)}, bf16[512,512]{1,0:T(8,128)(2,1)S(1)}, u32[]{:S(2)}, u32[]{:S(2)}) collective-permute-start(bf16[512,512]{1,0:T(8,128)(2,1)S(1)} %get-tuple-element.54), channel_id=1, source_target_pairs={{0,64},{1,65},{2,66},{3,67},{4,68},{5,69},{6,70},{7,71},{8,72},{9,... | collective-permute-start | bytes 1572872 | tf_op jit(solution)/shard_map/ppermute | solution.py:393
  60.7 10.3 %collective-permute-done.15 = bf16[512,512]{1,0:T(8,128)(2,1)S(1)} collective-permute-done((bf16[512,512]{1,0:T(8,128)(2,1)S(1)}, bf16[512,512]{1,0:T(8,128)(2,1)S(1)}, u32[]{:S(2)}, u32[]{:S(2)}) %collective-permute-start.15) | collective-permute-done | bytes 524320 | tf_op jit(solution)/shard_map/ppermute | solution.py:393
  70.9 4.5 %collective-permute-done.16 = bf16[512,512]{1,0:T(8,128)(2,1)S(1)} collective-permute-done((bf16[512,512]{1,0:T(8,128)(2,1)S(1)}, bf16[512,512]{1,0:T(8,128)(2,1)S(1)}, u32[]{:S(2)}, u32[]{:S(2)}) %collective-permute-start.16) | collective-permute-done | bytes 524320 | tf_op jit(solution)/shard_map/ppermute | solution.py:393
  75.5 1.2 %convert_add_fusion = f32[512,512]{1,0:T(8,128)} fusion(bf16[512,512]{1,0:T(8,128)(2,1)S(1)} %collective-permute-done.16, f32[512,512]{1,0:T(8,128)S(1)} %get-tuple-element.52, bf16[512,512]{1,0:T(8,128)(2,1)S(1)} %collective-permute-done.15), kind=kLoop, calls=%fused_computation | loop fusion | flops 1048576 | bytes 3145728 | tf_op jit(solution)/shard_map/add | solution.py:435
  (26 shorter events, 4.5 us)
Async XLA Ops:
  0.0 15.7 %collective-permute-start = (bf16[512,512]{1,0:T(8,128)(2,1)}, bf16[512,512]{1,0:T(8,128)(2,1)S(1)}, u32[]{:S(2)}, u32[]{:S(2)}) collective-permute-start(bf16[512,512]{1,0:T(8,128)(2,1)} %refs_0_.1), channel_id=1, source_target_pairs={{0,32},{1,33},{2,34},{3,35},{4,36},{5,37},{6,38},{7,39},{8,40},{9,... | collective-permute-start | bytes 1572872 | tf_op jit(solution)/shard_map/ppermute | solution.py:393
  1.2 14.6 %collective-permute-start.1 = (bf16[512,512]{1,0:T(8,128)(2,1)}, bf16[512,512]{1,0:T(8,128)(2,1)S(1)}, u32[]{:S(2)}, u32[]{:S(2)}) collective-permute-start(bf16[512,512]{1,0:T(8,128)(2,1)} %refs_0_.1), channel_id=1, source_target_pairs={{32,96},{33,97},{34,98},{35,99},{36,100},{37,101},{38,102},{39,103... | collective-permute-start | bytes 1572872 | tf_op jit(solution)/shard_map/ppermute | solution.py:393
  5.4 6.6 %collective-permute-start.5 = (s32[9,4]{1,0:T(8,128)S(1)}, s32[9,4]{1,0:T(8,128)S(1)}, u32[]{:S(2)}, u32[]{:S(2)}) collective-permute-start(s32[9,4]{1,0:T(8,128)S(1)} %add_add_fusion), channel_id=1, source_target_pairs={{1,34},{2,33},{3,36},{4,35},{5,38},{6,37},{7,40},{8,39},{9,42},{10... | collective-permute-start | bytes 440 | tf_op jit(solution)/shard_map/ppermute | solution.py:393
  7.3 11.0 %collective-permute-start.2 = (s32[9,4]{1,0:T(8,128)S(1)}, s32[9,4]{1,0:T(8,128)S(1)}, u32[]{:S(2)}, u32[]{:S(2)}) collective-permute-start(s32[9,4]{1,0:T(8,128)S(1)} %add_add_fusion), channel_id=1, source_target_pairs={{0,32},{1,33},{2,34},{3,35},{4,36},{5,37},{6,38},{7,39},{8,40},{9,... | collective-permute-start | bytes 440 | tf_op jit(solution)/shard_map/ppermute | solution.py:393
  8.2 11.6 %collective-permute-start.4 = (bf16[4,2,128,128]{3,2,1,0:T(8,128)(2,1)}, bf16[4,2,128,128]{3,2,1,0:T(8,128)(2,1)S(1)}, u32[]{:S(2)}, u32[]{:S(2)}) collective-permute-start(bf16[4,2,128,128]{3,2,1,0:T(8,128)(2,1)} %bitcast.19), channel_id=1, source_target_pairs={{0,32},{1,33},{2,34},{3,35},{4,36},{5,37},{6,38},{7,39},{8,40},{9,... | collective-permute-start | bytes 786440 | tf_op jit(solution)/shard_map/ppermute | solution.py:393
  9.5 6.3 %copy-start = (bf16[512,512]{1,0:T(8,128)(2,1)S(1)}, bf16[512,512]{1,0:T(8,128)(2,1)}, u32[]{:S(2)}) copy-start(bf16[512,512]{1,0:T(8,128)(2,1)} %refs_0_.1) | copy-start | bytes 1572868
  12.0 7.9 %collective-permute-start.3 = (s32[9,4]{1,0:T(8,128)S(1)}, s32[9,4]{1,0:T(8,128)S(1)}, u32[]{:S(2)}, u32[]{:S(2)}) collective-permute-start(s32[9,4]{1,0:T(8,128)S(1)} %add_add_fusion), channel_id=1, source_target_pairs={{0,33},{1,32},{2,35},{3,34},{4,37},{5,36},{6,39},{7,38},{8,41},{9,... | collective-permute-start | bytes 440 | tf_op jit(solution)/shard_map/ppermute | solution.py:393
  15.7 11.7 %collective-permute-start.6 = (bf16[512,512]{1,0:T(8,128)(2,1)S(1)}, bf16[512,512]{1,0:T(8,128)(2,1)S(1)}, u32[]{:S(2)}, u32[]{:S(2)}) collective-permute-start(bf16[512,512]{1,0:T(8,128)(2,1)S(1)} %copy-done), channel_id=1, source_target_pairs={{0,1},{1,0},{2,3},{3,2},{4,5},{5,4},{6,7},{7,6},{8,9},{9,8},{10,11... | collective-permute-start | bytes 1572872 | tf_op jit(solution)/shard_map/ppermute | solution.py:393
  19.8 7.6 %collective-permute-start.7 = (bf16[512,512]{1,0:T(8,128)(2,1)S(1)}, bf16[512,512]{1,0:T(8,128)(2,1)S(1)}, u32[]{:S(2)}, u32[]{:S(2)}) collective-permute-start(bf16[512,512]{1,0:T(8,128)(2,1)S(1)} %collective-permute-done.refs_1_), channel_id=1, source_target_pairs={{0,1},{1,0},{2,3},{3,2},{4,5},{5,4},{6,7},{7,6},{8,9},{9,8},{10,11... | collective-permute-start | bytes 1572872 | tf_op jit(solution)/shard_map/ppermute | solution.py:393
  19.9 7.6 %collective-permute-start.8 = (bf16[512,512]{1,0:T(8,128)(2,1)S(1)}, bf16[512,512]{1,0:T(8,128)(2,1)S(1)}, u32[]{:S(2)}, u32[]{:S(2)}) collective-permute-start(bf16[512,512]{1,0:T(8,128)(2,1)S(1)} %collective-permute-done.1.refs_2_), channel_id=1, source_target_pairs={{0,1},{1,0},{2,3},{3,2},{4,5},{5,4},{6,7},{7,6},{8,9},{9,8},{10,11... | collective-permute-start | bytes 1572872 | tf_op jit(solution)/shard_map/ppermute | solution.py:393
  20.4 14.0 %collective-permute-start.9 = (bf16[2,2,128,256]{3,2,1,0:T(8,128)(2,1)S(1)}, bf16[2,2,128,256]{3,2,1,0:T(8,128)(2,1)S(1)}, u32[]{:S(2)}, u32[]{:S(2)}) collective-permute-start(bf16[2,2,128,256]{3,2,1,0:T(8,128)(2,1)S(1)} %forward_outer0.1), channel_id=1, source_target_pairs={{1,2},{2,1},{3,4},{4,3},{5,6},{6,5},{7,8},{8,7},{9,10},{10,9},{11,... | collective-permute-start | bytes 786440 | tf_op jit(solution)/shard_map/ppermute | solution.py:393
  22.4 15.6 %collective-permute-start.10 = (bf16[2,2,128,256]{3,2,1,0:T(8,128)(2,1)S(1)}, bf16[2,2,128,256]{3,2,1,0:T(8,128)(2,1)S(1)}, u32[]{:S(2)}, u32[]{:S(2)}) collective-permute-start(bf16[2,2,128,256]{3,2,1,0:T(8,128)(2,1)S(1)} %forward_outer2.1), channel_id=1, source_target_pairs={{1,2},{2,1},{3,4},{4,3},{5,6},{6,5},{7,8},{8,7},{9,10},{10,9},{11,... | collective-permute-start | bytes 786440 | tf_op jit(solution)/shard_map/ppermute | solution.py:393
  35.1 12.9 %collective-permute-start.14 = (bf16[2,2,128,256]{3,2,1,0:T(8,128)(2,1)S(1)}, bf16[2,2,128,256]{3,2,1,0:T(8,128)(2,1)S(1)}, u32[]{:S(2)}, u32[]{:S(2)}) collective-permute-start(bf16[2,2,128,256]{3,2,1,0:T(8,128)(2,1)S(1)} %scale0.1.refs_0_), channel_id=1, source_target_pairs={{1,2},{2,1},{3,4},{4,3},{5,6},{6,5},{7,8},{8,7},{9,10},{10,9},{11,... | collective-permute-start | bytes 786440 | tf_op jit(solution)/shard_map/ppermute | solution.py:393
  38.8 11.4 %collective-permute-start.13 = (bf16[2,2,128,256]{3,2,1,0:T(8,128)(2,1)S(1)}, bf16[2,2,128,256]{3,2,1,0:T(8,128)(2,1)S(1)}, u32[]{:S(2)}, u32[]{:S(2)}) collective-permute-start(bf16[2,2,128,256]{3,2,1,0:T(8,128)(2,1)S(1)} %scale2.1.refs_1_), channel_id=1, source_target_pairs={{0,1},{1,0},{2,3},{3,2},{4,5},{5,4},{6,7},{7,6},{8,9},{9,8},{10,11... | collective-permute-start | bytes 786440 | tf_op jit(solution)/shard_map/ppermute | solution.py:393
  40.1 10.1 %collective-permute-start.12 = (bf16[2,2,128,256]{3,2,1,0:T(8,128)(2,1)S(1)}, bf16[2,2,128,256]{3,2,1,0:T(8,128)(2,1)S(1)}, u32[]{:S(2)}, u32[]{:S(2)}) collective-permute-start(bf16[2,2,128,256]{3,2,1,0:T(8,128)(2,1)S(1)} %scale0.1.refs_0_), channel_id=1, source_target_pairs={{0,1},{1,0},{2,3},{3,2},{4,5},{5,4},{6,7},{7,6},{8,9},{9,8},{10,11... | collective-permute-start | bytes 786440 | tf_op jit(solution)/shard_map/ppermute | solution.py:393
  40.2 12.1 %collective-permute-start.11 = (bf16[2,2,128,256]{3,2,1,0:T(8,128)(2,1)S(1)}, bf16[2,2,128,256]{3,2,1,0:T(8,128)(2,1)S(1)}, u32[]{:S(2)}, u32[]{:S(2)}) collective-permute-start(bf16[2,2,128,256]{3,2,1,0:T(8,128)(2,1)S(1)} %scale2.1.refs_1_), channel_id=1, source_target_pairs={{1,2},{2,1},{3,4},{4,3},{5,6},{6,5},{7,8},{8,7},{9,10},{10,9},{11,... | collective-permute-start | bytes 786440 | tf_op jit(solution)/shard_map/ppermute | solution.py:393
  53.4 17.5 %collective-permute-start.15 = (bf16[512,512]{1,0:T(8,128)(2,1)S(1)}, bf16[512,512]{1,0:T(8,128)(2,1)S(1)}, u32[]{:S(2)}, u32[]{:S(2)}) collective-permute-start(bf16[512,512]{1,0:T(8,128)(2,1)S(1)} %get-tuple-element.53), channel_id=1, source_target_pairs={{0,32},{1,33},{2,34},{3,35},{4,36},{5,37},{6,38},{7,39},{8,40},{9,... | collective-permute-start | bytes 1572872 | tf_op jit(solution)/shard_map/ppermute | solution.py:393
  59.4 16.1 %collective-permute-start.16 = (bf16[512,512]{1,0:T(8,128)(2,1)S(1)}, bf16[512,512]{1,0:T(8,128)(2,1)S(1)}, u32[]{:S(2)}, u32[]{:S(2)}) collective-permute-start(bf16[512,512]{1,0:T(8,128)(2,1)S(1)} %get-tuple-element.54), channel_id=1, source_target_pairs={{0,64},{1,65},{2,66},{3,67},{4,68},{5,69},{6,70},{7,71},{8,72},{9,... | collective-permute-start | bytes 1572872 | tf_op jit(solution)/shard_map/ppermute | solution.py:393

commit v7 on v6

--- a/solution.py
+++ b/solution.py
@@ -228,7 +228,7 @@
         def pointing(s, carry):
             def uv(k, c):
                 w = weight[s, k].astype(f32)
-                v = mine[s, k] + outer[s - begin, k].astype(f32)
+                v = mine[s, k] + outer[s, k].astype(f32)
                 out[s - begin, k, :, :UVB] = (v[:, :UVB] * w).astype(bf16)
                 out[s - begin, k, :, UVB:] = (v[:, UVB:] * w).astype(bf16)
                 return c
@@ -411,19 +411,17 @@
         skies = (own_sky, pair_sky, far_sky)
         meta_near = send(meta, "row_pair_near")
         chunks = tuple(range(0, SLOTS, CHUNK))
-        from_outer = []
-        for begin in chunks:
-            v_outer = forward("outer", (begin, begin + CHUNK), ctl, meta_outer, [skies], stacked, flipped)
-            from_outer.append(send(v_outer, "outer"))
-            meta_outer, v_outer = lax.optimization_barrier((meta_outer, v_outer))
+        v_outer = forward("outer", (0, SLOTS), ctl, meta_outer, [skies], stacked, flipped)
+        from_outer = send(v_outer, "outer")
+        meta_outer, v_outer = lax.optimization_barrier((meta_outer, v_outer))
         pair_sky, far_sky, meta_own, meta_near, weight, meta_outer = lax.optimization_barrier(
             (pair_sky, far_sky, meta_own, meta_near, weight, meta_outer)
         )
         near_skies = [send(x, "near") for x in (sky, pair_sky, far_sky)]
         v_own = forward("own", (0, SLOTS), ctl, meta_own, [skies, near_skies], stacked, flipped)
         scaled = []
-        for begin, part in zip(chunks, from_outer):
-            scaled.append(scale(begin, meta_own, v_own, part, weight))
+        for begin in chunks:
+            scaled.append(scale(begin, meta_own, v_own, from_outer, weight))
             meta_own, _ = lax.optimization_barrier((meta_own, scaled[-1]))
         scaled_outer = [send(x, "outer") for x in scaled]
         scaled_near = [send(x, "near") for x in scaled]

time: 76.9 us -> 77.3 us (level)
  the two profiles are of different devices: /device:TPU:124 before, /device:TPU:61 now
where the time goes in v7:
time: 77.3 us
  starting transfers between devices  30 us (39%)
  Pallas kernels  23.6 us (31%)
  waiting for transfers between devices  20.6 us (27%)
  other arithmetic  2.04 us (3%)
  between operations  0.88 us (1%)
    ppermute x16, starting transfers between devices, send(): return lax.ppermute(x, ('ty', 'tx'), moves[what])  30 us
    ppermute x16, waiting for transfers between devices, send(): return lax.ppermute(x, ('ty', 'tx'), moves[what])  20.6 us
    pallas_call x4, Pallas kernels, adjoint(): pl.pallas_call(kernel, out_shape=[pltpu.VMEM((TILE, TILE), kept) for kept...  10.5 us
    pallas_call x2, Pallas kernels, forward(): pl.pallas_call(kernel, out_shape=pltpu.VMEM(shape, f32 if kind == 'own' e...  9.23 us
    pallas_call x1, Pallas kernels, stage(): pl.pallas_call(kernel, out_shape=[pltpu.VMEM(x.shape, bf16) for x in arra...  2.46 us
  transfers between devices with their start and end apart: 16, of which 3 were waited for; matrix products, arithmetic and copies ran while one was open for 1% of the time, Pallas kernels for 25%

profile of v7, /device:TPU:61, one launch (start us, length us, event | category | flops | bytes accessed | tf_op | source)
XLA Modules:
  0.0 77.3 jit_solution(13701531351552839109)
XLA Ops:
  0.0 0.9 %collective-permute-start = (bf16[512,512]{1,0:T(8,128)(2,1)}, bf16[512,512]{1,0:T(8,128)(2,1)S(1)}, u32[]{:S(2)}, u32[]{:S(2)}) collective-permute-start(bf16[512,512]{1,0:T(8,128)(2,1)} %refs_0_.1), channel_id=1, source_target_pairs={{0,32},{1,33},{2,34},{3,35},{4,36},{5,37},{6,38},{7,39},{8,40},{9,... | collective-permute-start | bytes 1572872 | tf_op jit(solution)/shard_map/ppermute | solution.py:393
  0.9 2.4 %collective-permute-start.1 = (bf16[512,512]{1,0:T(8,128)(2,1)}, bf16[512,512]{1,0:T(8,128)(2,1)S(1)}, u32[]{:S(2)}, u32[]{:S(2)}) collective-permute-start(bf16[512,512]{1,0:T(8,128)(2,1)} %refs_0_.1), channel_id=1, source_target_pairs={{32,96},{33,97},{34,98},{35,99},{36,100},{37,101},{38,102},{39,103... | collective-permute-start | bytes 1572872 | tf_op jit(solution)/shard_map/ppermute | solution.py:393
  4.1 0.8 %add_add_fusion = s32[9,4]{1,0:T(8,128)S(1)} fusion(s32[1,4]{1,0:T(1,128)} %bitcast.17, s32[4,4]{1,0:T(4,128)} %bitcast.15, s32[2,4]{1,0:T(2,128)} %bitcast.16, s32[9]{0:T(128)S(1)} %pad.30, bf16[1,4]{1,0:T(2,128)(2,1)} %bitcast.18), kind=kLoop, calls=%fused_computation.1 | loop fusion | flops 180 | bytes 300 | tf_op jit(solution)/shard_map/add | solution.py:404
  4.9 5.4 %collective-permute-start.5 = (s32[9,4]{1,0:T(8,128)S(1)}, s32[9,4]{1,0:T(8,128)S(1)}, u32[]{:S(2)}, u32[]{:S(2)}) collective-permute-start(s32[9,4]{1,0:T(8,128)S(1)} %add_add_fusion), channel_id=1, source_target_pairs={{1,34},{2,33},{3,36},{4,35},{5,38},{6,37},{7,40},{8,39},{9,42},{10... | collective-permute-start | bytes 440 | tf_op jit(solution)/shard_map/ppermute | solution.py:393
  10.9 2.5 %stage.1 = (bf16[512,512]{1,0:T(8,128)(2,1)S(1)}, bf16[8,256,512]{2,1,0:T(8,128)(2,1)S(1)}, bf16[8,512,256]{2,1,0:T(8,128)(2,1)S(1)}) custom-call(bf16[512,512]{1,0:T(8,128)(2,1)} %refs_0_.1, bf16[8,256,512]{2,1,0:T(8,128)(2,1)} %constant.33.clone.refs_1_, bf16[8,512,256]{2,1,0:T(8,128)(2,1)} %constant.34.clone.refs_2_), custom_call_target="tpu_custom_call" | custom-call | bytes 18874368 | tf_op jit(solution)/shard_map/stage/pallas_call | solution.py:135
  13.4 0.6 collective-permute-start.3
  14.0 1.7 %collective-permute-start.6 = (bf16[512,512]{1,0:T(8,128)(2,1)S(1)}, bf16[512,512]{1,0:T(8,128)(2,1)S(1)}, u32[]{:S(2)}, u32[]{:S(2)}) collective-permute-start(bf16[512,512]{1,0:T(8,128)(2,1)S(1)} %copy-done), channel_id=1, source_target_pairs={{0,1},{1,0},{2,3},{3,2},{4,5},{5,4},{6,7},{7,6},{8,9},{9,8},{10,11... | collective-permute-start | bytes 1572872 | tf_op jit(solution)/shard_map/ppermute | solution.py:393
  15.7 4.6 %forward_outer0.1 = bf16[4,2,128,256]{3,2,1,0:T(8,128)(2,1)S(1)} custom-call(s32[2]{0:T(128)S(1)} %pad_add_fusion.ctl, s32[9,4]{1,0:T(8,128)S(1)} %collective-permute-done.5.meta, bf16[512,512]{1,0:T(8,128)(2,1)S(1)} %get-tuple-element.29.refs_0_, bf16[512,512]{1,0:T(8,128)(2,1)S(1)} %collective-permute-done.refs_1_, ...), custom_call_target="tpu_custom_call" | custom-call | flops 1006632960 | bytes 1048576 | tf_op jit(solution)/shard_map/forward_outer0/pallas_call | solution.py:211
  21.0 3.3 %collective-permute-start.9 = (bf16[4,2,128,256]{3,2,1,0:T(8,128)(2,1)S(1)}, bf16[4,2,128,256]{3,2,1,0:T(8,128)(2,1)S(1)}, u32[]{:S(2)}, u32[]{:S(2)}) collective-permute-start(bf16[4,2,128,256]{3,2,1,0:T(8,128)(2,1)S(1)} %forward_outer0.1), channel_id=1, source_target_pairs={{1,2},{2,1},{3,4},{4,3},{5,6},{6,5},{7,8},{8,7},{9,10},{10,9},{11,... | collective-permute-start | bytes 1572872 | tf_op jit(solution)/shard_map/ppermute | solution.py:393
  24.4 4.6 %forward_own0.1.mine = f32[4,2,128,256]{3,2,1,0:T(8,128)S(1)} custom-call(s32[2]{0:T(128)S(1)} %pad_add_fusion.ctl, s32[9,4]{1,0:T(8,128)S(1)} %collective-permute-done.2.meta, bf16[512,512]{1,0:T(8,128)(2,1)S(1)} %get-tuple-element.29.refs_0_, bf16[512,512]{1,0:T(8,128)(2,1)S(1)} %collective-permute-done.refs_1_, ...), custom_call_target="tpu_custom_call" | custom-call | flops 2013265920 | bytes 1048576 | tf_op jit(solution)/shard_map/forward_own0/pallas_call | solution.py:211
  28.9 5.0 %collective-permute-done.9.outer = bf16[4,2,128,256]{3,2,1,0:T(8,128)(2,1)S(1)} collective-permute-done((bf16[4,2,128,256]{3,2,1,0:T(8,128)(2,1)S(1)}, bf16[4,2,128,256]{3,2,1,0:T(8,128)(2,1)S(1)}, u32[]{:S(2)}, u32[]{:S(2)}) %collective-permute-start.9) | collective-permute-done | bytes 524320 | tf_op jit(solution)/shard_map/ppermute | solution.py:393
  34.0 0.7 scale0.1.refs_0_
  34.7 3.4 %collective-permute-start.13 = (bf16[2,2,128,256]{3,2,1,0:T(8,128)(2,1)S(1)}, bf16[2,2,128,256]{3,2,1,0:T(8,128)(2,1)S(1)}, u32[]{:S(2)}, u32[]{:S(2)}) collective-permute-start(bf16[2,2,128,256]{3,2,1,0:T(8,128)(2,1)S(1)} %scale0.1.refs_0_), channel_id=1, source_target_pairs={{1,2},{2,1},{3,4},{4,3},{5,6},{6,5},{7,8},{8,7},{9,10},{10,9},{11,... | collective-permute-start | bytes 786440 | tf_op jit(solution)/shard_map/ppermute | solution.py:393
  38.1 0.7 scale2.1.refs_1_
  38.8 3.4 %collective-permute-start.12 = (bf16[2,2,128,256]{3,2,1,0:T(8,128)(2,1)S(1)}, bf16[2,2,128,256]{3,2,1,0:T(8,128)(2,1)S(1)}, u32[]{:S(2)}, u32[]{:S(2)}) collective-permute-start(bf16[2,2,128,256]{3,2,1,0:T(8,128)(2,1)S(1)} %scale2.1.refs_1_), channel_id=1, source_target_pairs={{0,1},{1,0},{2,3},{3,2},{4,5},{5,4},{6,7},{7,6},{8,9},{9,8},{10,11... | collective-permute-start | bytes 786440 | tf_op jit(solution)/shard_map/ppermute | solution.py:393
  42.4 6.2 %collective-permute-start.10 = (bf16[2,2,128,256]{3,2,1,0:T(8,128)(2,1)S(1)}, bf16[2,2,128,256]{3,2,1,0:T(8,128)(2,1)S(1)}, u32[]{:S(2)}, u32[]{:S(2)}) collective-permute-start(bf16[2,2,128,256]{3,2,1,0:T(8,128)(2,1)S(1)} %scale2.1.refs_1_), channel_id=1, source_target_pairs={{1,2},{2,1},{3,4},{4,3},{5,6},{6,5},{7,8},{8,7},{9,10},{10,9},{11,... | collective-permute-start | bytes 786440 | tf_op jit(solution)/shard_map/ppermute | solution.py:393
  48.6 3.4 %adjoint_own0.1 = (f32[512,512]{1,0:T(8,128)S(1)}, f32[512,512]{1,0:T(8,128)S(1)}, f32[512,512]{1,0:T(8,128)S(1)}) custom-call(s32[2]{0:T(128)S(1)} %pad_add_fusion.ctl, s32[9,4]{1,0:T(8,128)S(1)} %collective-permute-done.2.meta, bf16[2,2,128,256]{3,2,1,0:T(8,128)(2,1)S(1)} %scale0.1.refs_0_, bf16[2,2,128,256]{3,2,1,0:T(8,128)(2,1)S(1)} %scale2.1.refs_1_, ...), custom_call_target="tpu_custom_call" | custom-call | flops 2013265920 | bytes 1048576 | tf_op jit(solution)/shard_map/adjoint_own0/pallas_call | solution.py:351
  52.0 2.9 %adjoint_outer0.1 = (f32[512,512]{1,0:T(8,128)S(1)}, f32[512,512]{1,0:T(8,128)S(1)}, f32[512,512]{1,0:T(8,128)S(1)}) custom-call(s32[2]{0:T(128)S(1)} %pad_add_fusion.ctl, s32[9,4]{1,0:T(8,128)S(1)} %collective-permute-done.5.meta, ...), custom_call_target="tpu_custom_call", output_to_operand_aliasing={{0}: (3, {}), {1}: (4, {}), {2}: (5, {})} | custom-call | flops 1006632960 | bytes 1048576 | tf_op jit(solution)/shard_map/adjoint_outer0/pallas_call | solution.py:351
  54.9 0.7 adjoint_near0.1
  55.6 3.5 %adjoint_outer2.1 = (f32[512,512]{1,0:T(8,128)S(1)}, bf16[512,512]{1,0:T(8,128)(2,1)S(1)}, bf16[512,512]{1,0:T(8,128)(2,1)S(1)}) custom-call(s32[2]{0:T(128)S(1)} %pad_add_fusion.ctl, s32[9,4]{1,0:T(8,128)S(1)} %collective-permute-done.5.meta, bf16[2,2,128,256]{3,2,1,0:T(8,128)(2,1)S(1)} %collective-permute-done.10.refs_0_, ...), custom_call_target="tpu_custom_call", output_to_operand_aliasing={{0}: (3, {})} | custom-call | flops 1006632960 | bytes 1048576 | tf_op jit(solution)/shard_map/adjoint_outer2/pallas_call | solution.py:351
  59.2 1.3 %collective-permute-start.15 = (bf16[512,512]{1,0:T(8,128)(2,1)S(1)}, bf16[512,512]{1,0:T(8,128)(2,1)S(1)}, u32[]{:S(2)}, u32[]{:S(2)}) collective-permute-start(bf16[512,512]{1,0:T(8,128)(2,1)S(1)} %get-tuple-element.52), channel_id=1, source_target_pairs={{0,64},{1,65},{2,66},{3,67},{4,68},{5,69},{6,70},{7,71},{8,72},{9,... | collective-permute-start | bytes 1572872 | tf_op jit(solution)/shard_map/ppermute | solution.py:393
  60.5 12.5 %collective-permute-done.14 = bf16[512,512]{1,0:T(8,128)(2,1)S(1)} collective-permute-done((bf16[512,512]{1,0:T(8,128)(2,1)S(1)}, bf16[512,512]{1,0:T(8,128)(2,1)S(1)}, u32[]{:S(2)}, u32[]{:S(2)}) %collective-permute-start.14) | collective-permute-done | bytes 524320 | tf_op jit(solution)/shard_map/ppermute | solution.py:393
  73.1 3.0 %collective-permute-done.15 = bf16[512,512]{1,0:T(8,128)(2,1)S(1)} collective-permute-done((bf16[512,512]{1,0:T(8,128)(2,1)S(1)}, bf16[512,512]{1,0:T(8,128)(2,1)S(1)}, u32[]{:S(2)}, u32[]{:S(2)}) %collective-permute-start.15) | collective-permute-done | bytes 524320 | tf_op jit(solution)/shard_map/ppermute | solution.py:393
  76.1 1.2 %convert_add_fusion = f32[512,512]{1,0:T(8,128)} fusion(bf16[512,512]{1,0:T(8,128)(2,1)S(1)} %collective-permute-done.15, f32[512,512]{1,0:T(8,128)S(1)} %get-tuple-element.50, bf16[512,512]{1,0:T(8,128)(2,1)S(1)} %collective-permute-done.14), kind=kLoop, calls=%fused_computation | loop fusion | flops 1048576 | bytes 3145728 | tf_op jit(solution)/shard_map/add | solution.py:433
  (23 shorter events, 1.5 us)
Async XLA Ops:
  0.0 14.0 %collective-permute-start = (bf16[512,512]{1,0:T(8,128)(2,1)}, bf16[512,512]{1,0:T(8,128)(2,1)S(1)}, u32[]{:S(2)}, u32[]{:S(2)}) collective-permute-start(bf16[512,512]{1,0:T(8,128)(2,1)} %refs_0_.1), channel_id=1, source_target_pairs={{0,32},{1,33},{2,34},{3,35},{4,36},{5,37},{6,38},{7,39},{8,40},{9,... | collective-permute-start | bytes 1572872 | tf_op jit(solution)/shard_map/ppermute | solution.py:393
  0.9 14.8 %collective-permute-start.1 = (bf16[512,512]{1,0:T(8,128)(2,1)}, bf16[512,512]{1,0:T(8,128)(2,1)S(1)}, u32[]{:S(2)}, u32[]{:S(2)}) collective-permute-start(bf16[512,512]{1,0:T(8,128)(2,1)} %refs_0_.1), channel_id=1, source_target_pairs={{32,96},{33,97},{34,98},{35,99},{36,100},{37,101},{38,102},{39,103... | collective-permute-start | bytes 1572872 | tf_op jit(solution)/shard_map/ppermute | solution.py:393
  3.3 17.1 %collective-permute-start.4 = (bf16[4,2,128,128]{3,2,1,0:T(8,128)(2,1)}, bf16[4,2,128,128]{3,2,1,0:T(8,128)(2,1)S(1)}, u32[]{:S(2)}, u32[]{:S(2)}) collective-permute-start(bf16[4,2,128,128]{3,2,1,0:T(8,128)(2,1)} %bitcast.19), channel_id=1, source_target_pairs={{0,32},{1,33},{2,34},{3,35},{4,36},{5,37},{6,38},{7,39},{8,40},{9,... | collective-permute-start | bytes 786440 | tf_op jit(solution)/shard_map/ppermute | solution.py:393
  4.9 8.4 %collective-permute-start.5 = (s32[9,4]{1,0:T(8,128)S(1)}, s32[9,4]{1,0:T(8,128)S(1)}, u32[]{:S(2)}, u32[]{:S(2)}) collective-permute-start(s32[9,4]{1,0:T(8,128)S(1)} %add_add_fusion), channel_id=1, source_target_pairs={{1,34},{2,33},{3,36},{4,35},{5,38},{6,37},{7,40},{8,39},{9,42},{10... | collective-permute-start | bytes 440 | tf_op jit(solution)/shard_map/ppermute | solution.py:393
  10.4 10.0 %collective-permute-start.2 = (s32[9,4]{1,0:T(8,128)S(1)}, s32[9,4]{1,0:T(8,128)S(1)}, u32[]{:S(2)}, u32[]{:S(2)}) collective-permute-start(s32[9,4]{1,0:T(8,128)S(1)} %add_add_fusion), channel_id=1, source_target_pairs={{0,32},{1,33},{2,34},{3,35},{4,36},{5,37},{6,38},{7,39},{8,40},{9,... | collective-permute-start | bytes 440 | tf_op jit(solution)/shard_map/ppermute | solution.py:393
  10.9 3.1 %copy-start = (bf16[512,512]{1,0:T(8,128)(2,1)S(1)}, bf16[512,512]{1,0:T(8,128)(2,1)}, u32[]{:S(2)}) copy-start(bf16[512,512]{1,0:T(8,128)(2,1)} %refs_0_.1) | copy-start | bytes 1572868
  13.4 7.0 %collective-permute-start.3 = (s32[9,4]{1,0:T(8,128)S(1)}, s32[9,4]{1,0:T(8,128)S(1)}, u32[]{:S(2)}, u32[]{:S(2)}) collective-permute-start(s32[9,4]{1,0:T(8,128)S(1)} %add_add_fusion), channel_id=1, source_target_pairs={{0,33},{1,32},{2,35},{3,34},{4,37},{5,36},{6,39},{7,38},{8,41},{9,... | collective-permute-start | bytes 440 | tf_op jit(solution)/shard_map/ppermute | solution.py:393
  14.0 10.4 %collective-permute-start.6 = (bf16[512,512]{1,0:T(8,128)(2,1)S(1)}, bf16[512,512]{1,0:T(8,128)(2,1)S(1)}, u32[]{:S(2)}, u32[]{:S(2)}) collective-permute-start(bf16[512,512]{1,0:T(8,128)(2,1)S(1)} %copy-done), channel_id=1, source_target_pairs={{0,1},{1,0},{2,3},{3,2},{4,5},{5,4},{6,7},{7,6},{8,9},{9,8},{10,11... | collective-permute-start | bytes 1572872 | tf_op jit(solution)/shard_map/ppermute | solution.py:393
  20.4 3.9 %collective-permute-start.7 = (bf16[512,512]{1,0:T(8,128)(2,1)S(1)}, bf16[512,512]{1,0:T(8,128)(2,1)S(1)}, u32[]{:S(2)}, u32[]{:S(2)}) collective-permute-start(bf16[512,512]{1,0:T(8,128)(2,1)S(1)} %collective-permute-done.refs_1_), channel_id=1, source_target_pairs={{0,1},{1,0},{2,3},{3,2},{4,5},{5,4},{6,7},{7,6},{8,9},{9,8},{10,11... | collective-permute-start | bytes 1572872 | tf_op jit(solution)/shard_map/ppermute | solution.py:393
  20.5 3.9 %collective-permute-start.8 = (bf16[512,512]{1,0:T(8,128)(2,1)S(1)}, bf16[512,512]{1,0:T(8,128)(2,1)S(1)}, u32[]{:S(2)}, u32[]{:S(2)}) collective-permute-start(bf16[512,512]{1,0:T(8,128)(2,1)S(1)} %collective-permute-done.1.refs_2_), channel_id=1, source_target_pairs={{0,1},{1,0},{2,3},{3,2},{4,5},{5,4},{6,7},{7,6},{8,9},{9,8},{10,11... | collective-permute-start | bytes 1572872 | tf_op jit(solution)/shard_map/ppermute | solution.py:393
  21.0 13.0 %collective-permute-start.9 = (bf16[4,2,128,256]{3,2,1,0:T(8,128)(2,1)S(1)}, bf16[4,2,128,256]{3,2,1,0:T(8,128)(2,1)S(1)}, u32[]{:S(2)}, u32[]{:S(2)}) collective-permute-start(bf16[4,2,128,256]{3,2,1,0:T(8,128)(2,1)S(1)} %forward_outer0.1), channel_id=1, source_target_pairs={{1,2},{2,1},{3,4},{4,3},{5,6},{6,5},{7,8},{8,7},{9,10},{10,9},{11,... | collective-permute-start | bytes 1572872 | tf_op jit(solution)/shard_map/ppermute | solution.py:393
  34.7 17.2 %collective-permute-start.13 = (bf16[2,2,128,256]{3,2,1,0:T(8,128)(2,1)S(1)}, bf16[2,2,128,256]{3,2,1,0:T(8,128)(2,1)S(1)}, u32[]{:S(2)}, u32[]{:S(2)}) collective-permute-start(bf16[2,2,128,256]{3,2,1,0:T(8,128)(2,1)S(1)} %scale0.1.refs_0_), channel_id=1, source_target_pairs={{1,2},{2,1},{3,4},{4,3},{5,6},{6,5},{7,8},{8,7},{9,10},{10,9},{11,... | collective-permute-start | bytes 786440 | tf_op jit(solution)/shard_map/ppermute | solution.py:393
  38.8 16.0 %collective-permute-start.12 = (bf16[2,2,128,256]{3,2,1,0:T(8,128)(2,1)S(1)}, bf16[2,2,128,256]{3,2,1,0:T(8,128)(2,1)S(1)}, u32[]{:S(2)}, u32[]{:S(2)}) collective-permute-start(bf16[2,2,128,256]{3,2,1,0:T(8,128)(2,1)S(1)} %scale2.1.refs_1_), channel_id=1, source_target_pairs={{0,1},{1,0},{2,3},{3,2},{4,5},{5,4},{6,7},{7,6},{8,9},{9,8},{10,11... | collective-permute-start | bytes 786440 | tf_op jit(solution)/shard_map/ppermute | solution.py:393
  42.3 12.6 %collective-permute-start.11 = (bf16[2,2,128,256]{3,2,1,0:T(8,128)(2,1)S(1)}, bf16[2,2,128,256]{3,2,1,0:T(8,128)(2,1)S(1)}, u32[]{:S(2)}, u32[]{:S(2)}) collective-permute-start(bf16[2,2,128,256]{3,2,1,0:T(8,128)(2,1)S(1)} %scale0.1.refs_0_), channel_id=1, source_target_pairs={{0,1},{1,0},{2,3},{3,2},{4,5},{5,4},{6,7},{7,6},{8,9},{9,8},{10,11... | collective-permute-start | bytes 786440 | tf_op jit(solution)/shard_map/ppermute | solution.py:393
  42.4 13.2 %collective-permute-start.10 = (bf16[2,2,128,256]{3,2,1,0:T(8,128)(2,1)S(1)}, bf16[2,2,128,256]{3,2,1,0:T(8,128)(2,1)S(1)}, u32[]{:S(2)}, u32[]{:S(2)}) collective-permute-start(bf16[2,2,128,256]{3,2,1,0:T(8,128)(2,1)S(1)} %scale2.1.refs_1_), channel_id=1, source_target_pairs={{1,2},{2,1},{3,4},{4,3},{5,6},{6,5},{7,8},{8,7},{9,10},{10,9},{11,... | collective-permute-start | bytes 786440 | tf_op jit(solution)/shard_map/ppermute | solution.py:393
  59.1 13.9 %collective-permute-start.14 = (bf16[512,512]{1,0:T(8,128)(2,1)S(1)}, bf16[512,512]{1,0:T(8,128)(2,1)S(1)}, u32[]{:S(2)}, u32[]{:S(2)}) collective-permute-start(bf16[512,512]{1,0:T(8,128)(2,1)S(1)} %get-tuple-element.51), channel_id=1, source_target_pairs={{0,32},{1,33},{2,34},{3,35},{4,36},{5,37},{6,38},{7,39},{8,40},{9,... | collective-permute-start | bytes 1572872 | tf_op jit(solution)/shard_map/ppermute | solution.py:393
  59.2 16.9 %collective-permute-start.15 = (bf16[512,512]{1,0:T(8,128)(2,1)S(1)}, bf16[512,512]{1,0:T(8,128)(2,1)S(1)}, u32[]{:S(2)}, u32[]{:S(2)}) collective-permute-start(bf16[512,512]{1,0:T(8,128)(2,1)S(1)} %get-tuple-element.52), channel_id=1, source_target_pairs={{0,64},{1,65},{2,66},{3,67},{4,68},{5,69},{6,70},{7,71},{8,72},{9,... | collective-permute-start | bytes 1572872 | tf_op jit(solution)/shard_map/ppermute | solution.py:393
